TPU v7x, 32 devices: a whole 2x2x4 slice. The times are simulated.
32 devices in a mesh: rep: 4 (over y, x), shard: 2 (over core), exp: 4 (over z).
Axes of the slice: x: 2, y: 2, z: 4, core: 2. Of those that a mesh axis runs over, the one named last changes fastest.
Arguments:
- tokens: bfloat16 [2048, 2560], P(('rep', 'exp')), may hold values from -6 to 6
- expert_of: int32 [2048, 1], P(('rep', 'exp')), may hold values from 0 to 3; in each aligned block of 128 rows (0 to 127, 128 to 255, ...) at most 80 rows name the same one
- w_gate: bfloat16 [4, 768, 2560], P('exp', 'shard'), may hold values from -0.125 to 0.125
- w_up: bfloat16 [4, 768, 2560], P('exp', 'shard'), may hold values from -0.125 to 0.125
- d_hidden: bfloat16 [4, 4, 4, 80, 768], P('rep', 'exp', None, None, 'shard'), may hold values from -6 to 6
Outputs:
- hidden: bfloat16 [4, 4, 4, 80, 768], P('rep', 'exp', None, None, 'shard')
- d_tokens: bfloat16 [2048, 2560], P(('rep', 'exp'), 'shard')
- grad_gate: bfloat16 [4, 768, 2560], P('exp', 'shard')
- grad_up: bfloat16 [4, 768, 2560], P('exp', 'shard')
Inputs may be any that keep to these rules, and one draw needn't show every extreme that they name: `expert_of`: each value names an expert. Among the 128 tokens of one device (aligned blocks of rows), no expert is named more than 80 times, a bound that some block reaches.
All inputs are finite; a program needn't handle non-finite values.
Results may differ from a plain program's by a relative error of at most 0.017.
Values may be sent and summed in bfloat16 or wider, within the bound.
No kernel may reach another device: no remote copies, remote signals or barrier semaphores. Data moves between devices by JAX's collectives and lax.ppermute only.
A program may use at most 64 MiB of HBM per device.

v0:
```python
import jax
import jax.numpy as jnp
from jax import lax
from jax.sharding import PartitionSpec as P


def local(tokens, expert_of, w_gate, w_up, d_hidden):
    expert_count = lax.axis_size("exp")
    replica_count = lax.axis_size("rep")
    capacity = d_hidden.shape[3]
    feature_width = tokens.shape[1]
    slots_all = expert_count * capacity
    routed = expert_of[:, 0]
    chosen = (routed[:, None] == jnp.arange(expert_count, dtype=jnp.int32)[None, :]).astype(
        jnp.int32
    )
    slot_index = jnp.sum(chosen * (jnp.cumsum(chosen, axis=0) - 1), axis=1)
    target = routed * capacity + slot_index
    placing = (jnp.arange(slots_all, dtype=jnp.int32)[:, None] == target[None, :]).astype(
        jnp.bfloat16
    )
    packed = jnp.dot(placing, tokens, preferred_element_type=jnp.float32).astype(jnp.bfloat16)
    arrived = lax.all_to_all(
        packed.reshape(expert_count, capacity, feature_width),
        "exp",
        split_axis=0,
        concat_axis=0,
        tiled=True,
    )
    expert_rows = arrived.reshape(slots_all, feature_width)
    gate_rows = w_gate[0]
    up_rows = w_up[0]
    contract_last = (((1,), (1,)), ((), ()))
    gate_act = lax.dot_general(
        expert_rows, gate_rows, contract_last, preferred_element_type=jnp.float32
    )
    up_act = lax.dot_general(
        expert_rows, up_rows, contract_last, preferred_element_type=jnp.float32
    )
    sigma = jax.nn.sigmoid(gate_act)
    hidden = (gate_act * sigma * up_act).astype(jnp.bfloat16)
    cotan = d_hidden.reshape(slots_all, gate_rows.shape[0]).astype(jnp.float32)
    grad_gate_act = (cotan * up_act * sigma * (1.0 + gate_act * (1.0 - sigma))).astype(jnp.bfloat16)
    grad_up_act = (cotan * gate_act * sigma).astype(jnp.bfloat16)
    contract_first = (((0,), (0,)), ((), ()))
    part_gate = lax.dot_general(
        grad_gate_act, expert_rows, contract_first, preferred_element_type=jnp.float32
    )
    part_up = lax.dot_general(
        grad_up_act, expert_rows, contract_first, preferred_element_type=jnp.float32
    )
    total_gate, total_up = (
        lax.psum(
            part_gate.astype(jnp.bfloat16).astype(jnp.float32).astype(jnp.bfloat16), "rep"
        ).astype(jnp.float32),
        lax.psum(
            part_up.astype(jnp.bfloat16).astype(jnp.float32).astype(jnp.bfloat16), "rep"
        ).astype(jnp.float32),
    )
    grad_gate = (total_gate * (1.0 / replica_count)).astype(jnp.bfloat16)[None]
    grad_up = (total_up * (1.0 / replica_count)).astype(jnp.bfloat16)[None]
    partial_value = jnp.dot(grad_gate_act, gate_rows, preferred_element_type=jnp.float32)
    partial_value = partial_value + jnp.dot(
        grad_up_act, up_rows, preferred_element_type=jnp.float32
    )
    outgoing = partial_value.astype(jnp.bfloat16).reshape(expert_count, capacity, feature_width)
    returned = lax.all_to_all(outgoing, "exp", split_axis=0, concat_axis=0, tiled=True)
    unpacked = lax.dot_general(
        placing,
        returned.reshape(slots_all, feature_width),
        contract_first,
        preferred_element_type=jnp.float32,
    )
    d_tokens = lax.psum_scatter(
        unpacked.astype(jnp.bfloat16), "shard", scatter_dimension=1, tiled=True
    )
    return (hidden.reshape(d_hidden.shape), d_tokens, grad_gate, grad_up)


def solution(mesh):
    in_specs = (
        P(("rep", "exp"), None),
        P(("rep", "exp"), None),
        P("exp", "shard", None),
        P("exp", "shard", None),
        P("rep", "exp", None, None, "shard"),
    )
    out_specs = (
        P("rep", "exp", None, None, "shard"),
        P(("rep", "exp"), "shard"),
        P("exp", "shard", None),
        P("exp", "shard", None),
    )
    return jax.shard_map(local, mesh=mesh, in_specs=in_specs, out_specs=out_specs, check_vma=False)
```

profile of v0, /device:TPU:9, one launch (start us, length us, event | category | flops | bytes accessed | tf_op | source)
XLA Modules:
  0.0 175.3 jit_solution(2150093289877161744)
XLA Ops:
  8.0 0.0 copy-start
  8.0 0.0 all-reduce.3.cloned.1.call-start
  8.1 0.9 fusion.17
  8.9 0.2 reduce_window_sum.11
  9.1 0.8 select_reduce_fusion
  9.9 0.7 multiply_add_fusion
  10.6 1.7 convolution_convert_fusion.2
  12.3 0.0 copy-start.1
  12.3 40.7 %all_to_all.10 = bf16[4,80,2560]{2,1,0:T(8,128)(2,1)S(1)} all-to-all(bf16[4,80,2560]{2,1,0:T(8,128)(2,1)S(1)} %bitcast.39), channel_id=1, replica_groups=mesh['rep'=4,'shard'=2,'exp'=4] {'exp'}, dimensions={0} | all-to-all | bytes 3276800 | tf_op jit(solution)/shard_map/all_to_all | solution.py:23
  53.0 0.0 copy-done.1
  53.0 0.0 copy-start.2
  53.0 1.0 fusion.8
  54.0 0.0 copy-done
  54.1 0.0 copy-done.2
  54.1 1.9 %fusion.12 = (bf16[320,384]{1,0:T(8,128)(2,1)S(1)}, bf16[320,384]{1,0:T(8,128)(2,1)}, bf16[320,384]{1,0:T(8,128)(2,1)S(1)}) fusion(f32[320,384]{1,0:T(8,128)S(1)} %fusion.8, bf16[1,1,4,80,384]{4,3,2,1,0:T(8,128)(2,1)S(1)} %copy-done.2, bf16[320,2560]{1,0:T(8,128)(2,1)S(1)} %bitcast.41, bf16[1,384,2560]{2,1,0:T(8,128)(2,1)S(1)} %copy-done), kind=kOutput, calls=%fused_computation.21 | convolution fusion | flops 631234560 | bytes 5079040 | tf_op jit(solution)/shard_map/dot_general | solution.py:37
  55.9 2.5 %convolution_convert_fusion.1 = bf16[384,2560]{1,0:T(8,128)(2,1)} fusion(bf16[320,384]{1,0:T(8,128)(2,1)S(1)} %get-tuple-element.6, bf16[320,2560]{1,0:T(8,128)(2,1)S(1)} %bitcast.42), kind=kOutput, calls=%fused_computation.2 | convolution fusion | flops 630128640 | bytes 3850240 | tf_op jit(solution)/shard_map/dot_general | solution.py:46
  58.4 2.5 %convolution_convert_fusion = bf16[384,2560]{1,0:T(8,128)(2,1)} fusion(bf16[320,384]{1,0:T(8,128)(2,1)S(1)} %get-tuple-element.8, bf16[320,2560]{1,0:T(8,128)(2,1)S(1)} %bitcast.43), kind=kOutput, calls=%fused_computation.1 | convolution fusion | flops 630128640 | bytes 3850240 | tf_op jit(solution)/shard_map/dot_general | solution.py:49
  60.9 0.0 all-reduce.3.cloned.1.call-update
  60.9 0.0 reduce-scatter.2.cloned.1.call-start
  61.0 2.5 %fusion.6 = f32[320,2560]{1,0:T(8,128)S(1)} fusion(bf16[320,384]{1,0:T(8,128)(2,1)S(1)} %get-tuple-element.6, bf16[1,384,2560]{2,1,0:T(8,128)(2,1)} %param.7), kind=kOutput, calls=%fused_computation.13 | convolution fusion | flops 629145600 | bytes 5488640 | tf_op jit(solution)/shard_map/dot_general | solution.py:62
  63.5 1.0 fusion
  64.6 40.4 %all_to_all.11 = bf16[4,80,2560]{2,1,0:T(8,128)(2,1)S(1)} all-to-all(bf16[4,80,2560]{2,1,0:T(8,128)(2,1)S(1)} %bitcast.37), channel_id=1, replica_groups=mesh['rep'=4,'shard'=2,'exp'=4] {'exp'}, dimensions={0} | all-to-all | bytes 3276800 | tf_op jit(solution)/shard_map/all_to_all | solution.py:67
  105.0 1.4 convolution_convert_fusion.3
  106.3 0.0 reduce-scatter.2.cloned.1.call-update
  106.4 56.8 %all-reduce.3.cloned.1.call-done = (bf16[384,2560]{1,0:T(8,128)(2,1)}, bf16[384,2560]{1,0:T(8,128)(2,1)}) async-done(((bf16[384,2560]{1,0:T(8,128)(2,1)}, bf16[384,2560]{1,0:T(8,128)(2,1)}), (bf16[384,2560]{1,0:T(8,128)(2,1)}, bf16[384,2560]{1,0:T(8,128)(2,1)})) %all-reduce.3.cloned.1.call-update) | async-done | bytes 3932176 | tf_op jit(solution)/shard_map/psum | solution.py:53
  163.2 4.7 %fusion.1 = (bf16[1,384,2560]{2,1,0:T(8,128)(2,1)}, bf16[1,384,2560]{2,1,0:T(8,128)(2,1)}) fusion(bf16[384,2560]{1,0:T(8,128)(2,1)} %get-tuple-element.4, bf16[384,2560]{1,0:T(8,128)(2,1)} %get-tuple-element.5), kind=kLoop, calls=%fused_computation.8 | loop fusion | flops 5898240 | bytes 7864320 | tf_op jit(solution)/shard_map/broadcast_in_dim | solution.py:60
  167.9 0.0 reduce-scatter.2.cloned.1.call-done
Async XLA Ops:
  8.0 46.1 %copy-start = (bf16[1,384,2560]{2,1,0:T(8,128)(2,1)S(1)}, bf16[1,384,2560]{2,1,0:T(8,128)(2,1)}, u32[]{:S(2)}) copy-start(bf16[1,384,2560]{2,1,0:T(8,128)(2,1)} %param.8) | copy-start | bytes 5898244
  8.0 155.1 %all-reduce.3.cloned.1.call-start = ((), (), s32[]{:S(2)}) async-start(), calls=%async_computation.4 | async-start | bytes 7864320 | tf_op jit(solution)/shard_map/psum | solution.py:53
  12.3 40.8 %copy-start.1 = (bf16[1,384,2560]{2,1,0:T(8,128)(2,1)S(1)}, bf16[1,384,2560]{2,1,0:T(8,128)(2,1)}, u32[]{:S(2)}) copy-start(bf16[1,384,2560]{2,1,0:T(8,128)(2,1)} %param.7) | copy-start | bytes 5898244
  53.0 1.0 copy-start.2
  60.9 107.0 %reduce-scatter.2.cloned.1.call-start = ((), (), s32[]{:S(2)}) async-start(), calls=%async_computation.3 | async-start | bytes 983040 | tf_op jit(solution)/shard_map/reduce_scatter | solution.py:74
Sparse Core Ops, SparseCore 0:
  61.1 102.0 all-reduce.2
Sparse Core Ops, SparseCore 1:
  106.4 10.1 reduce-scatter.1
where the time goes:
time: 177 us; the launch traced here: 175 us
  blocking collectives  81.1 us (46%)
  waiting for transfers between devices  56.8 us (32%)
  between operations  15.5 us (9%)
  matrix products  14.5 us (8%)
  other arithmetic  7.28 us (4%)
    psum x1, waiting for transfers between devices, local(): lax.psum(part_gate.astype(jnp.bfloat16).astype(jnp.float32).astype(jnp.bf...  56.8 us
    all_to_all x1, blocking collectives, local(): lax.all_to_all(packed.reshape(expert_count, capacity, feature_width), 'ex...  40.7 us
    all_to_all x1, blocking collectives, local(): lax.all_to_all(outgoing, 'exp', split_axis=0, concat_axis=0, tiled=True)  40.4 us
    broadcast_in_dim x1, other arithmetic, local(): grad_gate = (total_gate * (1.0 / replica_count)).astype(jnp.bfloat16)[None]  4.75 us
  transfers between devices with their start and end apart: 2, of which 1 were waited for; matrix products, arithmetic and copies ran while one was open for 6% of the time, Pallas kernels for 0%

commit v1 on v0

v1 whole, which is shorter than its diff:
```python
import jax
import jax.numpy as jnp
from jax import lax
from jax.sharding import PartitionSpec as P

BF16 = jnp.bfloat16
F32 = jnp.float32
LAST = (((1,), (1,)), ((), ()))
FIRST = (((0,), (0,)), ((), ()))
MATMUL = (((1,), (0,)), ((), ()))


def dot(a, b, dims):
    return lax.dot_general(a, b, dims, preferred_element_type=F32)


def targets(expert_of, expert_count, capacity, first):
    routed = expert_of[:, 0]
    chosen = (routed[:, None] == jnp.arange(expert_count, dtype=jnp.int32)[None, :]).astype(
        jnp.int32
    )
    slot_index = jnp.sum(chosen * (jnp.cumsum(chosen, axis=0) - 1), axis=1)
    return lax.rem(routed - first + expert_count, expert_count) * capacity + slot_index


def placement(target, slots_all):
    return (jnp.arange(slots_all, dtype=jnp.int32)[:, None] == target[None, :]).astype(BF16)


def gradients(gate_act, up_act, cotan):
    sigma = jax.nn.sigmoid(gate_act)
    cotan = cotan.astype(F32)
    d_gate = (cotan * up_act * sigma * (1.0 + gate_act * (1.0 - sigma))).astype(BF16)
    d_up = (cotan * gate_act * sigma).astype(BF16)
    return sigma, d_gate, d_up


def reduce_plan(tokens, expert_of, w_gate, w_up, d_hidden):
    expert_count = lax.axis_size("exp")
    replica_count = lax.axis_size("rep")
    capacity = d_hidden.shape[3]
    feature_width = tokens.shape[1]
    slots_all = expert_count * capacity
    placing = placement(targets(expert_of, expert_count, capacity, 0), slots_all)
    packed = dot(placing, tokens, MATMUL).astype(BF16)
    arrived = lax.all_to_all(
        packed.reshape(expert_count, capacity, feature_width), "exp", 0, 0, tiled=True
    )
    rows = arrived.reshape(slots_all, feature_width)
    gate_act, up_act = dot(rows, w_gate[0], LAST), dot(rows, w_up[0], LAST)
    cotan = d_hidden.reshape(slots_all, w_gate.shape[1])
    sigma, d_gate, d_up = gradients(gate_act, up_act, cotan)
    hidden = (gate_act * sigma * up_act).astype(BF16)

    def reduced(d_act):
        total = lax.psum(dot(d_act, rows, FIRST).astype(BF16), "rep").astype(F32)
        return (total * (1.0 / replica_count)).astype(BF16)[None]

    term = dot(d_gate, w_gate[0], MATMUL) + dot(d_up, w_up[0], MATMUL)
    outgoing = term.astype(BF16).reshape(expert_count, capacity, feature_width)
    returned = lax.all_to_all(outgoing, "exp", 0, 0, tiled=True)
    unpacked = dot(placing, returned.reshape(slots_all, feature_width), FIRST)
    d_tokens = lax.psum_scatter(unpacked.astype(BF16), "shard", scatter_dimension=1, tiled=True)
    return hidden.reshape(d_hidden.shape), d_tokens, reduced(d_gate), reduced(d_up)


def across(x, axis, bit):
    size = lax.axis_size(axis)
    return lax.ppermute(x, axis, [(i, i ^ bit) for i in range(size)])


def turned(x, axis, step):
    size = lax.axis_size(axis)
    return lax.ppermute(x, axis, [(i, (i + step) % size) for i in range(size)])


def gather_rep(x):
    half = x.shape[0] // 2
    a, b = x[:half], x[half:]
    a1, b2 = across(a, "rep", 1), across(b, "rep", 2)
    near = jnp.concatenate([a1, b2])
    a23 = across(jnp.concatenate([a, a1]), "rep", 2)
    b13 = across(jnp.concatenate([b, b2]), "rep", 1)
    return near, jnp.concatenate([a23, b13])


def gather_plan(tokens, expert_of, w_gate, w_up, d_hidden):
    expert_count = lax.axis_size("exp")
    replica_count = lax.axis_size("rep")
    capacity = d_hidden.shape[3]
    half = tokens.shape[1] // 2
    slots_all = expert_count * capacity
    me, core = lax.axis_index("exp"), lax.axis_index("shard")
    gate_rows, up_rows = w_gate[0], w_up[0]

    order = lax.rem(me - jnp.arange(expert_count, dtype=jnp.int32) + expert_count, expert_count)
    cotan = d_hidden[0, 0][order].reshape(slots_all, -1)
    cotan_near, cotan_far = gather_rep(cotan)

    placing = placement(targets(expert_of, expert_count, capacity, me), slots_all)
    mine = lax.dynamic_slice_in_dim(tokens, core * half, half, axis=1)
    packed = dot(placing, mine, MATMUL).astype(BF16)
    blocks = [packed[k * capacity : (k + 1) * capacity] for k in range(expert_count)]
    arrived = [blocks[0]] + [turned(blocks[k], "exp", k) for k in range(1, expert_count)]
    rows = jnp.concatenate(arrived)
    near, far = gather_rep(rows)

    def whole(own):
        other = across(own, "shard", 1)
        return jnp.where(
            core == 0,
            jnp.concatenate([own, other], axis=1),
            jnp.concatenate([other, own], axis=1),
        )

    def back(own, cotan):
        full = whole(own)
        gate_act, up_act = dot(full, gate_rows, LAST), dot(full, up_rows, LAST)
        sigma, d_gate, d_up = gradients(gate_act, up_act, cotan)
        return full, gate_act * sigma * up_act, d_gate, d_up

    full, hidden, d_gate, d_up = back(rows, cotan)
    hidden = hidden.astype(BF16).reshape(d_hidden.shape[2:])[order]
    term = dot(d_gate, gate_rows, MATMUL) + dot(d_up, up_rows, MATMUL)
    left, right = term[:, :half], term[:, half:]
    kept = jnp.where(core == 0, left, right)
    sent = jnp.where(core == 0, right, left).astype(BF16)
    d_packed = (kept + across(sent, "shard", 1).astype(F32)).astype(BF16)
    pieces = [d_packed[k * capacity : (k + 1) * capacity] for k in range(expert_count)]
    returned = [pieces[0]] + [turned(pieces[k], "exp", -k) for k in range(1, expert_count)]
    d_tokens = dot(placing, jnp.concatenate(returned), FIRST).astype(BF16)

    grad_gate, grad_up = dot(d_gate, full, FIRST), dot(d_up, full, FIRST)
    for own, cotan_part in ((near, cotan_near), (far, cotan_far)):
        full, _, d_gate, d_up = back(own, cotan_part)
        grad_gate = grad_gate + dot(d_gate, full, FIRST)
        grad_up = grad_up + dot(d_up, full, FIRST)
    scale = 1.0 / replica_count
    grad_gate = (grad_gate * scale).astype(BF16)[None]
    grad_up = (grad_up * scale).astype(BF16)[None]
    return hidden.reshape(d_hidden.shape), d_tokens, grad_gate, grad_up


def local(tokens, expert_of, w_gate, w_up, d_hidden):
    replica_count, shard_count = lax.axis_size("rep"), lax.axis_size("shard")
    slots_all = d_hidden.shape[2] * d_hidden.shape[3]
    hidden_width, feature_width = w_gate.shape[1:]
    gathered = slots_all * (feature_width // shard_count + hidden_width) * replica_count
    reduced = 4 * hidden_width * feature_width
    if replica_count == 4 and shard_count == 2 and gathered < reduced:
        return gather_plan(tokens, expert_of, w_gate, w_up, d_hidden)
    return reduce_plan(tokens, expert_of, w_gate, w_up, d_hidden)


def solution(mesh):
    in_specs = (
        P(("rep", "exp"), None),
        P(("rep", "exp"), None),
        P("exp", "shard", None),
        P("exp", "shard", None),
        P("rep", "exp", None, None, "shard"),
    )
    out_specs = (
        P("rep", "exp", None, None, "shard"),
        P(("rep", "exp"), "shard"),
        P("exp", "shard", None),
        P("exp", "shard", None),
    )
    return jax.shard_map(local, mesh=mesh, in_specs=in_specs, out_specs=out_specs, check_vma=False)
```

time: 177 us -> 152 us (0.86)
  blocking collectives: 81.1 us -> 0 us
  matrix products: 14.5 us -> 64 us
  starting transfers between devices: 0.08 us -> 23 us
  waiting for transfers between devices: 56.8 us -> 36.8 us
  between operations: 15.5 us -> 0.87 us
  local copies, waits for them, and re-layouts: 0.02 us -> 12.8 us
  other arithmetic: 7.28 us -> 13.4 us
    all_to_all x2 -> x0, blocking collectives: 81.1 us -> none  [the longest x1 40.7 us: local(): lax.all_to_all(packed.reshape(expert_count, capacity, feature_width), 'ex...]
    psum x1 -> x0, waiting for transfers between devices: 56.8 us -> none  [local(): lax.psum(part_gate.astype(jnp.bfloat16).astype(jnp.float32).astype(jnp.bf...]
    dot_general x8 -> x14, matrix products: 14.5 us -> 64 us  [dot(): return lax.dot_general(a, b, dims, preferred_element_type=F32)]
    ppermute x0 -> x18, waiting for transfers between devices: none -> 36.8 us  [the longest x6 23.7 us: turned(): return lax.ppermute(x, axis, [(i, (i + step) % size) for i in range(size)])]
    ppermute x0 -> x18, starting transfers between devices: none -> 23 us  [the longest x12 12.6 us: across(): return lax.ppermute(x, axis, [(i, i ^ bit) for i in range(size)])]
    concatenate x0 -> x5, other arithmetic: none -> 7.54 us  [the longest x2 4.3 us: gather_rep(): b13 = across(jnp.concatenate([b, b2]), 'rep', 1)]
    unnamed x6 -> x38, local copies, waits for them, and re-layouts: 0.02 us -> 6.55 us
    broadcast_in_dim x1 -> x0, other arithmetic: 4.75 us -> none  [local(): grad_gate = (total_gate * (1.0 / replica_count)).astype(jnp.bfloat16)[None]]
  transfers between devices with their start and end apart: 2 -> 18, of which waited for: 1 -> 9; matrix products, arithmetic and copies ran while one was open for 6% -> 38% of each run, Pallas kernels for 0% -> 0%
where the time goes in v1:
time: 152 us; the launch traced here: 151 us
  matrix products  64 us (42%)
  waiting for transfers between devices  36.8 us (24%)
  starting transfers between devices  23 us (15%)
  other arithmetic  13.4 us (9%)
  local copies, waits for them, and re-layouts  12.8 us (8%)
    dot_general x14, matrix products, dot(): return lax.dot_general(a, b, dims, preferred_element_type=F32)  64 us
    ppermute x6, waiting for transfers between devices, turned(): return lax.ppermute(x, axis, [(i, (i + step) % size) for i in range(size)])  23.7 us
    ppermute x12, waiting for transfers between devices, across(): return lax.ppermute(x, axis, [(i, i ^ bit) for i in range(size)])  13.2 us
    ppermute x12, starting transfers between devices, across(): return lax.ppermute(x, axis, [(i, i ^ bit) for i in range(size)])  12.6 us
    ppermute x6, starting transfers between devices, turned(): return lax.ppermute(x, axis, [(i, (i + step) % size) for i in range(size)])  10.4 us
    unnamed x38, local copies, waits for them, and re-layouts  6.55 us
    concatenate x2, other arithmetic, gather_rep(): b13 = across(jnp.concatenate([b, b2]), 'rep', 1)  4.3 us
  transfers between devices with their start and end apart: 18, of which 9 were waited for; matrix products, arithmetic and copies ran while one was open for 38% of the time, Pallas kernels for 0%

profile of v1, /device:TPU:9, one launch (start us, length us, event | category | flops | bytes accessed | tf_op | source)
XLA Modules:
  0.0 150.9 jit_solution(8998753065143603727)
XLA Ops:
  3.2 1.3 convolution_convert_fusion
  4.7 2.5 %collective-permute-start.1 = (bf16[80,1280]{1,0:T(8,128)(2,1)S(1)}, bf16[80,1280]{1,0:T(8,128)(2,1)S(1)}, u32[]{:S(2)}, u32[]{:S(2)}) collective-permute-start(bf16[80,1280]{1,0:T(8,128)(2,1)S(1)} %get-tuple-element.12), channel_id=1, source_target_pairs={{0,2},{1,3},{2,0},{3,1},{4,6},{5,7},{6,4},{7,5},{8,10},{9,11},{10,... | collective-permute-start | bytes 614408 | tf_op jit(solution)/shard_map/ppermute | solution.py:74
  7.1 2.2 %collective-permute-start = (bf16[80,1280]{1,0:T(8,128)(2,1)S(1)}, bf16[80,1280]{1,0:T(8,128)(2,1)S(1)}, u32[]{:S(2)}, u32[]{:S(2)}) collective-permute-start(bf16[80,1280]{1,0:T(8,128)(2,1)S(1)} %get-tuple-element.13), channel_id=1, source_target_pairs={{0,1},{1,2},{2,3},{3,0},{4,5},{5,6},{6,7},{7,4},{8,9},{9,10},{10,1... | collective-permute-start | bytes 614408 | tf_op jit(solution)/shard_map/ppermute | solution.py:74
  10.6 9.4 %collective-permute-done.1 = bf16[80,1280]{1,0:T(8,128)(2,1)S(1)} collective-permute-done((bf16[80,1280]{1,0:T(8,128)(2,1)S(1)}, bf16[80,1280]{1,0:T(8,128)(2,1)S(1)}, u32[]{:S(2)}, u32[]{:S(2)}) %collective-permute-start.1) | collective-permute-done | bytes 204832 | tf_op jit(solution)/shard_map/ppermute | solution.py:74
  22.7 1.7 %collective-permute-done = bf16[80,1280]{1,0:T(8,128)(2,1)S(1)} collective-permute-done((bf16[80,1280]{1,0:T(8,128)(2,1)S(1)}, bf16[80,1280]{1,0:T(8,128)(2,1)S(1)}, u32[]{:S(2)}, u32[]{:S(2)}) %collective-permute-start) | collective-permute-done | bytes 204832 | tf_op jit(solution)/shard_map/ppermute | solution.py:74
  27.1 1.5 %gather_fusion.1 = bf16[4,80,384]{2,1,0:T(8,128)(2,1)S(1)} fusion(bf16[4,80,384]{2,1,0:T(8,128)(2,1)} %bitcast.61, s32[1024]{0:T(1024)S(1)} %pad_clamp_fusion), kind=kCustom, calls=%fused_computation.1 | custom fusion | bytes 491536 | tf_op jit(solution)/shard_map/gather | solution.py:97
  30.5 5.3 %collective-permute-done.10 = bf16[160,1280]{1,0:T(8,128)(2,1)S(1)} collective-permute-done((bf16[160,1280]{1,0:T(8,128)(2,1)}, bf16[160,1280]{1,0:T(8,128)(2,1)S(1)}, u32[]{:S(2)}, u32[]{:S(2)}) %collective-permute-start.10) | collective-permute-done | bytes 409632 | tf_op jit(solution)/shard_map/ppermute | solution.py:69
  35.7 2.6 %pad_maximum_fusion.3 = (bf16[320,1280]{1,0:T(8,128)(2,1)}, bf16[320,1280]{1,0:T(8,128)(2,1)}, bf16[320,1280]{1,0:T(8,128)(2,1)}) fusion(bf16[160,1280]{1,0:T(8,128)(2,1)S(1)} %collective-permute-done.11, bf16[80,1280]{1,0:T(8,128)(2,1)S(1)} %collective-permute-done.2, bf16[80,1280]{1,0:T(8,128)(2,1)} %copy-done.4, bf16[80,1280]{1,0:T(8,128)(2,1)} %copy-done.7, ...), kind=kLoop, calls=%fused_computation.58 | loop fusion | flops 6963200 | bytes 4096000 | tf_op jit(solution)/shard_map/concatenate | solution.py:83
  38.3 3.5 %collective-permute-start.3 = (bf16[320,1280]{1,0:T(8,128)(2,1)}, bf16[320,1280]{1,0:T(8,128)(2,1)}, u32[]{:S(2)}, u32[]{:S(2)}) collective-permute-start(bf16[320,1280]{1,0:T(8,128)(2,1)} %get-tuple-element.16), channel_id=1, source_target_pairs={{0,4},{4,0},{1,5},{5,1},{2,6},{6,2},{3,7},{7,3},{8,12},{12,8},{9,1... | collective-permute-start | bytes 2457608 | tf_op jit(solution)/shard_map/ppermute | solution.py:69
  43.1 1.7 %pad_maximum_fusion.11 = bf16[320,384]{1,0:T(8,128)(2,1)} fusion(bf16[160,384]{1,0:T(8,128)(2,1)} %collective-permute-done.8, bf16[160,384]{1,0:T(8,128)(2,1)} %bitcast.9), kind=kLoop, calls=%fused_computation.87 | loop fusion | flops 491520 | bytes 491520 | tf_op jit(solution)/shard_map/concatenate | solution.py:82
  45.0 2.1 %collective-permute-done.9 = bf16[160,384]{1,0:T(8,128)(2,1)} collective-permute-done((bf16[160,384]{1,0:T(8,128)(2,1)}, bf16[160,384]{1,0:T(8,128)(2,1)}, u32[]{:S(2)}, u32[]{:S(2)}) %collective-permute-start.9) | collective-permute-done | bytes 122912 | tf_op jit(solution)/shard_map/ppermute | solution.py:69
  47.1 1.7 %pad_maximum_fusion.9 = bf16[320,384]{1,0:T(8,128)(2,1)} fusion(bf16[160,384]{1,0:T(8,128)(2,1)} %collective-permute-done.9, bf16[160,384]{1,0:T(8,128)(2,1)} %bitcast.10), kind=kLoop, calls=%fused_computation.84 | loop fusion | flops 491520 | bytes 491520 | tf_op jit(solution)/shard_map/concatenate | solution.py:83
  52.4 1.6 %collective-permute-start.15 = (bf16[320,1280]{1,0:T(8,128)(2,1)}, bf16[320,1280]{1,0:T(8,128)(2,1)}, u32[]{:S(2)}, u32[]{:S(2)}) collective-permute-start(bf16[320,1280]{1,0:T(8,128)(2,1)} %get-tuple-element.17), channel_id=1, source_target_pairs={{0,16},{8,24},{16,0},{24,8},{1,17},{9,25},{17,1},{25,9},{2,18},{10... | collective-permute-start | bytes 2457608 | tf_op jit(solution)/shard_map/ppermute | solution.py:69
  54.0 7.9 %fusion.21 = f32[320,384]{1,0:T(8,128)S(1)} fusion(bf16[1,384,2560]{2,1,0:T(8,128)(2,1)} %param.7, bf16[320,1280]{1,0:T(8,128)(2,1)} %collective-permute-done.3, bf16[80,1280]{1,0:T(8,128)(2,1)S(1)} %collective-permute-done.2, bf16[80,1280]{1,0:T(8,128)(2,1)} %copy-done.4, bf16[80,1280]{1,0:T(8,128)(2,1)} %copy-done.7, ...), kind=kOutput, calls=%fused_computation.29 | convolution fusion | flops 646348800 | bytes 4096001 | tf_op jit(solution)/shard_map/dot_general | solution.py:14
  62.0 3.5 %fusion.67 = (bf16[320,384]{1,0:T(8,128)(2,1)}, bf16[320,384]{1,0:T(8,128)(2,1)}, bf16[320,384]{1,0:T(8,128)(2,1)}) fusion(f32[320,384]{1,0:T(8,128)S(1)} %fusion.21, bf16[4,80,384]{2,1,0:T(8,128)(2,1)S(1)} %gather_fusion.1, bf16[1,384,2560]{2,1,0:T(8,128)(2,1)S(1)} %copy-done, bf16[320,1280]{1,0:T(8,128)(2,1)} %collective-permute-done.3, ...), kind=kOutput, calls=%fused_computation.68 | convolution fusion | flops 648437760 | bytes 5079041 | tf_op jit(solution)/shard_map/dot_general | solution.py:14
  65.4 2.2 %gather_fusion = bf16[4,80,384]{2,1,0:T(8,128)(2,1)} fusion(bf16[4,80,384]{2,1,0:T(8,128)(2,1)} %bitcast.63, s32[1024]{0:T(1024)S(1)} %pad_clamp_fusion), kind=kCustom, calls=%fused_computation | custom fusion | bytes 491536 | tf_op jit(solution)/shard_map/gather | solution.py:123
  67.7 4.9 %collective-permute-done.15 = bf16[320,1280]{1,0:T(8,128)(2,1)} collective-permute-done((bf16[320,1280]{1,0:T(8,128)(2,1)}, bf16[320,1280]{1,0:T(8,128)(2,1)}, u32[]{:S(2)}, u32[]{:S(2)}) %collective-permute-start.15) | collective-permute-done | bytes 819232 | tf_op jit(solution)/shard_map/ppermute | solution.py:69
  72.6 2.1 %constant_dynamic-update-slice_fusion.3 = bf16[640,1280]{1,0:T(8,128)(2,1)} fusion(bf16[320,1280]{1,0:T(8,128)(2,1)} %collective-permute-done.15), kind=kLoop, calls=%fused_computation.99 | loop fusion | bytes 1638400
  78.7 1.7 %copy-done.1 = f32[320,2560]{1,0:T(8,128)} copy-done((f32[320,2560]{1,0:T(8,128)}, f32[320,2560]{1,0:T(8,128)S(1)}, u32[]{:S(2)}) %copy-start.1) | copy-done | bytes 3276824
  81.4 3.8 %fusion.17 = f32[320,384]{1,0:T(8,128)} fusion(bf16[1,384,2560]{2,1,0:T(8,128)(2,1)S(1)} %copy-done.2, bf16[320,1280]{1,0:T(8,128)(2,1)} %collective-permute-done.12, bf16[320,1280]{1,0:T(8,128)(2,1)} %constant_dynamic-update-slice_fusion, pred[]{:T(512)S(6)} %eq.14), kind=kOutput, calls=%fused_computation.25 | convolution fusion | flops 636518400 | bytes 4096001 | tf_op jit(solution)/shard_map/dot_general | solution.py:14
  85.2 7.7 %fusion.48 = f32[384,2560]{1,0:T(8,128)} fusion(bf16[1,384,2560]{2,1,0:T(8,128)(2,1)S(1)} %copy-done, f32[320,384]{1,0:T(8,128)} %fusion.17, bf16[160,384]{1,0:T(8,128)(2,1)} %collective-permute-done.9, bf16[160,384]{1,0:T(8,128)(2,1)} %collective-permute-done.8, bf16[320,1280]{1,0:T(8,128)(2,1)} %collective-permute-done.12, ...), kind=kOutput, calls=%fused_computation.44 | convolution fusion | flops 1274757120 | bytes 8273921 | tf_op jit(solution)/shard_map/dot_general | solution.py:14
  92.9 2.3 %add_convert_fusion = bf16[320,1280]{1,0:T(8,128)(2,1)S(1)} fusion(bf16[320,1280]{1,0:T(8,128)(2,1)S(1)} %collective-permute-done.4, f32[320,2560]{1,0:T(8,128)} %copy-done.1, pred[]{:T(512)S(6)} %eq.14), kind=kLoop, calls=%fused_computation.33 | loop fusion | flops 1638400 | bytes 4915201 | tf_op jit(solution)/shard_map/convert_element_type | solution.py:128
  95.3 2.3 %collective-permute-start.7 = (bf16[80,1280]{1,0:T(8,128)(2,1)S(1)}, bf16[80,1280]{1,0:T(8,128)(2,1)S(1)}, u32[]{:S(2)}, u32[]{:S(2)}) collective-permute-start(bf16[80,1280]{1,0:T(8,128)(2,1)S(1)} %get-tuple-element.7), channel_id=1, source_target_pairs={{0,1},{1,2},{2,3},{3,0},{4,5},{5,6},{6,7},{7,4},{8,9},{9,10},{10,1... | collective-permute-start | bytes 614408 | tf_op jit(solution)/shard_map/ppermute | solution.py:74
  97.5 3.4 %collective-permute-start.6 = (bf16[80,1280]{1,0:T(8,128)(2,1)S(1)}, bf16[80,1280]{1,0:T(8,128)(2,1)S(1)}, u32[]{:S(2)}, u32[]{:S(2)}) collective-permute-start(bf16[80,1280]{1,0:T(8,128)(2,1)S(1)} %get-tuple-element.8), channel_id=1, source_target_pairs={{0,2},{1,3},{2,0},{3,1},{4,6},{5,7},{6,4},{7,5},{8,10},{9,11},{10,... | collective-permute-start | bytes 614408 | tf_op jit(solution)/shard_map/ppermute | solution.py:74
  100.9 5.4 %fusion.78 = f32[384,2560]{1,0:T(8,128)} fusion(f32[320,384]{1,0:T(8,128)S(1)} %copy-done.17, bf16[160,384]{1,0:T(8,128)(2,1)} %collective-permute-done.9, bf16[160,384]{1,0:T(8,128)(2,1)} %collective-permute-done.8, bf16[320,1280]{1,0:T(8,128)(2,1)} %collective-permute-done.12, bf16[320,1280]{1,0:T(8,128)(2,1)} %constant_dynamic-update-slice_fusion, ...), kind=kOutput, calls=%fused_computation.86 | convolution fusion | flops 637747200 | bytes 6307841 | tf_op jit(solution)/shard_map/dot_general | solution.py:14
  106.7 7.9 %collective-permute-done.6 = bf16[80,1280]{1,0:T(8,128)(2,1)S(1)} collective-permute-done((bf16[80,1280]{1,0:T(8,128)(2,1)S(1)}, bf16[80,1280]{1,0:T(8,128)(2,1)S(1)}, u32[]{:S(2)}, u32[]{:S(2)}) %collective-permute-start.6) | collective-permute-done | bytes 204832 | tf_op jit(solution)/shard_map/ppermute | solution.py:74
  114.6 3.4 %collective-permute-done.5 = bf16[80,1280]{1,0:T(8,128)(2,1)S(1)} collective-permute-done((bf16[80,1280]{1,0:T(8,128)(2,1)S(1)}, bf16[80,1280]{1,0:T(8,128)(2,1)S(1)}, u32[]{:S(2)}, u32[]{:S(2)}) %collective-permute-start.5) | collective-permute-done | bytes 204832 | tf_op jit(solution)/shard_map/ppermute | solution.py:74
  119.2 5.8 %fusion.15 = f32[640,384]{1,0:T(8,128)} fusion(bf16[1,384,2560]{2,1,0:T(8,128)(2,1)S(1)} %copy-done.3, bf16[640,1280]{1,0:T(8,128)(2,1)} %collective-permute-done.17, bf16[640,1280]{1,0:T(8,128)(2,1)} %constant_dynamic-update-slice_fusion.2, pred[]{:T(512)S(6)} %eq.14), kind=kOutput, calls=%fused_computation.23 | convolution fusion | flops 1273036800 | bytes 6225921 | tf_op jit(solution)/shard_map/dot_general | solution.py:14
  125.0 11.5 %fusion.60 = f32[384,2560]{1,0:T(8,128)} fusion(bf16[1,384,2560]{2,1,0:T(8,128)(2,1)S(1)} %copy-done, f32[640,384]{1,0:T(8,128)} %fusion.15, bf16[320,384]{1,0:T(8,128)(2,1)} %collective-permute-done.14, bf16[320,384]{1,0:T(8,128)(2,1)} %collective-permute-done.13, bf16[640,1280]{1,0:T(8,128)(2,1)} %collective-permute-done.17, ...), kind=kOutput, calls=%fused_computation.59 | convolution fusion | flops 2549514240 | bytes 10649601 | tf_op jit(solution)/shard_map/dot_general | solution.py:14
  136.5 5.4 %fusion.70 = f32[384,2560]{1,0:T(8,128)S(1)} fusion(f32[640,384]{1,0:T(8,128)} %fusion.15, bf16[320,384]{1,0:T(8,128)(2,1)} %collective-permute-done.14, bf16[320,384]{1,0:T(8,128)(2,1)} %collective-permute-done.13, bf16[640,1280]{1,0:T(8,128)(2,1)} %collective-permute-done.17, bf16[640,1280]{1,0:T(8,128)(2,1)} %constant_dynamic-update-slice_fusion.2, ...), kind=kOutput, calls=%fused_computation.71 | convolution fusion | flops 1275494400 | bytes 8683521 | tf_op jit(solution)/shard_map/dot_general | solution.py:14
  142.5 4.3 %fusion.7 = bf16[1,384,2560]{2,1,0:T(8,128)(2,1)} fusion(f32[384,2560]{1,0:T(8,128)S(1)} %copy-done.16, f32[384,2560]{1,0:T(8,128)S(1)} %copy-done.15, bf16[320,384]{1,0:T(8,128)(2,1)S(1)} %copy-done.12, bf16[320,1280]{1,0:T(8,128)(2,1)} %collective-permute-done.3, bf16[80,1280]{1,0:T(8,128)(2,1)S(1)} %collective-permute-done.2, ...), kind=kOutput, calls=%fused_computation.12 | convolution fusion | flops 650280960 | bytes 11714561 | tf_op jit(solution)/shard_map/dot_general | solution.py:14
  146.8 4.2 %fusion.6 = bf16[1,384,2560]{2,1,0:T(8,128)(2,1)} fusion(f32[384,2560]{1,0:T(8,128)S(1)} %fusion.70, f32[384,2560]{1,0:T(8,128)S(1)} %copy-done.14, bf16[320,384]{1,0:T(8,128)(2,1)S(1)} %copy-done.10, bf16[320,1280]{1,0:T(8,128)(2,1)} %collective-permute-done.3, bf16[80,1280]{1,0:T(8,128)(2,1)S(1)} %collective-permute-done.2, ...), kind=kOutput, calls=%fused_computation.11 | convolution fusion | flops 650280960 | bytes 11714561 | tf_op jit(solution)/shard_map/dot_general | solution.py:14
  (76 shorter events, 23.3 us)
Async XLA Ops:
  0.6 61.3 %copy-start = (bf16[1,384,2560]{2,1,0:T(8,128)(2,1)S(1)}, bf16[1,384,2560]{2,1,0:T(8,128)(2,1)}, u32[]{:S(2)}) copy-start(bf16[1,384,2560]{2,1,0:T(8,128)(2,1)} %param.8) | copy-start | bytes 5898244
  4.6 6.0 %collective-permute-start.2 = (bf16[80,1280]{1,0:T(8,128)(2,1)S(1)}, bf16[80,1280]{1,0:T(8,128)(2,1)S(1)}, u32[]{:S(2)}, u32[]{:S(2)}) collective-permute-start(bf16[80,1280]{1,0:T(8,128)(2,1)S(1)} %get-tuple-element.11), channel_id=1, source_target_pairs={{0,3},{1,0},{2,1},{3,2},{4,7},{5,4},{6,5},{7,6},{8,11},{9,8},{10,9... | collective-permute-start | bytes 614408 | tf_op jit(solution)/shard_map/ppermute | solution.py:74
  4.7 15.3 %collective-permute-start.1 = (bf16[80,1280]{1,0:T(8,128)(2,1)S(1)}, bf16[80,1280]{1,0:T(8,128)(2,1)S(1)}, u32[]{:S(2)}, u32[]{:S(2)}) collective-permute-start(bf16[80,1280]{1,0:T(8,128)(2,1)S(1)} %get-tuple-element.12), channel_id=1, source_target_pairs={{0,2},{1,3},{2,0},{3,1},{4,6},{5,7},{6,4},{7,5},{8,10},{9,11},{10,... | collective-permute-start | bytes 614408 | tf_op jit(solution)/shard_map/ppermute | solution.py:74
  7.1 17.2 %collective-permute-start = (bf16[80,1280]{1,0:T(8,128)(2,1)S(1)}, bf16[80,1280]{1,0:T(8,128)(2,1)S(1)}, u32[]{:S(2)}, u32[]{:S(2)}) collective-permute-start(bf16[80,1280]{1,0:T(8,128)(2,1)S(1)} %get-tuple-element.13), channel_id=1, source_target_pairs={{0,1},{1,2},{2,3},{3,0},{4,5},{5,6},{6,7},{7,4},{8,9},{9,10},{10,1... | collective-permute-start | bytes 614408 | tf_op jit(solution)/shard_map/ppermute | solution.py:74
  21.4 9.0 %collective-permute-start.11 = (bf16[160,1280]{1,0:T(8,128)(2,1)}, bf16[160,1280]{1,0:T(8,128)(2,1)S(1)}, u32[]{:S(2)}, u32[]{:S(2)}) collective-permute-start(bf16[160,1280]{1,0:T(8,128)(2,1)} %pad_maximum_fusion.6), channel_id=1, source_target_pairs={{0,16},{8,24},{16,0},{24,8},{1,17},{9,25},{17,1},{25,9},{2,18},{10... | collective-permute-start | bytes 1228808 | tf_op jit(solution)/shard_map/ppermute | solution.py:69
  25.8 9.9 %collective-permute-start.10 = (bf16[160,1280]{1,0:T(8,128)(2,1)}, bf16[160,1280]{1,0:T(8,128)(2,1)S(1)}, u32[]{:S(2)}, u32[]{:S(2)}) collective-permute-start(bf16[160,1280]{1,0:T(8,128)(2,1)} %pad_maximum_fusion.5), channel_id=1, source_target_pairs={{0,8},{8,0},{16,24},{24,16},{1,9},{9,1},{17,25},{25,17},{2,10},{10... | collective-permute-start | bytes 1228808 | tf_op jit(solution)/shard_map/ppermute | solution.py:69
  29.3 13.8 %collective-permute-start.8 = (bf16[160,384]{1,0:T(8,128)(2,1)}, bf16[160,384]{1,0:T(8,128)(2,1)}, u32[]{:S(2)}, u32[]{:S(2)}) collective-permute-start(bf16[160,384]{1,0:T(8,128)(2,1)} %bitcast.9), channel_id=1, source_target_pairs={{0,8},{8,0},{16,24},{24,16},{1,9},{9,1},{17,25},{25,17},{2,10},{10... | collective-permute-start | bytes 368648 | tf_op jit(solution)/shard_map/ppermute | solution.py:69
  38.3 15.7 %collective-permute-start.3 = (bf16[320,1280]{1,0:T(8,128)(2,1)}, bf16[320,1280]{1,0:T(8,128)(2,1)}, u32[]{:S(2)}, u32[]{:S(2)}) collective-permute-start(bf16[320,1280]{1,0:T(8,128)(2,1)} %get-tuple-element.16), channel_id=1, source_target_pairs={{0,4},{4,0},{1,5},{5,1},{2,6},{6,2},{3,7},{7,3},{8,12},{12,8},{9,1... | collective-permute-start | bytes 2457608 | tf_op jit(solution)/shard_map/ppermute | solution.py:69
  41.9 5.3 %collective-permute-start.9 = (bf16[160,384]{1,0:T(8,128)(2,1)}, bf16[160,384]{1,0:T(8,128)(2,1)}, u32[]{:S(2)}, u32[]{:S(2)}) collective-permute-start(bf16[160,384]{1,0:T(8,128)(2,1)} %bitcast.10), channel_id=1, source_target_pairs={{0,16},{8,24},{16,0},{24,8},{1,17},{9,25},{17,1},{25,9},{2,18},{10... | collective-permute-start | bytes 368648 | tf_op jit(solution)/shard_map/ppermute | solution.py:69
  44.8 80.2 %collective-permute-start.13 = (bf16[320,384]{1,0:T(8,128)(2,1)}, bf16[320,384]{1,0:T(8,128)(2,1)}, u32[]{:S(2)}, u32[]{:S(2)}) collective-permute-start(bf16[320,384]{1,0:T(8,128)(2,1)} %pad_maximum_fusion.11), channel_id=1, source_target_pairs={{0,16},{8,24},{16,0},{24,8},{1,17},{9,25},{17,1},{25,9},{2,18},{10... | collective-permute-start | bytes 737288 | tf_op jit(solution)/shard_map/ppermute | solution.py:69
  50.4 31.0 %collective-permute-start.12 = (bf16[320,1280]{1,0:T(8,128)(2,1)}, bf16[320,1280]{1,0:T(8,128)(2,1)}, u32[]{:S(2)}, u32[]{:S(2)}) collective-permute-start(bf16[320,1280]{1,0:T(8,128)(2,1)} %constant_dynamic-update-slice_fusion), channel_id=1, source_target_pairs={{0,4},{4,0},{1,5},{5,1},{2,6},{6,2},{3,7},{7,3},{8,12},{12,8},{9,1... | collective-permute-start | bytes 2457608 | tf_op jit(solution)/shard_map/ppermute | solution.py:69
  51.1 23.5 %collective-permute-start.16 = (bf16[320,1280]{1,0:T(8,128)(2,1)}, bf16[320,1280]{1,0:T(8,128)(2,1)S(1)}, u32[]{:S(2)}, u32[]{:S(2)}) collective-permute-start(bf16[320,1280]{1,0:T(8,128)(2,1)} %get-tuple-element.15), channel_id=1, source_target_pairs={{0,8},{8,0},{16,24},{24,16},{1,9},{9,1},{17,25},{25,17},{2,10},{10... | collective-permute-start | bytes 2457608 | tf_op jit(solution)/shard_map/ppermute | solution.py:69
  52.4 9.6 %copy-start.5 = (bf16[80,1280]{1,0:T(8,128)(2,1)S(1)}, bf16[80,1280]{1,0:T(8,128)(2,1)}, u32[]{:S(2)}) copy-start(bf16[80,1280]{1,0:T(8,128)(2,1)} %copy-done.4) | copy-start | bytes 614404
  52.4 9.6 %copy-start.8 = (bf16[80,1280]{1,0:T(8,128)(2,1)S(1)}, bf16[80,1280]{1,0:T(8,128)(2,1)}, u32[]{:S(2)}) copy-start(bf16[80,1280]{1,0:T(8,128)(2,1)} %copy-done.7) | copy-start | bytes 614404
  52.4 20.2 %collective-permute-start.15 = (bf16[320,1280]{1,0:T(8,128)(2,1)}, bf16[320,1280]{1,0:T(8,128)(2,1)}, u32[]{:S(2)}, u32[]{:S(2)}) collective-permute-start(bf16[320,1280]{1,0:T(8,128)(2,1)} %get-tuple-element.17), channel_id=1, source_target_pairs={{0,16},{8,24},{16,0},{24,8},{1,17},{9,25},{17,1},{25,9},{2,18},{10... | collective-permute-start | bytes 2457608 | tf_op jit(solution)/shard_map/ppermute | solution.py:69
  67.7 8.9 %copy-start.2 = (bf16[1,384,2560]{2,1,0:T(8,128)(2,1)S(1)}, bf16[1,384,2560]{2,1,0:T(8,128)(2,1)}, u32[]{:S(2)}) copy-start(bf16[1,384,2560]{2,1,0:T(8,128)(2,1)} %param.7) | copy-start | bytes 5898244
  67.7 8.9 %copy-start.11 = (bf16[320,384]{1,0:T(8,128)(2,1)S(1)}, bf16[320,384]{1,0:T(8,128)(2,1)}, u32[]{:S(2)}) copy-start(bf16[320,384]{1,0:T(8,128)(2,1)} %get-tuple-element.4) | copy-start | bytes 737284
  75.6 43.5 %collective-permute-start.17 = (bf16[640,1280]{1,0:T(8,128)(2,1)}, bf16[640,1280]{1,0:T(8,128)(2,1)}, u32[]{:S(2)}, u32[]{:S(2)}) collective-permute-start(bf16[640,1280]{1,0:T(8,128)(2,1)} %constant_dynamic-update-slice_fusion.2), channel_id=1, source_target_pairs={{0,4},{4,0},{1,5},{5,1},{2,6},{6,2},{3,7},{7,3},{8,12},{12,8},{9,1... | collective-permute-start | bytes 4915208 | tf_op jit(solution)/shard_map/ppermute | solution.py:69
  81.4 11.5 %collective-permute-start.4 = (bf16[320,1280]{1,0:T(8,128)(2,1)}, bf16[320,1280]{1,0:T(8,128)(2,1)S(1)}, u32[]{:S(2)}, u32[]{:S(2)}) collective-permute-start(bf16[320,1280]{1,0:T(8,128)(2,1)} %select_convert_fusion), channel_id=1, source_target_pairs={{0,4},{4,0},{1,5},{5,1},{2,6},{6,2},{3,7},{7,3},{8,12},{12,8},{9,1... | collective-permute-start | bytes 2457608 | tf_op jit(solution)/shard_map/ppermute | solution.py:69
  92.9 8.1 %copy-start.17 = (f32[320,384]{1,0:T(8,128)S(1)}, f32[320,384]{1,0:T(8,128)}, u32[]{:S(2)}) copy-start(f32[320,384]{1,0:T(8,128)} %fusion.17) | copy-start | bytes 1474564
  95.3 11.1 %collective-permute-start.7 = (bf16[80,1280]{1,0:T(8,128)(2,1)S(1)}, bf16[80,1280]{1,0:T(8,128)(2,1)S(1)}, u32[]{:S(2)}, u32[]{:S(2)}) collective-permute-start(bf16[80,1280]{1,0:T(8,128)(2,1)S(1)} %get-tuple-element.7), channel_id=1, source_target_pairs={{0,1},{1,2},{2,3},{3,0},{4,5},{5,6},{6,7},{7,4},{8,9},{9,10},{10,1... | collective-permute-start | bytes 614408 | tf_op jit(solution)/shard_map/ppermute | solution.py:74
  97.5 17.1 %collective-permute-start.6 = (bf16[80,1280]{1,0:T(8,128)(2,1)S(1)}, bf16[80,1280]{1,0:T(8,128)(2,1)S(1)}, u32[]{:S(2)}, u32[]{:S(2)}) collective-permute-start(bf16[80,1280]{1,0:T(8,128)(2,1)S(1)} %get-tuple-element.8), channel_id=1, source_target_pairs={{0,2},{1,3},{2,0},{3,1},{4,6},{5,7},{6,4},{7,5},{8,10},{9,11},{10,... | collective-permute-start | bytes 614408 | tf_op jit(solution)/shard_map/ppermute | solution.py:74
  100.9 5.4 %copy-start.13 = (bf16[320,384]{1,0:T(8,128)(2,1)S(1)}, bf16[320,384]{1,0:T(8,128)(2,1)}, u32[]{:S(2)}) copy-start(bf16[320,384]{1,0:T(8,128)(2,1)} %pad_maximum_fusion.9) | copy-start | bytes 737284
  100.9 18.2 %copy-start.3 = (bf16[1,384,2560]{2,1,0:T(8,128)(2,1)S(1)}, bf16[1,384,2560]{2,1,0:T(8,128)(2,1)}, u32[]{:S(2)}) copy-start(bf16[1,384,2560]{2,1,0:T(8,128)(2,1)} %param.7) | copy-start | bytes 5898244
  100.9 17.1 %collective-permute-start.5 = (bf16[80,1280]{1,0:T(8,128)(2,1)S(1)}, bf16[80,1280]{1,0:T(8,128)(2,1)S(1)}, u32[]{:S(2)}, u32[]{:S(2)}) collective-permute-start(bf16[80,1280]{1,0:T(8,128)(2,1)S(1)} %get-tuple-element.9), channel_id=1, source_target_pairs={{0,3},{1,0},{2,1},{3,2},{4,7},{5,4},{6,5},{7,6},{8,11},{9,8},{10,9... | collective-permute-start | bytes 614408 | tf_op jit(solution)/shard_map/ppermute | solution.py:74
  106.4 18.6 %collective-permute-start.14 = (bf16[320,384]{1,0:T(8,128)(2,1)S(1)}, bf16[320,384]{1,0:T(8,128)(2,1)}, u32[]{:S(2)}, u32[]{:S(2)}) collective-permute-start(bf16[320,384]{1,0:T(8,128)(2,1)S(1)} %copy-done.13), channel_id=1, source_target_pairs={{0,8},{8,0},{16,24},{24,16},{1,9},{9,1},{17,25},{25,17},{2,10},{10... | collective-permute-start | bytes 737288 | tf_op jit(solution)/shard_map/ppermute | solution.py:69
  136.5 5.4 %copy-start.6 = (bf16[80,1280]{1,0:T(8,128)(2,1)S(1)}, bf16[80,1280]{1,0:T(8,128)(2,1)}, u32[]{:S(2)}) copy-start(bf16[80,1280]{1,0:T(8,128)(2,1)} %copy-done.4) | copy-start | bytes 614404
  136.5 5.5 %copy-start.9 = (bf16[80,1280]{1,0:T(8,128)(2,1)S(1)}, bf16[80,1280]{1,0:T(8,128)(2,1)}, u32[]{:S(2)}) copy-start(bf16[80,1280]{1,0:T(8,128)(2,1)} %copy-done.7) | copy-start | bytes 614404
  136.5 5.5 %copy-start.12 = (bf16[320,384]{1,0:T(8,128)(2,1)S(1)}, bf16[320,384]{1,0:T(8,128)(2,1)}, u32[]{:S(2)}) copy-start(bf16[320,384]{1,0:T(8,128)(2,1)} %get-tuple-element.4) | copy-start | bytes 737284
  136.5 5.5 %copy-start.15 = (f32[384,2560]{1,0:T(8,128)S(1)}, f32[384,2560]{1,0:T(8,128)}, u32[]{:S(2)}) copy-start(f32[384,2560]{1,0:T(8,128)} %fusion.48) | copy-start | bytes 11796484
  136.5 6.0 %copy-start.16 = (f32[384,2560]{1,0:T(8,128)S(1)}, f32[384,2560]{1,0:T(8,128)}, u32[]{:S(2)}) copy-start(f32[384,2560]{1,0:T(8,128)} %fusion.60) | copy-start | bytes 11796484
  142.5 4.3 %copy-start.14 = (f32[384,2560]{1,0:T(8,128)S(1)}, f32[384,2560]{1,0:T(8,128)}, u32[]{:S(2)}) copy-start(f32[384,2560]{1,0:T(8,128)} %fusion.78) | copy-start | bytes 11796484
  (4 other events, 5.0 us)

commit v2 on v1

v2 whole, which is shorter than its diff:
```python
import functools

import jax
import jax.numpy as jnp
from jax import lax
from jax.experimental import pallas as pl
from jax.experimental.pallas import tpu as pltpu
from jax.sharding import PartitionSpec as P

BF16 = jnp.bfloat16
F32 = jnp.float32
LAST = (((1,), (1,)), ((), ()))
FIRST = (((0,), (0,)), ((), ()))
MATMUL = (((1,), (0,)), ((), ()))


def dot(a, b, dims):
    return lax.dot_general(a, b, dims, preferred_element_type=F32)


def targets(expert_of, expert_count, capacity, first):
    routed = expert_of[:, 0]
    chosen = (routed[:, None] == jnp.arange(expert_count, dtype=jnp.int32)[None, :]).astype(
        jnp.int32
    )
    slot_index = jnp.sum(chosen * (jnp.cumsum(chosen, axis=0) - 1), axis=1)
    return lax.rem(routed - first + expert_count, expert_count) * capacity + slot_index


def placement(target, slots_all):
    return (jnp.arange(slots_all, dtype=jnp.int32)[:, None] == target[None, :]).astype(BF16)


def gradients(gate_act, up_act, cotan):
    sigma = jax.nn.sigmoid(gate_act)
    cotan = cotan.astype(F32)
    d_gate = (cotan * up_act * sigma * (1.0 + gate_act * (1.0 - sigma))).astype(BF16)
    d_up = (cotan * gate_act * sigma).astype(BF16)
    return sigma, d_gate, d_up


def reduce_plan(tokens, expert_of, w_gate, w_up, d_hidden):
    expert_count = lax.axis_size("exp")
    replica_count = lax.axis_size("rep")
    capacity = d_hidden.shape[3]
    feature_width = tokens.shape[1]
    slots_all = expert_count * capacity
    placing = placement(targets(expert_of, expert_count, capacity, 0), slots_all)
    packed = dot(placing, tokens, MATMUL).astype(BF16)
    arrived = lax.all_to_all(
        packed.reshape(expert_count, capacity, feature_width), "exp", 0, 0, tiled=True
    )
    rows = arrived.reshape(slots_all, feature_width)
    gate_act, up_act = dot(rows, w_gate[0], LAST), dot(rows, w_up[0], LAST)
    cotan = d_hidden.reshape(slots_all, w_gate.shape[1])
    sigma, d_gate, d_up = gradients(gate_act, up_act, cotan)
    hidden = (gate_act * sigma * up_act).astype(BF16)

    def reduced(d_act):
        total = lax.psum(dot(d_act, rows, FIRST).astype(BF16), "rep").astype(F32)
        return (total * (1.0 / replica_count)).astype(BF16)[None]

    term = dot(d_gate, w_gate[0], MATMUL) + dot(d_up, w_up[0], MATMUL)
    outgoing = term.astype(BF16).reshape(expert_count, capacity, feature_width)
    returned = lax.all_to_all(outgoing, "exp", 0, 0, tiled=True)
    unpacked = dot(placing, returned.reshape(slots_all, feature_width), FIRST)
    d_tokens = lax.psum_scatter(unpacked.astype(BF16), "shard", scatter_dimension=1, tiled=True)
    return hidden.reshape(d_hidden.shape), d_tokens, reduced(d_gate), reduced(d_up)


def across(x, axis, bit):
    size = lax.axis_size(axis)
    return lax.ppermute(x, axis, [(i, i ^ bit) for i in range(size)])


def turned(x, axis, step):
    size = lax.axis_size(axis)
    return lax.ppermute(x, axis, [(i, (i + step) % size) for i in range(size)])


SMEM = pl.BlockSpec(memory_space=pltpu.SMEM)
VMEM = pl.BlockSpec(memory_space=pltpu.VMEM)
ANY = pl.BlockSpec(memory_space=pl.ANY)


def call(kernel, ins, outs, args, scratch=(), flops=0, name=None):
    moved = sum(a.size * a.dtype.itemsize for a in args)
    moved += sum(o.size * o.dtype.itemsize for o in outs)
    return pl.pallas_call(
        kernel,
        in_specs=ins,
        out_specs=[VMEM] * len(outs),
        out_shape=outs,
        scratch_shapes=list(scratch),
        compiler_params=pltpu.CompilerParams(vmem_limit_bytes=48 << 20),
        cost_estimate=pl.CostEstimate(flops=flops, transcendentals=0, bytes_accessed=moved),
        name=name,
    )(*args)


def like(*shape, dtype=BF16):
    return jax.ShapeDtypeStruct(shape, dtype)


def place_rows(expert_ref, count, capacity, first):
    tokens = expert_ref.shape[0]
    routed = jnp.transpose(jnp.broadcast_to(expert_ref[...], (tokens, tokens)))
    rows = lax.broadcasted_iota(jnp.int32, (tokens, tokens), 0)
    columns = lax.broadcasted_iota(jnp.int32, (tokens, tokens), 1)
    chosen = routed == rows
    before = dot(chosen.astype(BF16), (rows < columns).astype(BF16), MATMUL)
    slot = jnp.sum(jnp.where(chosen, before, 0.0), axis=0, keepdims=True).astype(jnp.int32)
    turn = routed[:1] - first
    target = jnp.where(turn < 0, turn + count, turn) * capacity + slot
    slots = lax.broadcasted_iota(jnp.int32, (count * capacity, tokens), 0)
    return (slots == target).astype(BF16)


def pack_kernel(count, capacity, ids, expert_ref, tokens_ref, *outs):
    half = tokens_ref.shape[1] // 2
    core = ids[1]
    placing = place_rows(expert_ref, count, capacity, ids[0])
    mine = tokens_ref[:, pl.ds(pl.multiple_of(core * half, 128), half)]
    theirs = tokens_ref[:, pl.ds(pl.multiple_of((1 - core) * half, 128), half)]
    packed = dot(placing, mine, MATMUL).astype(BF16)
    for k in range(count):
        outs[k][...] = packed[k * capacity : (k + 1) * capacity]
    outs[count][...] = dot(placing[:capacity], theirs, MATMUL).astype(BF16)


def unpack_kernel(count, capacity, ids, expert_ref, *refs):
    *pieces, out = refs
    placing = place_rows(expert_ref, count, capacity, ids[0])
    rows = jnp.concatenate([p[...] for p in pieces])
    out[...] = dot(placing, rows, FIRST).astype(BF16)


def sum_kernel(count, kept_ref, got_ref, *outs):
    capacity = kept_ref.shape[0] // count
    for k in range(count):
        at = pl.ds(k * capacity, capacity)
        outs[k][...] = (kept_ref[at].astype(F32) + got_ref[at].astype(F32)).astype(BF16)


def fill(pieces, others, full, core, sem):
    half = full.shape[1] // 2
    copies, start = [], 0
    for piece, other in zip(pieces, others):
        at = pl.ds(start, piece.shape[0])
        for ref, side in ((piece, core), (other, 1 - core)):
            columns = pl.ds(pl.multiple_of(side * half, 128), half)
            copies.append(pltpu.make_async_copy(ref, full.at[at, columns], sem.at[0]))
        start += piece.shape[0]
    return copies


def own_kernel(count, ids, *refs):
    pieces, others = refs[:count], refs[count : 2 * count]
    cotan_ref, gate_ref, up_ref = refs[2 * count : 2 * count + 3]
    full, d_gate_ref, d_up_ref, hidden_ref, kept_ref, sent_ref, sem = refs[2 * count + 3 :]
    me, core = ids[0], ids[1]
    capacity, half = pieces[0].shape[0], full.shape[1] // 2
    copies = fill(pieces, others, full, core, sem)
    for c in copies:
        c.start()
    for c in copies:
        c.wait()
    rows = full[...]
    gate_act, up_act = dot(rows, gate_ref[...], LAST), dot(rows, up_ref[...], LAST)
    for k in range(count):
        at = slice(k * capacity, (k + 1) * capacity)
        source = lax.rem(me - k + count, count)
        gate, up = gate_act[at], up_act[at]
        sigma, d_gate, d_up = gradients(gate, up, cotan_ref[source])
        hidden_ref[source] = (gate * sigma * up).astype(BF16)
        d_gate_ref[at] = d_gate
        d_up_ref[at] = d_up
    for side, out in ((1 - core, sent_ref), (core, kept_ref)):
        columns = pl.ds(pl.multiple_of(side * half, 128), half)
        term = dot(d_gate_ref[...], gate_ref[:, columns], MATMUL)
        term += dot(d_up_ref[...], up_ref[:, columns], MATMUL)
        out[...] = term.astype(BF16)


def part_kernel(count, blocks, ids, *refs):
    n = 2 * len(blocks)
    pieces, others = refs[:n], refs[n : 2 * n]
    cotans, (gate_ref, up_ref) = refs[2 * n : 2 * n + 3], refs[2 * n + 3 : 2 * n + 5]
    full, d_gate_ref, d_up_ref, sem = refs[2 * n + 5 :]
    me, core = ids[0], ids[1]
    copies = fill(pieces, others, full, core, sem)
    for c in copies:
        c.start()
    for c in copies:
        c.wait()
    rows = full[...]
    gate_act, up_act = dot(rows, gate_ref[...], LAST), dot(rows, up_ref[...], LAST)
    start, capacity = 0, pieces[0].shape[0]
    for k in blocks:
        source = lax.rem(me - k + count, count)
        for group in (k % 2, 1 - k % 2, 2):
            at = slice(start, start + capacity)
            _, d_gate, d_up = gradients(gate_act[at], up_act[at], cotans[group][source])
            d_gate_ref[at] = d_gate
            d_up_ref[at] = d_up
            start += capacity


def grad_kernel(scale, n, *refs):
    fulls, gates, ups = refs[:n], refs[n : 2 * n], refs[2 * n : 3 * n]
    for parts, out in ((gates, refs[3 * n]), (ups, refs[3 * n + 1])):
        total = sum(dot(d[...], full[...], FIRST) for d, full in zip(parts, fulls))
        out[...] = (total * scale).astype(BF16)


def gather_plan(tokens, expert_of, w_gate, w_up, d_hidden):
    count = lax.axis_size("exp")
    replica_count = lax.axis_size("rep")
    capacity = d_hidden.shape[3]
    width = tokens.shape[1]
    half = width // 2
    slots_all = count * capacity
    hidden_width = w_gate.shape[1]
    gate_rows, up_rows = w_gate[0], w_up[0]
    ids = jnp.stack([lax.axis_index("exp"), lax.axis_index("shard")]).astype(jnp.int32)
    cotan = d_hidden[0, 0]

    piece = like(capacity, half)
    *blocks, other = call(
        functools.partial(pack_kernel, count, capacity),
        [SMEM, VMEM, VMEM],
        [piece] * (count + 1),
        [ids, expert_of, tokens],
        flops=2 * tokens.size * slots_all,
        name="pack",
    )
    rows = [blocks[0]] + [turned(blocks[k], "exp", k) for k in range(1, count)]
    cotans = [across(cotan, "rep", bit) for bit in (1, 2, 3)]
    others = [other] + [across(r, "shard", 1) for r in rows[1:]]

    full, d_gate, d_up, hidden, kept, sent = call(
        functools.partial(own_kernel, count),
        [SMEM] + [ANY] * (2 * count) + [VMEM] * 3,
        [like(slots_all, width)]
        + [like(slots_all, hidden_width)] * 2
        + [like(count, capacity, hidden_width)]
        + [like(slots_all, half)] * 2,
        [ids, *rows, *others, cotan, gate_rows, up_rows],
        scratch=[pltpu.SemaphoreType.DMA((1,))],
        flops=8 * slots_all * width * hidden_width,
        name="own",
    )
    got = across(sent, "shard", 1)
    returns = call(
        functools.partial(sum_kernel, count), [VMEM] * 2, [piece] * count, [kept, got], name="sum"
    )
    returned = [returns[0]] + [turned(returns[k], "exp", -k) for k in range(1, count)]
    (d_tokens,) = call(
        functools.partial(unpack_kernel, count, capacity),
        [SMEM, VMEM] + [VMEM] * count,
        [like(tokens.shape[0], half)],
        [ids, expert_of, *returned],
        flops=2 * slots_all * tokens.shape[0] * half,
        name="unpack",
    )

    fulls, gates, ups = [full], [d_gate], [d_up]
    for pair in ((0, 1), (2, 3)):
        pieces = []
        for k in pair:
            near = across(rows[k], "rep", 1 + k % 2)
            far = across(jnp.concatenate([rows[k], near]), "rep", 2 - k % 2)
            pieces += [near, far]
        count_rows = sum(p.shape[0] for p in pieces)
        full, d_gate, d_up = call(
            functools.partial(part_kernel, count, pair),
            [SMEM] + [ANY] * (2 * len(pieces)) + [VMEM] * 5,
            [like(count_rows, width)] + [like(count_rows, hidden_width)] * 2,
            [ids, *pieces, *[across(p, "shard", 1) for p in pieces], *cotans, gate_rows, up_rows],
            scratch=[pltpu.SemaphoreType.DMA((1,))],
            flops=4 * count_rows * width * hidden_width,
            name="part",
        )
        fulls.append(full)
        gates.append(d_gate)
        ups.append(d_up)
    grad_gate, grad_up = call(
        functools.partial(grad_kernel, 1.0 / replica_count, len(fulls)),
        [VMEM] * (3 * len(fulls)),
        [like(hidden_width, width)] * 2,
        [*fulls, *gates, *ups],
        flops=4 * replica_count * slots_all * width * hidden_width,
        name="grads",
    )
    return hidden.reshape(d_hidden.shape), d_tokens, grad_gate[None], grad_up[None]


def local(tokens, expert_of, w_gate, w_up, d_hidden):
    replica_count, shard_count = lax.axis_size("rep"), lax.axis_size("shard")
    slots_all = d_hidden.shape[2] * d_hidden.shape[3]
    hidden_width, feature_width = w_gate.shape[1:]
    gathered = slots_all * (feature_width // shard_count + hidden_width) * replica_count
    reduced = 4 * hidden_width * feature_width
    if replica_count == 4 and shard_count == 2 and lax.axis_size("exp") == 4 and gathered < reduced:
        return gather_plan(tokens, expert_of, w_gate, w_up, d_hidden)
    return reduce_plan(tokens, expert_of, w_gate, w_up, d_hidden)


def solution(mesh):
    in_specs = (
        P(("rep", "exp"), None),
        P(("rep", "exp"), None),
        P("exp", "shard", None),
        P("exp", "shard", None),
        P("rep", "exp", None, None, "shard"),
    )
    out_specs = (
        P("rep", "exp", None, None, "shard"),
        P(("rep", "exp"), "shard"),
        P("exp", "shard", None),
        P("exp", "shard", None),
    )
    return jax.shard_map(local, mesh=mesh, in_specs=in_specs, out_specs=out_specs, check_vma=False)
```

time: 152 us -> 92.7 us (0.61)
  matrix products: 64 us -> 0 us
  Pallas kernels: 0 us -> 28.2 us
  waiting for transfers between devices: 36.8 us -> 22.3 us
  starting transfers between devices: 23 us -> 37.3 us
  other arithmetic: 13.4 us -> 0.18 us
  local copies, waits for them, and re-layouts: 12.8 us -> 3.02 us
    dot_general x14 -> x0, matrix products: 64 us -> none  [dot(): return lax.dot_general(a, b, dims, preferred_element_type=F32)]
    pallas_call x0 -> x7, Pallas kernels: none -> 28.2 us  [call(): pl.pallas_call(kernel, in_specs=ins, out_specs=[VMEM] * len(outs), out_sh...]
    ppermute x12 -> x23, starting transfers between devices: 12.6 us -> 27 us  [across(): return lax.ppermute(x, axis, [(i, i ^ bit) for i in range(size)])]
    ppermute x6, waiting for transfers between devices: 23.7 us -> 10.3 us  [turned(): return lax.ppermute(x, axis, [(i, (i + step) % size) for i in range(size)])]
    concatenate x5 -> x4, other arithmetic: 7.54 us -> 0.11 us  [gather_plan(): far = across(jnp.concatenate([rows[k], near]), 'rep', 2 - k % 2)]
    convert_element_type x3 -> x0, other arithmetic: 4.21 us -> none  [the longest x1 2.3 us: gather_plan(): d_packed = (kept + across(sent, 'shard', 1).astype(F32)).astype(BF16)]
    gather x2 -> x0, local copies, waits for them, and re-layouts: 3.76 us -> none  [the longest x1 2.22 us: gather_plan(): hidden = hidden.astype(BF16).reshape(d_hidden.shape[2:])[order]]
    unnamed x38 -> x13, local copies, waits for them, and re-layouts: 6.55 us -> 3.02 us
  transfers between devices with their start and end apart: 18 -> 29, of which waited for: 9 -> 7; matrix products, arithmetic and copies ran while one was open for 38% -> 0% of each run, Pallas kernels for 0% -> 27%
where the time goes in v2:
time: 92.7 us; the launch traced here: 91.8 us
  starting transfers between devices  37.3 us (40%)
  Pallas kernels  28.2 us (30%)
  waiting for transfers between devices  22.3 us (24%)
  local copies, waits for them, and re-layouts  3.02 us (3%)
    pallas_call x7, Pallas kernels, call(): pl.pallas_call(kernel, in_specs=ins, out_specs=[VMEM] * len(outs), out_sh...  28.2 us
    ppermute x23, starting transfers between devices, across(): return lax.ppermute(x, axis, [(i, i ^ bit) for i in range(size)])  27 us
    ppermute x23, waiting for transfers between devices, across(): return lax.ppermute(x, axis, [(i, i ^ bit) for i in range(size)])  12 us
    ppermute x6, starting transfers between devices, turned(): return lax.ppermute(x, axis, [(i, (i + step) % size) for i in range(size)])  10.4 us
    ppermute x6, waiting for transfers between devices, turned(): return lax.ppermute(x, axis, [(i, (i + step) % size) for i in range(size)])  10.3 us
    unnamed x13, local copies, waits for them, and re-layouts  3.02 us
  transfers between devices with their start and end apart: 29, of which 7 were waited for; matrix products, arithmetic and copies ran while one was open for 0% of the time, Pallas kernels for 27%

profile of v2, /device:TPU:9, one launch (start us, length us, event | category | flops | bytes accessed | tf_op | source)
XLA Modules:
  0.0 91.8 jit_solution(358880352961025962)
XLA Ops:
  1.5 1.1 %copy-done.2 = bf16[128,2560]{1,0:T(8,128)(2,1)S(1)} copy-done((bf16[128,2560]{1,0:T(8,128)(2,1)S(1)}, bf16[128,2560]{1,0:T(8,128)(2,1)}, u32[]{:S(2)}) %copy-start.2) | copy-done | bytes 655384
  2.6 1.2 %pack.1 = (bf16[80,1280]{1,0:T(8,128)(2,1)S(1)}, bf16[80,1280]{1,0:T(8,128)(2,1)S(1)}, bf16[80,1280]{1,0:T(8,128)(2,1)S(1)}, bf16[80,1280]{1,0:T(8,128)(2,1)S(1)}, bf16[80,1280]{1,0:T(8,128)(2,1)S(1)}) custom-call(s32[2]{0:T(128)S(1)} %pad_add_fusion.ids, s32[128,1]{1,0:T(8,128)S(1)} %copy.9.expert_ref, bf16[128,2560]{1,0:T(8,128)(2,1)S(1)} %copy-done.2), custom_call_target="tpu_custom_call" | custom-call | flops 209715200 | bytes 1679880 | tf_op jit(solution)/shard_map/pack/pallas_call | solution.py:89
  3.8 1.3 %collective-permute-start = (bf16[80,1280]{1,0:T(8,128)(2,1)S(1)}, bf16[80,1280]{1,0:T(8,128)(2,1)S(1)}, u32[]{:S(2)}, u32[]{:S(2)}) collective-permute-start(bf16[80,1280]{1,0:T(8,128)(2,1)S(1)} %get-tuple-element.28), channel_id=1, source_target_pairs={{0,1},{1,2},{2,3},{3,0},{4,5},{5,6},{6,7},{7,4},{8,9},{9,10},{10,1... | collective-permute-start | bytes 614408 | tf_op jit(solution)/shard_map/ppermute | solution.py:78
  5.2 1.2 %collective-permute-start.10 = (bf16[80,1280]{1,0:T(8,128)(2,1)S(1)}, bf16[80,1280]{1,0:T(8,128)(2,1)S(1)}, u32[]{:S(2)}, u32[]{:S(2)}) collective-permute-start(bf16[80,1280]{1,0:T(8,128)(2,1)S(1)} %get-tuple-element.27.refs_0_), channel_id=1, source_target_pairs={{0,8},{8,0},{16,24},{24,16},{1,9},{9,1},{17,25},{25,17},{2,10},{10... | collective-permute-start | bytes 614408 | tf_op jit(solution)/shard_map/ppermute | solution.py:73
  6.6 1.2 %collective-permute-start.19 = (bf16[4,80,384]{2,1,0:T(8,128)(2,1)}, bf16[4,80,384]{2,1,0:T(8,128)(2,1)S(1)}, u32[]{:S(2)}, u32[]{:S(2)}) collective-permute-start(bf16[4,80,384]{2,1,0:T(8,128)(2,1)} %bitcast.12), channel_id=1, source_target_pairs={{0,16},{8,24},{16,0},{24,8},{1,17},{9,25},{17,1},{25,9},{2,18},{10... | collective-permute-start | bytes 737288 | tf_op jit(solution)/shard_map/ppermute | solution.py:73
  7.9 1.1 %collective-permute-start.1 = (bf16[80,1280]{1,0:T(8,128)(2,1)S(1)}, bf16[80,1280]{1,0:T(8,128)(2,1)S(1)}, u32[]{:S(2)}, u32[]{:S(2)}) collective-permute-start(bf16[80,1280]{1,0:T(8,128)(2,1)S(1)} %get-tuple-element.29), channel_id=1, source_target_pairs={{0,2},{1,3},{2,0},{3,1},{4,6},{5,7},{6,4},{7,5},{8,10},{9,11},{10,... | collective-permute-start | bytes 614408 | tf_op jit(solution)/shard_map/ppermute | solution.py:78
  9.8 2.4 %collective-permute-start.2 = (bf16[80,1280]{1,0:T(8,128)(2,1)S(1)}, bf16[80,1280]{1,0:T(8,128)(2,1)S(1)}, u32[]{:S(2)}, u32[]{:S(2)}) collective-permute-start(bf16[80,1280]{1,0:T(8,128)(2,1)S(1)} %get-tuple-element.30), channel_id=1, source_target_pairs={{0,3},{1,0},{2,1},{3,2},{4,7},{5,4},{6,5},{7,6},{8,11},{9,8},{10,9... | collective-permute-start | bytes 614408 | tf_op jit(solution)/shard_map/ppermute | solution.py:78
  12.2 1.0 %collective-permute-start.12 = (bf16[80,1280]{1,0:T(8,128)(2,1)S(1)}, bf16[80,1280]{1,0:T(8,128)(2,1)S(1)}, u32[]{:S(2)}, u32[]{:S(2)}) collective-permute-start(bf16[80,1280]{1,0:T(8,128)(2,1)S(1)} %collective-permute-done.refs_1_), channel_id=1, source_target_pairs={{0,16},{8,24},{16,0},{24,8},{1,17},{9,25},{17,1},{25,9},{2,18},{10... | collective-permute-start | bytes 614408 | tf_op jit(solution)/shard_map/ppermute | solution.py:73
  13.2 9.4 %collective-permute-done.1.refs_2_ = bf16[80,1280]{1,0:T(8,128)(2,1)S(1)} collective-permute-done((bf16[80,1280]{1,0:T(8,128)(2,1)S(1)}, bf16[80,1280]{1,0:T(8,128)(2,1)S(1)}, u32[]{:S(2)}, u32[]{:S(2)}) %collective-permute-start.1) | collective-permute-done | bytes 204832 | tf_op jit(solution)/shard_map/ppermute | solution.py:78
  22.5 1.1 %collective-permute-start.3 = (bf16[80,1280]{1,0:T(8,128)(2,1)S(1)}, bf16[80,1280]{1,0:T(8,128)(2,1)S(1)}, u32[]{:S(2)}, u32[]{:S(2)}) collective-permute-start(bf16[80,1280]{1,0:T(8,128)(2,1)S(1)} %collective-permute-done.refs_1_), channel_id=1, source_target_pairs={{0,4},{4,0},{1,5},{5,1},{2,6},{6,2},{3,7},{7,3},{8,12},{12,8},{9,1... | collective-permute-start | bytes 614408 | tf_op jit(solution)/shard_map/ppermute | solution.py:73
  23.6 1.2 %collective-permute-start.21 = (bf16[80,1280]{1,0:T(8,128)(2,1)S(1)}, bf16[80,1280]{1,0:T(8,128)(2,1)S(1)}, u32[]{:S(2)}, u32[]{:S(2)}) collective-permute-start(bf16[80,1280]{1,0:T(8,128)(2,1)S(1)} %collective-permute-done.1.refs_2_), channel_id=1, source_target_pairs={{0,8},{8,0},{16,24},{24,16},{1,9},{9,1},{17,25},{25,17},{2,10},{10... | collective-permute-start | bytes 614408 | tf_op jit(solution)/shard_map/ppermute | solution.py:73
  24.9 1.2 %collective-permute-start.20 = (bf16[4,80,384]{2,1,0:T(8,128)(2,1)S(1)}, bf16[4,80,384]{2,1,0:T(8,128)(2,1)S(1)}, u32[]{:S(2)}, u32[]{:S(2)}) collective-permute-start(bf16[4,80,384]{2,1,0:T(8,128)(2,1)S(1)} %bitcast.13), channel_id=1, source_target_pairs={{0,24},{8,16},{16,8},{24,0},{1,25},{9,17},{17,9},{25,1},{2,26},{10... | collective-permute-start | bytes 737288 | tf_op jit(solution)/shard_map/ppermute | solution.py:73
  26.2 3.1 %collective-permute-start.4 = (bf16[80,1280]{1,0:T(8,128)(2,1)S(1)}, bf16[80,1280]{1,0:T(8,128)(2,1)S(1)}, u32[]{:S(2)}, u32[]{:S(2)}) collective-permute-start(bf16[80,1280]{1,0:T(8,128)(2,1)S(1)} %collective-permute-done.1.refs_2_), channel_id=1, source_target_pairs={{0,4},{4,0},{1,5},{5,1},{2,6},{6,2},{3,7},{7,3},{8,12},{12,8},{9,1... | collective-permute-start | bytes 614408 | tf_op jit(solution)/shard_map/ppermute | solution.py:73
  29.2 4.3 %collective-permute-start.5 = (bf16[80,1280]{1,0:T(8,128)(2,1)S(1)}, bf16[80,1280]{1,0:T(8,128)(2,1)S(1)}, u32[]{:S(2)}, u32[]{:S(2)}) collective-permute-start(bf16[80,1280]{1,0:T(8,128)(2,1)S(1)} %collective-permute-done.2.refs_3_), channel_id=1, source_target_pairs={{0,4},{4,0},{1,5},{5,1},{2,6},{6,2},{3,7},{7,3},{8,12},{12,8},{9,1... | collective-permute-start | bytes 614408 | tf_op jit(solution)/shard_map/ppermute | solution.py:73
  33.6 1.5 %collective-permute-start.11 = (bf16[160,1280]{1,0:T(8,128)(2,1)S(1)}, bf16[160,1280]{1,0:T(8,128)(2,1)S(1)}, u32[]{:S(2)}, u32[]{:S(2)}) collective-permute-start(bf16[160,1280]{1,0:T(8,128)(2,1)S(1)} %pad_maximum_fusion), channel_id=1, source_target_pairs={{0,16},{8,24},{16,0},{24,8},{1,17},{9,25},{17,1},{25,9},{2,18},{10... | collective-permute-start | bytes 1228808 | tf_op jit(solution)/shard_map/ppermute | solution.py:73
  35.1 1.0 %collective-permute-start.23 = (bf16[80,1280]{1,0:T(8,128)(2,1)S(1)}, bf16[80,1280]{1,0:T(8,128)(2,1)S(1)}, u32[]{:S(2)}, u32[]{:S(2)}) collective-permute-start(bf16[80,1280]{1,0:T(8,128)(2,1)S(1)} %collective-permute-done.2.refs_3_), channel_id=1, source_target_pairs={{0,16},{8,24},{16,0},{24,8},{1,17},{9,25},{17,1},{25,9},{2,18},{10... | collective-permute-start | bytes 614408 | tf_op jit(solution)/shard_map/ppermute | solution.py:73
  36.1 6.1 %own.1 = (bf16[320,2560]{1,0:T(8,128)(2,1)S(1)}, bf16[320,384]{1,0:T(8,128)(2,1)S(1)}, bf16[320,384]{1,0:T(8,128)(2,1)S(1)}, bf16[4,80,384]{2,1,0:T(8,128)(2,1)}...) custom-call(s32[2]{0:T(128)S(1)} %pad_add_fusion.ids, bf16[80,1280]{1,0:T(8,128)(2,1)S(1)} %get-tuple-element.27.refs_0_, ...), custom_call_target="tpu_custom_call" | custom-call | flops 2516582400 | bytes 9830408 | tf_op jit(solution)/shard_map/own/pallas_call | solution.py:89
  42.2 1.2 %copy-done.4 = bf16[320,2560]{1,0:T(8,128)(2,1)} copy-done((bf16[320,2560]{1,0:T(8,128)(2,1)}, bf16[320,2560]{1,0:T(8,128)(2,1)S(1)}, u32[]{:S(2)}) %copy-start.4) | copy-done | bytes 1638424
  44.1 1.2 %collective-permute-start.13 = (bf16[160,1280]{1,0:T(8,128)(2,1)S(1)}, bf16[160,1280]{1,0:T(8,128)(2,1)S(1)}, u32[]{:S(2)}, u32[]{:S(2)}) collective-permute-start(bf16[160,1280]{1,0:T(8,128)(2,1)S(1)} %pad_maximum_fusion.1), channel_id=1, source_target_pairs={{0,8},{8,0},{16,24},{24,16},{1,9},{9,1},{17,25},{25,17},{2,10},{10... | collective-permute-start | bytes 1228808 | tf_op jit(solution)/shard_map/ppermute | solution.py:73
  45.3 4.8 %collective-permute-done.23.refs_2_ = bf16[80,1280]{1,0:T(8,128)(2,1)S(1)} collective-permute-done((bf16[80,1280]{1,0:T(8,128)(2,1)S(1)}, bf16[80,1280]{1,0:T(8,128)(2,1)S(1)}, u32[]{:S(2)}, u32[]{:S(2)}) %collective-permute-start.23) | collective-permute-done | bytes 204832 | tf_op jit(solution)/shard_map/ppermute | solution.py:73
  51.5 1.2 %collective-permute-start.24 = (bf16[160,1280]{1,0:T(8,128)(2,1)S(1)}, bf16[160,1280]{1,0:T(8,128)(2,1)S(1)}, u32[]{:S(2)}, u32[]{:S(2)}) collective-permute-start(bf16[160,1280]{1,0:T(8,128)(2,1)S(1)} %pad_maximum_fusion.3), channel_id=1, source_target_pairs={{0,8},{8,0},{16,24},{24,16},{1,9},{9,1},{17,25},{25,17},{2,10},{10... | collective-permute-start | bytes 1228808 | tf_op jit(solution)/shard_map/ppermute | solution.py:73
  53.3 1.4 %collective-permute-done.13.refs_3_ = bf16[160,1280]{1,0:T(8,128)(2,1)S(1)} collective-permute-done((bf16[160,1280]{1,0:T(8,128)(2,1)S(1)}, bf16[160,1280]{1,0:T(8,128)(2,1)S(1)}, u32[]{:S(2)}, u32[]{:S(2)}) %collective-permute-start.13) | collective-permute-done | bytes 409632 | tf_op jit(solution)/shard_map/ppermute | solution.py:73
  54.7 2.1 %collective-permute-start.17 = (bf16[160,1280]{1,0:T(8,128)(2,1)S(1)}, bf16[160,1280]{1,0:T(8,128)(2,1)S(1)}, u32[]{:S(2)}, u32[]{:S(2)}) collective-permute-start(bf16[160,1280]{1,0:T(8,128)(2,1)S(1)} %collective-permute-done.13.refs_3_), channel_id=1, source_target_pairs={{0,4},{4,0},{1,5},{5,1},{2,6},{6,2},{3,7},{7,3},{8,12},{12,8},{9,1... | collective-permute-start | bytes 1228808 | tf_op jit(solution)/shard_map/ppermute | solution.py:73
  56.8 4.8 %collective-permute-done.22.refs_1_ = bf16[160,1280]{1,0:T(8,128)(2,1)S(1)} collective-permute-done((bf16[160,1280]{1,0:T(8,128)(2,1)S(1)}, bf16[160,1280]{1,0:T(8,128)(2,1)S(1)}, u32[]{:S(2)}, u32[]{:S(2)}) %collective-permute-start.22) | collective-permute-done | bytes 409632 | tf_op jit(solution)/shard_map/ppermute | solution.py:73
  62.5 1.0 %collective-permute-done.24.refs_3_ = bf16[160,1280]{1,0:T(8,128)(2,1)S(1)} collective-permute-done((bf16[160,1280]{1,0:T(8,128)(2,1)S(1)}, bf16[160,1280]{1,0:T(8,128)(2,1)S(1)}, u32[]{:S(2)}, u32[]{:S(2)}) %collective-permute-start.24) | collective-permute-done | bytes 409632 | tf_op jit(solution)/shard_map/ppermute | solution.py:73
  63.5 1.3 %collective-permute-start.28 = (bf16[160,1280]{1,0:T(8,128)(2,1)S(1)}, bf16[160,1280]{1,0:T(8,128)(2,1)S(1)}, u32[]{:S(2)}, u32[]{:S(2)}) collective-permute-start(bf16[160,1280]{1,0:T(8,128)(2,1)S(1)} %collective-permute-done.24.refs_3_), channel_id=1, source_target_pairs={{0,4},{4,0},{1,5},{5,1},{2,6},{6,2},{3,7},{7,3},{8,12},{12,8},{9,1... | collective-permute-start | bytes 1228808 | tf_op jit(solution)/shard_map/ppermute | solution.py:73
  65.5 4.7 %part.2 = (bf16[480,2560]{1,0:T(8,128)(2,1)}, bf16[480,384]{1,0:T(8,128)(2,1)S(1)}, bf16[480,384]{1,0:T(8,128)(2,1)S(1)}) custom-call(s32[2]{0:T(128)S(1)} %pad_add_fusion.ids, bf16[80,1280]{1,0:T(8,128)(2,1)S(1)} %collective-permute-done.10.refs_0_, bf16[160,1280]{1,0:T(8,128)(2,1)S(1)} %collective-permute-done.11.refs_1_, ...), custom_call_target="tpu_custom_call" | custom-call | flops 1887436800 | bytes 10321928 | tf_op jit(solution)/shard_map/part/pallas_call | solution.py:89
  70.3 3.2 %collective-permute-start.8 = (bf16[80,1280]{1,0:T(8,128)(2,1)S(1)}, bf16[80,1280]{1,0:T(8,128)(2,1)S(1)}, u32[]{:S(2)}, u32[]{:S(2)}) collective-permute-start(bf16[80,1280]{1,0:T(8,128)(2,1)S(1)} %get-tuple-element.37), channel_id=1, source_target_pairs={{0,2},{1,3},{2,0},{3,1},{4,6},{5,7},{6,4},{7,5},{8,10},{9,11},{10,... | collective-permute-start | bytes 614408 | tf_op jit(solution)/shard_map/ppermute | solution.py:78
  73.4 2.3 %collective-permute-start.9 = (bf16[80,1280]{1,0:T(8,128)(2,1)S(1)}, bf16[80,1280]{1,0:T(8,128)(2,1)S(1)}, u32[]{:S(2)}, u32[]{:S(2)}) collective-permute-start(bf16[80,1280]{1,0:T(8,128)(2,1)S(1)} %get-tuple-element.38), channel_id=1, source_target_pairs={{0,1},{1,2},{2,3},{3,0},{4,5},{5,6},{6,7},{7,4},{8,9},{9,10},{10,1... | collective-permute-start | bytes 614408 | tf_op jit(solution)/shard_map/ppermute | solution.py:78
  75.8 4.7 %part.3 = (bf16[480,2560]{1,0:T(8,128)(2,1)}, bf16[480,384]{1,0:T(8,128)(2,1)S(1)}, bf16[480,384]{1,0:T(8,128)(2,1)S(1)}) custom-call(s32[2]{0:T(128)S(1)} %pad_add_fusion.ids, bf16[80,1280]{1,0:T(8,128)(2,1)S(1)} %collective-permute-done.21.refs_0_, bf16[160,1280]{1,0:T(8,128)(2,1)S(1)} %collective-permute-done.22.refs_1_, ...), custom_call_target="tpu_custom_call" | custom-call | flops 1887436800 | bytes 10321928 | tf_op jit(solution)/shard_map/part/pallas_call | solution.py:89
  80.5 9.3 %grads.1 = (bf16[384,2560]{1,0:T(8,128)(2,1)}, bf16[384,2560]{1,0:T(8,128)(2,1)}) custom-call(bf16[320,2560]{1,0:T(8,128)(2,1)S(1)} %copy-done.5, bf16[480,2560]{1,0:T(8,128)(2,1)S(1)} %copy-done.1, bf16[480,2560]{1,0:T(8,128)(2,1)} %get-tuple-element.41.refs_2_, bf16[320,384]{1,0:T(8,128)(2,1)S(1)} %get-tuple-element.42.refs_3_, ...), custom_call_target="tpu_custom_call" | custom-call | flops 5033164800 | bytes 12451840 | tf_op jit(solution)/shard_map/grads/pallas_call | solution.py:89
  89.9 1.9 %unpack.1 = bf16[128,1280]{1,0:T(8,128)(2,1)} custom-call(s32[2]{0:T(128)S(1)} %pad_add_fusion.ids, s32[128,1]{1,0:T(8,128)S(1)} %copy.9.expert_ref, bf16[80,1280]{1,0:T(8,128)(2,1)S(1)} %get-tuple-element.35.refs_0_, bf16[80,1280]{1,0:T(8,128)(2,1)S(1)} %collective-permute-done.7.refs_1_, bf16[80,1280]{1,0:T(8,128)(2,1)S(1)} %collective-permute-done.8.refs_2_, ...), custom_call_target="tpu_custom_call" | custom-call | flops 104857600 | bytes 1147400 | tf_op jit(solution)/shard_map/unpack/pallas_call | solution.py:89
  (51 shorter events, 6.5 us)
Async XLA Ops:
  2.6 22.4 %copy-start.3 = (bf16[1,1,4,80,384]{4,3,2,1,0:T(8,128)(2,1)S(1)}, bf16[1,1,4,80,384]{4,3,2,1,0:T(8,128)(2,1)}, u32[]{:S(2)}) copy-start(bf16[1,1,4,80,384]{4,3,2,1,0:T(8,128)(2,1)} %param.9) | copy-start | bytes 737284
  3.8 6.0 %collective-permute-start = (bf16[80,1280]{1,0:T(8,128)(2,1)S(1)}, bf16[80,1280]{1,0:T(8,128)(2,1)S(1)}, u32[]{:S(2)}, u32[]{:S(2)}) collective-permute-start(bf16[80,1280]{1,0:T(8,128)(2,1)S(1)} %get-tuple-element.28), channel_id=1, source_target_pairs={{0,1},{1,2},{2,3},{3,0},{4,5},{5,6},{6,7},{7,4},{8,9},{9,10},{10,1... | collective-permute-start | bytes 614408 | tf_op jit(solution)/shard_map/ppermute | solution.py:78
  5.2 7.0 %collective-permute-start.10 = (bf16[80,1280]{1,0:T(8,128)(2,1)S(1)}, bf16[80,1280]{1,0:T(8,128)(2,1)S(1)}, u32[]{:S(2)}, u32[]{:S(2)}) collective-permute-start(bf16[80,1280]{1,0:T(8,128)(2,1)S(1)} %get-tuple-element.27.refs_0_), channel_id=1, source_target_pairs={{0,8},{8,0},{16,24},{24,16},{1,9},{9,1},{17,25},{25,17},{2,10},{10... | collective-permute-start | bytes 614408 | tf_op jit(solution)/shard_map/ppermute | solution.py:73
  6.4 36.9 %collective-permute-start.18 = (bf16[4,80,384]{2,1,0:T(8,128)(2,1)}, bf16[4,80,384]{2,1,0:T(8,128)(2,1)S(1)}, u32[]{:S(2)}, u32[]{:S(2)}) collective-permute-start(bf16[4,80,384]{2,1,0:T(8,128)(2,1)} %bitcast.11), channel_id=1, source_target_pairs={{0,8},{8,0},{16,24},{24,16},{1,9},{9,1},{17,25},{25,17},{2,10},{10... | collective-permute-start | bytes 737288 | tf_op jit(solution)/shard_map/ppermute | solution.py:73
  6.6 37.4 %collective-permute-start.19 = (bf16[4,80,384]{2,1,0:T(8,128)(2,1)}, bf16[4,80,384]{2,1,0:T(8,128)(2,1)S(1)}, u32[]{:S(2)}, u32[]{:S(2)}) collective-permute-start(bf16[4,80,384]{2,1,0:T(8,128)(2,1)} %bitcast.12), channel_id=1, source_target_pairs={{0,16},{8,24},{16,0},{24,8},{1,17},{9,25},{17,1},{25,9},{2,18},{10... | collective-permute-start | bytes 737288 | tf_op jit(solution)/shard_map/ppermute | solution.py:73
  7.9 14.7 %collective-permute-start.1 = (bf16[80,1280]{1,0:T(8,128)(2,1)S(1)}, bf16[80,1280]{1,0:T(8,128)(2,1)S(1)}, u32[]{:S(2)}, u32[]{:S(2)}) collective-permute-start(bf16[80,1280]{1,0:T(8,128)(2,1)S(1)} %get-tuple-element.29), channel_id=1, source_target_pairs={{0,2},{1,3},{2,0},{3,1},{4,6},{5,7},{6,4},{7,5},{8,10},{9,11},{10,... | collective-permute-start | bytes 614408 | tf_op jit(solution)/shard_map/ppermute | solution.py:78
  9.8 15.1 %collective-permute-start.2 = (bf16[80,1280]{1,0:T(8,128)(2,1)S(1)}, bf16[80,1280]{1,0:T(8,128)(2,1)S(1)}, u32[]{:S(2)}, u32[]{:S(2)}) collective-permute-start(bf16[80,1280]{1,0:T(8,128)(2,1)S(1)} %get-tuple-element.30), channel_id=1, source_target_pairs={{0,3},{1,0},{2,1},{3,2},{4,7},{5,4},{6,5},{7,6},{8,11},{9,8},{10,9... | collective-permute-start | bytes 614408 | tf_op jit(solution)/shard_map/ppermute | solution.py:78
  12.2 11.5 %collective-permute-start.12 = (bf16[80,1280]{1,0:T(8,128)(2,1)S(1)}, bf16[80,1280]{1,0:T(8,128)(2,1)S(1)}, u32[]{:S(2)}, u32[]{:S(2)}) collective-permute-start(bf16[80,1280]{1,0:T(8,128)(2,1)S(1)} %collective-permute-done.refs_1_), channel_id=1, source_target_pairs={{0,16},{8,24},{16,0},{24,8},{1,17},{9,25},{17,1},{25,9},{2,18},{10... | collective-permute-start | bytes 614408 | tf_op jit(solution)/shard_map/ppermute | solution.py:73
  22.5 3.6 %collective-permute-start.3 = (bf16[80,1280]{1,0:T(8,128)(2,1)S(1)}, bf16[80,1280]{1,0:T(8,128)(2,1)S(1)}, u32[]{:S(2)}, u32[]{:S(2)}) collective-permute-start(bf16[80,1280]{1,0:T(8,128)(2,1)S(1)} %collective-permute-done.refs_1_), channel_id=1, source_target_pairs={{0,4},{4,0},{1,5},{5,1},{2,6},{6,2},{3,7},{7,3},{8,12},{12,8},{9,1... | collective-permute-start | bytes 614408 | tf_op jit(solution)/shard_map/ppermute | solution.py:73
  23.6 5.6 %collective-permute-start.21 = (bf16[80,1280]{1,0:T(8,128)(2,1)S(1)}, bf16[80,1280]{1,0:T(8,128)(2,1)S(1)}, u32[]{:S(2)}, u32[]{:S(2)}) collective-permute-start(bf16[80,1280]{1,0:T(8,128)(2,1)S(1)} %collective-permute-done.1.refs_2_), channel_id=1, source_target_pairs={{0,8},{8,0},{16,24},{24,16},{1,9},{9,1},{17,25},{25,17},{2,10},{10... | collective-permute-start | bytes 614408 | tf_op jit(solution)/shard_map/ppermute | solution.py:73
  24.9 19.1 %collective-permute-start.20 = (bf16[4,80,384]{2,1,0:T(8,128)(2,1)S(1)}, bf16[4,80,384]{2,1,0:T(8,128)(2,1)S(1)}, u32[]{:S(2)}, u32[]{:S(2)}) collective-permute-start(bf16[4,80,384]{2,1,0:T(8,128)(2,1)S(1)} %bitcast.13), channel_id=1, source_target_pairs={{0,24},{8,16},{16,8},{24,0},{1,25},{9,17},{17,9},{25,1},{2,26},{10... | collective-permute-start | bytes 737288 | tf_op jit(solution)/shard_map/ppermute | solution.py:73
  26.2 7.5 %collective-permute-start.4 = (bf16[80,1280]{1,0:T(8,128)(2,1)S(1)}, bf16[80,1280]{1,0:T(8,128)(2,1)S(1)}, u32[]{:S(2)}, u32[]{:S(2)}) collective-permute-start(bf16[80,1280]{1,0:T(8,128)(2,1)S(1)} %collective-permute-done.1.refs_2_), channel_id=1, source_target_pairs={{0,4},{4,0},{1,5},{5,1},{2,6},{6,2},{3,7},{7,3},{8,12},{12,8},{9,1... | collective-permute-start | bytes 614408 | tf_op jit(solution)/shard_map/ppermute | solution.py:73
  29.2 5.8 %collective-permute-start.5 = (bf16[80,1280]{1,0:T(8,128)(2,1)S(1)}, bf16[80,1280]{1,0:T(8,128)(2,1)S(1)}, u32[]{:S(2)}, u32[]{:S(2)}) collective-permute-start(bf16[80,1280]{1,0:T(8,128)(2,1)S(1)} %collective-permute-done.2.refs_3_), channel_id=1, source_target_pairs={{0,4},{4,0},{1,5},{5,1},{2,6},{6,2},{3,7},{7,3},{8,12},{12,8},{9,1... | collective-permute-start | bytes 614408 | tf_op jit(solution)/shard_map/ppermute | solution.py:73
  33.6 17.8 %collective-permute-start.11 = (bf16[160,1280]{1,0:T(8,128)(2,1)S(1)}, bf16[160,1280]{1,0:T(8,128)(2,1)S(1)}, u32[]{:S(2)}, u32[]{:S(2)}) collective-permute-start(bf16[160,1280]{1,0:T(8,128)(2,1)S(1)} %pad_maximum_fusion), channel_id=1, source_target_pairs={{0,16},{8,24},{16,0},{24,8},{1,17},{9,25},{17,1},{25,9},{2,18},{10... | collective-permute-start | bytes 1228808 | tf_op jit(solution)/shard_map/ppermute | solution.py:73
  35.1 15.0 %collective-permute-start.23 = (bf16[80,1280]{1,0:T(8,128)(2,1)S(1)}, bf16[80,1280]{1,0:T(8,128)(2,1)S(1)}, u32[]{:S(2)}, u32[]{:S(2)}) collective-permute-start(bf16[80,1280]{1,0:T(8,128)(2,1)S(1)} %collective-permute-done.2.refs_3_), channel_id=1, source_target_pairs={{0,16},{8,24},{16,0},{24,8},{1,17},{9,25},{17,1},{25,9},{2,18},{10... | collective-permute-start | bytes 614408 | tf_op jit(solution)/shard_map/ppermute | solution.py:73
  43.3 22.2 %copy-start = (bf16[1,384,2560]{2,1,0:T(8,128)(2,1)S(1)}, bf16[1,384,2560]{2,1,0:T(8,128)(2,1)}, u32[]{:S(2)}) copy-start(bf16[1,384,2560]{2,1,0:T(8,128)(2,1)} %param.7) | copy-start | bytes 5898244
  43.3 7.2 %collective-permute-start.14 = (bf16[80,1280]{1,0:T(8,128)(2,1)S(1)}, bf16[80,1280]{1,0:T(8,128)(2,1)S(1)}, u32[]{:S(2)}, u32[]{:S(2)}) collective-permute-start(bf16[80,1280]{1,0:T(8,128)(2,1)S(1)} %collective-permute-done.10.refs_0_), channel_id=1, source_target_pairs={{0,4},{4,0},{1,5},{5,1},{2,6},{6,2},{3,7},{7,3},{8,12},{12,8},{9,1... | collective-permute-start | bytes 614408 | tf_op jit(solution)/shard_map/ppermute | solution.py:73
  44.0 20.8 %collective-permute-start.6 = (bf16[320,1280]{1,0:T(8,128)(2,1)S(1)}, bf16[320,1280]{1,0:T(8,128)(2,1)S(1)}, u32[]{:S(2)}, u32[]{:S(2)}) collective-permute-start(bf16[320,1280]{1,0:T(8,128)(2,1)S(1)} %get-tuple-element.34), channel_id=1, source_target_pairs={{0,4},{4,0},{1,5},{5,1},{2,6},{6,2},{3,7},{7,3},{8,12},{12,8},{9,1... | collective-permute-start | bytes 2457608 | tf_op jit(solution)/shard_map/ppermute | solution.py:73
  44.1 10.6 %collective-permute-start.13 = (bf16[160,1280]{1,0:T(8,128)(2,1)S(1)}, bf16[160,1280]{1,0:T(8,128)(2,1)S(1)}, u32[]{:S(2)}, u32[]{:S(2)}) collective-permute-start(bf16[160,1280]{1,0:T(8,128)(2,1)S(1)} %pad_maximum_fusion.1), channel_id=1, source_target_pairs={{0,8},{8,0},{16,24},{24,16},{1,9},{9,1},{17,25},{25,17},{2,10},{10... | collective-permute-start | bytes 1228808 | tf_op jit(solution)/shard_map/ppermute | solution.py:73
  50.1 2.6 %collective-permute-start.16 = (bf16[80,1280]{1,0:T(8,128)(2,1)S(1)}, bf16[80,1280]{1,0:T(8,128)(2,1)S(1)}, u32[]{:S(2)}, u32[]{:S(2)}) collective-permute-start(bf16[80,1280]{1,0:T(8,128)(2,1)S(1)} %collective-permute-done.12.refs_2_), channel_id=1, source_target_pairs={{0,4},{4,0},{1,5},{5,1},{2,6},{6,2},{3,7},{7,3},{8,12},{12,8},{9,1... | collective-permute-start | bytes 614408 | tf_op jit(solution)/shard_map/ppermute | solution.py:73
  50.5 11.1 %collective-permute-start.22 = (bf16[160,1280]{1,0:T(8,128)(2,1)S(1)}, bf16[160,1280]{1,0:T(8,128)(2,1)S(1)}, u32[]{:S(2)}, u32[]{:S(2)}) collective-permute-start(bf16[160,1280]{1,0:T(8,128)(2,1)S(1)} %pad_maximum_fusion.2), channel_id=1, source_target_pairs={{0,16},{8,24},{16,0},{24,8},{1,17},{9,25},{17,1},{25,9},{2,18},{10... | collective-permute-start | bytes 1228808 | tf_op jit(solution)/shard_map/ppermute | solution.py:73
  51.5 12.0 %collective-permute-start.24 = (bf16[160,1280]{1,0:T(8,128)(2,1)S(1)}, bf16[160,1280]{1,0:T(8,128)(2,1)S(1)}, u32[]{:S(2)}, u32[]{:S(2)}) collective-permute-start(bf16[160,1280]{1,0:T(8,128)(2,1)S(1)} %pad_maximum_fusion.3), channel_id=1, source_target_pairs={{0,8},{8,0},{16,24},{24,16},{1,9},{9,1},{17,25},{25,17},{2,10},{10... | collective-permute-start | bytes 1228808 | tf_op jit(solution)/shard_map/ppermute | solution.py:73
  52.7 12.0 %collective-permute-start.15 = (bf16[160,1280]{1,0:T(8,128)(2,1)S(1)}, bf16[160,1280]{1,0:T(8,128)(2,1)S(1)}, u32[]{:S(2)}, u32[]{:S(2)}) collective-permute-start(bf16[160,1280]{1,0:T(8,128)(2,1)S(1)} %collective-permute-done.11.refs_1_), channel_id=1, source_target_pairs={{0,4},{4,0},{1,5},{5,1},{2,6},{6,2},{3,7},{7,3},{8,12},{12,8},{9,1... | collective-permute-start | bytes 1228808 | tf_op jit(solution)/shard_map/ppermute | solution.py:73
  54.7 10.8 %collective-permute-start.17 = (bf16[160,1280]{1,0:T(8,128)(2,1)S(1)}, bf16[160,1280]{1,0:T(8,128)(2,1)S(1)}, u32[]{:S(2)}, u32[]{:S(2)}) collective-permute-start(bf16[160,1280]{1,0:T(8,128)(2,1)S(1)} %collective-permute-done.13.refs_3_), channel_id=1, source_target_pairs={{0,4},{4,0},{1,5},{5,1},{2,6},{6,2},{3,7},{7,3},{8,12},{12,8},{9,1... | collective-permute-start | bytes 1228808 | tf_op jit(solution)/shard_map/ppermute | solution.py:73
  61.6 14.2 %collective-permute-start.26 = (bf16[160,1280]{1,0:T(8,128)(2,1)S(1)}, bf16[160,1280]{1,0:T(8,128)(2,1)S(1)}, u32[]{:S(2)}, u32[]{:S(2)}) collective-permute-start(bf16[160,1280]{1,0:T(8,128)(2,1)S(1)} %collective-permute-done.22.refs_1_), channel_id=1, source_target_pairs={{0,4},{4,0},{1,5},{5,1},{2,6},{6,2},{3,7},{7,3},{8,12},{12,8},{9,1... | collective-permute-start | bytes 1228808 | tf_op jit(solution)/shard_map/ppermute | solution.py:73
  63.5 12.3 %collective-permute-start.28 = (bf16[160,1280]{1,0:T(8,128)(2,1)S(1)}, bf16[160,1280]{1,0:T(8,128)(2,1)S(1)}, u32[]{:S(2)}, u32[]{:S(2)}) collective-permute-start(bf16[160,1280]{1,0:T(8,128)(2,1)S(1)} %collective-permute-done.24.refs_3_), channel_id=1, source_target_pairs={{0,4},{4,0},{1,5},{5,1},{2,6},{6,2},{3,7},{7,3},{8,12},{12,8},{9,1... | collective-permute-start | bytes 1228808 | tf_op jit(solution)/shard_map/ppermute | solution.py:73
  64.7 5.5 %collective-permute-start.25 = (bf16[80,1280]{1,0:T(8,128)(2,1)S(1)}, bf16[80,1280]{1,0:T(8,128)(2,1)S(1)}, u32[]{:S(2)}, u32[]{:S(2)}) collective-permute-start(bf16[80,1280]{1,0:T(8,128)(2,1)S(1)} %collective-permute-done.21.refs_0_), channel_id=1, source_target_pairs={{0,4},{4,0},{1,5},{5,1},{2,6},{6,2},{3,7},{7,3},{8,12},{12,8},{9,1... | collective-permute-start | bytes 614408 | tf_op jit(solution)/shard_map/ppermute | solution.py:73
  64.7 8.7 %collective-permute-start.27 = (bf16[80,1280]{1,0:T(8,128)(2,1)S(1)}, bf16[80,1280]{1,0:T(8,128)(2,1)S(1)}, u32[]{:S(2)}, u32[]{:S(2)}) collective-permute-start(bf16[80,1280]{1,0:T(8,128)(2,1)S(1)} %collective-permute-done.23.refs_2_), channel_id=1, source_target_pairs={{0,4},{4,0},{1,5},{5,1},{2,6},{6,2},{3,7},{7,3},{8,12},{12,8},{9,1... | collective-permute-start | bytes 614408 | tf_op jit(solution)/shard_map/ppermute | solution.py:73
  65.4 24.4 %collective-permute-start.7 = (bf16[80,1280]{1,0:T(8,128)(2,1)S(1)}, bf16[80,1280]{1,0:T(8,128)(2,1)S(1)}, u32[]{:S(2)}, u32[]{:S(2)}) collective-permute-start(bf16[80,1280]{1,0:T(8,128)(2,1)S(1)} %get-tuple-element.36), channel_id=1, source_target_pairs={{0,3},{1,0},{2,1},{3,2},{4,7},{5,4},{6,5},{7,6},{8,11},{9,8},{10,9... | collective-permute-start | bytes 614408 | tf_op jit(solution)/shard_map/ppermute | solution.py:78
  70.3 19.6 %collective-permute-start.8 = (bf16[80,1280]{1,0:T(8,128)(2,1)S(1)}, bf16[80,1280]{1,0:T(8,128)(2,1)S(1)}, u32[]{:S(2)}, u32[]{:S(2)}) collective-permute-start(bf16[80,1280]{1,0:T(8,128)(2,1)S(1)} %get-tuple-element.37), channel_id=1, source_target_pairs={{0,2},{1,3},{2,0},{3,1},{4,6},{5,7},{6,4},{7,5},{8,10},{9,11},{10,... | collective-permute-start | bytes 614408 | tf_op jit(solution)/shard_map/ppermute | solution.py:78
  73.4 7.1 %copy-start.5 = (bf16[320,2560]{1,0:T(8,128)(2,1)S(1)}, bf16[320,2560]{1,0:T(8,128)(2,1)}, u32[]{:S(2)}) copy-start(bf16[320,2560]{1,0:T(8,128)(2,1)} %copy-done.4) | copy-start | bytes 4915204
  73.4 16.4 %collective-permute-start.9 = (bf16[80,1280]{1,0:T(8,128)(2,1)S(1)}, bf16[80,1280]{1,0:T(8,128)(2,1)S(1)}, u32[]{:S(2)}, u32[]{:S(2)}) collective-permute-start(bf16[80,1280]{1,0:T(8,128)(2,1)S(1)} %get-tuple-element.38), channel_id=1, source_target_pairs={{0,1},{1,2},{2,3},{3,0},{4,5},{5,6},{6,7},{7,4},{8,9},{9,10},{10,1... | collective-permute-start | bytes 614408 | tf_op jit(solution)/shard_map/ppermute | solution.py:78
  (3 other events, 9.3 us)

commit v3 on v2

v3 whole, which is shorter than its diff:
```python
import functools

import jax
import jax.numpy as jnp
from jax import lax
from jax.experimental import pallas as pl
from jax.experimental.pallas import tpu as pltpu
from jax.sharding import PartitionSpec as P

BF16 = jnp.bfloat16
F32 = jnp.float32
LAST = (((1,), (1,)), ((), ()))
FIRST = (((0,), (0,)), ((), ()))
MATMUL = (((1,), (0,)), ((), ()))


def dot(a, b, dims):
    return lax.dot_general(a, b, dims, preferred_element_type=F32)


def targets(expert_of, expert_count, capacity, first):
    routed = expert_of[:, 0]
    chosen = (routed[:, None] == jnp.arange(expert_count, dtype=jnp.int32)[None, :]).astype(
        jnp.int32
    )
    slot_index = jnp.sum(chosen * (jnp.cumsum(chosen, axis=0) - 1), axis=1)
    return lax.rem(routed - first + expert_count, expert_count) * capacity + slot_index


def placement(target, slots_all):
    return (jnp.arange(slots_all, dtype=jnp.int32)[:, None] == target[None, :]).astype(BF16)


def gradients(gate_act, up_act, cotan):
    sigma = jax.nn.sigmoid(gate_act)
    cotan = cotan.astype(F32)
    d_gate = (cotan * up_act * sigma * (1.0 + gate_act * (1.0 - sigma))).astype(BF16)
    d_up = (cotan * gate_act * sigma).astype(BF16)
    return sigma, d_gate, d_up


def reduce_plan(tokens, expert_of, w_gate, w_up, d_hidden):
    expert_count = lax.axis_size("exp")
    replica_count = lax.axis_size("rep")
    capacity = d_hidden.shape[3]
    feature_width = tokens.shape[1]
    slots_all = expert_count * capacity
    placing = placement(targets(expert_of, expert_count, capacity, 0), slots_all)
    packed = dot(placing, tokens, MATMUL).astype(BF16)
    arrived = lax.all_to_all(
        packed.reshape(expert_count, capacity, feature_width), "exp", 0, 0, tiled=True
    )
    rows = arrived.reshape(slots_all, feature_width)
    gate_act, up_act = dot(rows, w_gate[0], LAST), dot(rows, w_up[0], LAST)
    cotan = d_hidden.reshape(slots_all, w_gate.shape[1])
    sigma, d_gate, d_up = gradients(gate_act, up_act, cotan)
    hidden = (gate_act * sigma * up_act).astype(BF16)

    def reduced(d_act):
        total = lax.psum(dot(d_act, rows, FIRST).astype(BF16), "rep").astype(F32)
        return (total * (1.0 / replica_count)).astype(BF16)[None]

    term = dot(d_gate, w_gate[0], MATMUL) + dot(d_up, w_up[0], MATMUL)
    outgoing = term.astype(BF16).reshape(expert_count, capacity, feature_width)
    returned = lax.all_to_all(outgoing, "exp", 0, 0, tiled=True)
    unpacked = dot(placing, returned.reshape(slots_all, feature_width), FIRST)
    d_tokens = lax.psum_scatter(unpacked.astype(BF16), "shard", scatter_dimension=1, tiled=True)
    return hidden.reshape(d_hidden.shape), d_tokens, reduced(d_gate), reduced(d_up)


def across(x, axis, bit):
    size = lax.axis_size(axis)
    return lax.ppermute(x, axis, [(i, i ^ bit) for i in range(size)])


def turned(x, axis, step):
    size = lax.axis_size(axis)
    return lax.ppermute(x, axis, [(i, (i + step) % size) for i in range(size)])


VMEM = pl.BlockSpec(memory_space=pltpu.VMEM)
ANY = pl.BlockSpec(memory_space=pl.ANY)
HBM = pl.BlockSpec(memory_space=pltpu.HBM)


def call(kernel, ins, outs, args, scratch=(), name=None, limit=24, flops=1):
    return pl.pallas_call(
        kernel,
        in_specs=ins,
        out_specs=[VMEM] * len(outs),
        out_shape=outs,
        scratch_shapes=list(scratch),
        compiler_params=pltpu.CompilerParams(vmem_limit_bytes=limit << 20),
        cost_estimate=pl.CostEstimate(flops=flops, transcendentals=0, bytes_accessed=1),
        name=name,
    )(*args)


def like(*shape, dtype=BF16):
    return jax.ShapeDtypeStruct(shape, dtype)


def after(values, *earlier):
    held = lax.optimization_barrier((tuple(values), earlier))
    return list(held[0])


def place_rows(expert_ref, capacity):
    count, first = lax.axis_size("exp"), lax.axis_index("exp")
    tokens = expert_ref.shape[1]
    routed = jnp.broadcast_to(expert_ref[...], (tokens, tokens))
    rows = lax.broadcasted_iota(jnp.int32, (tokens, tokens), 0)
    columns = lax.broadcasted_iota(jnp.int32, (tokens, tokens), 1)
    chosen = routed == rows
    before = dot(chosen.astype(BF16), (rows < columns).astype(BF16), MATMUL)
    slot = jnp.sum(jnp.where(chosen, before, 0.0), axis=0, keepdims=True).astype(jnp.int32)
    turn = routed[:1] - first
    target = jnp.where(turn < 0, turn + count, turn) * capacity + slot
    slots = lax.broadcasted_iota(jnp.int32, (count * capacity, tokens), 0)
    return (slots == target).astype(BF16)


def side_of(core, half):
    return pl.ds(pl.multiple_of(core * half, 128), half)


def load_kernel(a_ref, b_ref, a_out, b_out, sem):
    copies = [
        pltpu.make_async_copy(a_ref, a_out, sem.at[0]),
        pltpu.make_async_copy(b_ref, b_out, sem.at[1]),
    ]
    for c in copies:
        c.start()
    for c in copies:
        c.wait()


def pack_kernel(capacity, expert_hbm, tokens_hbm, *refs):
    *outs, experts, mine, theirs, sem = refs
    count, core = lax.axis_size("exp"), lax.axis_index("shard")
    half = mine.shape[1]
    first = pltpu.make_async_copy(expert_hbm, experts, sem.at[0])
    second = pltpu.make_async_copy(tokens_hbm.at[:, side_of(core, half)], mine, sem.at[1])
    third = pltpu.make_async_copy(tokens_hbm.at[:, side_of(1 - core, half)], theirs, sem.at[2])
    first.start()
    second.start()
    third.start()
    first.wait()
    placing = place_rows(experts, capacity)
    second.wait()
    packed = dot(placing, mine[...], MATMUL).astype(BF16)
    for k in range(count):
        outs[k][...] = packed[k * capacity : (k + 1) * capacity]
    third.wait()
    outs[count][...] = dot(placing[:capacity], theirs[...], MATMUL).astype(BF16)


def unpack_kernel(capacity, expert_ref, *refs):
    *pieces, out = refs
    rows = jnp.concatenate([p[...] for p in pieces])
    out[...] = dot(place_rows(expert_ref, capacity), rows, FIRST).astype(BF16)


def sum_kernel(kept_ref, *refs):
    n = len(refs) // 2
    capacity = refs[0].shape[0]
    for k, (got, out) in enumerate(zip(refs[:n], refs[n:])):
        at = pl.ds(k * capacity, capacity)
        out[...] = (kept_ref[at].astype(F32) + got[...].astype(F32)).astype(BF16)


def fill(pieces, others, full, sem):
    core, half = lax.axis_index("shard"), full.shape[1] // 2
    copies, start = [], 0
    for piece, other in zip(pieces, others):
        at = pl.ds(start, piece.shape[0])
        for ref, side in ((piece, core), (other, 1 - core)):
            copies.append(pltpu.make_async_copy(ref, full.at[at, side_of(side, half)], sem.at[0]))
        start += piece.shape[0]
    for c in copies:
        c.start()
    for c in copies:
        c.wait()


def source_of(k):
    count = lax.axis_size("exp")
    return lax.rem(lax.axis_index("exp") - k + count, count)


def own_kernel(blocks, earlier, n, *refs):
    pieces, others = refs[:n], refs[n : 2 * n]
    cotan_ref, gate_ref, up_ref = refs[2 * n : 2 * n + 3]
    refs = refs[2 * n + 3 :]
    full, d_gate_ref, d_up_ref, kept_ref, *sent_refs = refs[len(refs) - 6 - len(blocks) : -2]
    hidden_ref, sem = refs[-2:]
    core, half = lax.axis_index("shard"), full.shape[1] // 2
    capacity = cotan_ref.shape[1]
    fill(pieces, others, full, sem)
    rows = full[...]
    gate_act, up_act = dot(rows, gate_ref[...], LAST), dot(rows, up_ref[...], LAST)
    for i, k in enumerate(blocks):
        at = slice(i * capacity, (i + 1) * capacity)
        gate, up = gate_act[at], up_act[at]
        sigma, d_gate, d_up = gradients(gate, up, cotan_ref[source_of(k)])
        hidden = (gate * sigma * up).astype(BF16)
        if len(blocks) + len(earlier) == lax.axis_size("exp"):
            hidden_ref[source_of(k)] = hidden
        else:
            hidden_ref[i] = hidden
        d_gate_ref[at] = d_gate
        d_up_ref[at] = d_up
    for i, k in enumerate(earlier):
        hidden_ref[source_of(k)] = refs[0][i]
    for side, outs in ((1 - core, sent_refs), (core, [kept_ref])):
        term = dot(d_gate_ref[...], gate_ref[:, side_of(side, half)], MATMUL)
        term += dot(d_up_ref[...], up_ref[:, side_of(side, half)], MATMUL)
        start = 0
        for out in outs:
            out[...] = term[start : start + out.shape[0]].astype(BF16)
            start += out.shape[0]


def part_kernel(plan, *refs):
    n = (len(refs) - 9) // 2
    pieces, others = refs[:n], refs[n : 2 * n]
    near, far, zero, gate_ref, up_ref, full, d_gate_ref, d_up_ref, sem = refs[2 * n :]
    fill(pieces, others, full, sem)
    rows = full[...]
    gate_act, up_act = dot(rows, gate_ref[...], LAST), dot(rows, up_ref[...], LAST)
    capacity = near.shape[1]
    for i, (k, group) in enumerate(plan):
        at = slice(i * capacity, (i + 1) * capacity)
        source = source_of(k)
        cotan = near[source] if group == 2 else far[0 if group == 1 else 1, source]
        _, d_gate, d_up = gradients(gate_act[at], up_act[at], cotan)
        d_gate_ref[at] = d_gate
        d_up_ref[at] = d_up


def grad_kernel(scale, n, *refs):
    fulls, gates, ups = refs[:n], refs[n : 2 * n], refs[2 * n : 3 * n]
    *earlier, gate_out, up_out = refs[3 * n :]
    for i, (parts, out) in enumerate(((gates, gate_out), (ups, up_out))):
        total = sum(dot(d[...], full[...], FIRST) for d, full in zip(parts, fulls))
        if earlier:
            total += earlier[i][...]
        out[...] = (total * scale).astype(out.dtype)


def swap(x):
    return across(x, "shard", 1)


def gather_plan(tokens, expert_of, w_gate, w_up, d_hidden):
    count = lax.axis_size("exp")
    capacity = d_hidden.shape[3]
    width = tokens.shape[1]
    half = width // 2
    hidden_width = w_gate.shape[1]
    gate_rows, up_rows, cotan = w_gate[0], w_up[0], d_hidden[0, 0]
    experts = expert_of.reshape(1, -1)
    sem = [pltpu.SemaphoreType.DMA((1,))]
    piece = like(capacity, half)

    def own(pair, rows, others, earlier, hidden):
        n = len(pair) * capacity
        return call(
            functools.partial(own_kernel, pair, earlier, len(rows)),
            [ANY] * (2 * len(rows)) + [VMEM] * (3 + len(hidden)),
            [like(n, width)]
            + [like(n, hidden_width)] * 2
            + [like(n, half)] + [piece] * len(pair)
            + [like(len(pair) + len(earlier), capacity, hidden_width)],
            [*rows, *others, cotan, gate_rows, up_rows, *hidden],
            scratch=sem,
            name="own",
        )

    def part(plan, pieces, near, far):
        n = sum(p.shape[0] for p in pieces)
        return call(
            functools.partial(part_kernel, plan),
            [ANY] * (2 * len(pieces)) + [VMEM] * 5,
            [like(n, width)] + [like(n, hidden_width)] * 2,
            [*pieces, *[swap(p) for p in pieces], near, far, near, gate_rows, up_rows],
            scratch=sem,
            name="part",
        )

    def add(kept, got):
        n = len(got)
        return call(sum_kernel, [VMEM] * (1 + n), [piece] * n, [kept, *got], name="sum")

    *blocks, other = call(
        functools.partial(pack_kernel, capacity),
        [HBM, HBM],
        [piece] * (count + 1),
        [pltpu.with_memory_space_constraint(x, pltpu.HBM) for x in (experts, tokens)],
        scratch=[
            pltpu.VMEM(experts.shape, jnp.int32),
            pltpu.VMEM((tokens.shape[0], half), BF16),
            pltpu.VMEM((tokens.shape[0], half), BF16),
            pltpu.SemaphoreType.DMA((3,)),
        ],
        name="pack",
    )
    c0 = blocks[0]
    z1, z2, z3 = (turned(blocks[k], "exp", k) for k in (1, 2, 3))
    (cotan_sent,) = after([cotan], c0)
    c0_near = across(c0, "rep", 1)
    cotan_near = across(cotan_sent, "rep", 2)
    gate_rows, up_rows = call(
        load_kernel,
        [HBM] * 2,
        [like(hidden_width, width)] * 2,
        after([pltpu.with_memory_space_constraint(x, pltpu.HBM) for x in (gate_rows, up_rows)], c0),
        scratch=[pltpu.SemaphoreType.DMA((2,))],
        name="load",
    )
    c0_kept, c0_near_kept = after([c0, c0_near], gate_rows, up_rows)
    c0_both = jnp.concatenate([c0_kept, c0_near_kept])
    cotan_both = jnp.stack([cotan, cotan_near])
    c0_far = across(c0_both, "rep", 2)
    cotan_far = across(cotan_both, "rep", 1)

    z1, z2, z3 = after([z1, z2, z3], c0_both, cotan_both)
    o1, o2, o3 = swap(z1), swap(z2), swap(z3)
    c123 = jnp.concatenate([z1, z2, z3])
    c123_x, c123_y, c123_d = (across(c123, "rep", bit) for bit in (1, 2, 3))
    o1, o2, o3 = after([o1, o2, o3], c0_far, cotan_far)
    full_a, d_gate_a, d_up_a, kept, *sent, hidden = own(
        (0, 1, 2, 3), [c0, z1, z2, z3], [other, o1, o2, o3], (), ()
    )
    r0, r1, r2, r3 = add(kept, [swap(s) for s in sent])
    r1, r2, r3 = turned(r1, "exp", -1), turned(r2, "exp", -2), turned(r3, "exp", -3)
    plan = ((0, 1), (0, 2), (0, 3))
    full_c, d_gate_c, d_up_c = part(plan, [c0_near, c0_far], cotan_near, cotan_far)
    wide = like(hidden_width, width, dtype=F32)
    total_gate, total_up = call(
        functools.partial(grad_kernel, 1.0, 2),
        [VMEM] * 6,
        [wide] * 2,
        [full_a, full_c, d_gate_a, d_gate_c, d_up_a, d_up_c],
        name="grads_near",
        limit=32,
    )
    r2, r3 = after([r2, r3], total_gate)
    (d_tokens,) = call(
        functools.partial(unpack_kernel, capacity),
        [VMEM] * (1 + count),
        [like(tokens.shape[0], half)],
        [experts, r0, r1, r2, r3],
        name="unpack",
    )
    c123_x, c123_y, c123_d = after([c123_x, c123_y, c123_d], d_tokens)
    plan = tuple((k, group) for group in (1, 2, 3) for k in (1, 2, 3))
    full_d, d_gate_d, d_up_d = part(plan, [c123_x, c123_y, c123_d], cotan_near, cotan_far)
    grad_gate, grad_up = call(
        functools.partial(grad_kernel, 1.0 / lax.axis_size("rep"), 1),
        [VMEM] * 5,
        [like(hidden_width, width)] * 2,
        [full_d, d_gate_d, d_up_d, total_gate, total_up],
        name="grads",
        limit=32,
    )
    return hidden.reshape(d_hidden.shape), d_tokens, grad_gate[None], grad_up[None]


def local(tokens, expert_of, w_gate, w_up, d_hidden):
    replica_count, shard_count = lax.axis_size("rep"), lax.axis_size("shard")
    slots_all = d_hidden.shape[2] * d_hidden.shape[3]
    hidden_width, feature_width = w_gate.shape[1:]
    gathered = slots_all * (feature_width // shard_count + hidden_width) * replica_count
    reduced = 4 * hidden_width * feature_width
    if replica_count == 4 and shard_count == 2 and lax.axis_size("exp") == 4 and gathered < reduced:
        return gather_plan(tokens, expert_of, w_gate, w_up, d_hidden)
    return reduce_plan(tokens, expert_of, w_gate, w_up, d_hidden)


def solution(mesh):
    in_specs = (
        P(("rep", "exp"), None),
        P(("rep", "exp"), None),
        P("exp", "shard", None),
        P("exp", "shard", None),
        P("rep", "exp", None, None, "shard"),
    )
    out_specs = (
        P("rep", "exp", None, None, "shard"),
        P(("rep", "exp"), "shard"),
        P("exp", "shard", None),
        P("exp", "shard", None),
    )
    return jax.shard_map(local, mesh=mesh, in_specs=in_specs, out_specs=out_specs, check_vma=False)
```

time: 92.7 us -> 77.2 us (0.83)
  starting transfers between devices: 37.3 us -> 15.8 us
  waiting for transfers between devices: 22.3 us -> 36.9 us
  Pallas kernels: 28.2 us -> 23.4 us
  local copies, waits for them, and re-layouts: 3.02 us -> 0.08 us
    ppermute x23 -> x19, starting transfers between devices: 27 us -> 10.6 us  [across(): return lax.ppermute(x, axis, [(i, i ^ bit) for i in range(size)])]
    ppermute x6, waiting for transfers between devices: 10.3 us -> 23.5 us  [turned(): return lax.ppermute(x, axis, [(i, (i + step) % size) for i in range(size)])]
    ppermute x6, starting transfers between devices: 10.4 us -> 5.2 us  [turned(): return lax.ppermute(x, axis, [(i, (i + step) % size) for i in range(size)])]
    pallas_call x7 -> x9, Pallas kernels: 28.2 us -> 23.4 us  [call(): pl.pallas_call(kernel, in_specs=ins, out_specs=[VMEM] * len(outs), out_sh...]
    unnamed x13 -> x7, local copies, waits for them, and re-layouts: 3.02 us -> 0.05 us
    ppermute x23 -> x19, waiting for transfers between devices: 12 us -> 13.4 us  [across(): return lax.ppermute(x, axis, [(i, i ^ bit) for i in range(size)])]
  transfers between devices with their start and end apart: 29 -> 25, of which waited for: 7 -> 13; matrix products, arithmetic and copies ran while one was open for 0% -> 0% of each run, Pallas kernels for 27% -> 17%
where the time goes in v3:
time: 77.2 us; the launch traced here: 77 us
  waiting for transfers between devices  36.9 us (48%)
  Pallas kernels  23.4 us (30%)
  starting transfers between devices  15.8 us (20%)
  between operations  0.78 us (1%)
    ppermute x6, waiting for transfers between devices, turned(): return lax.ppermute(x, axis, [(i, (i + step) % size) for i in range(size)])  23.5 us
    pallas_call x9, Pallas kernels, call(): pl.pallas_call(kernel, in_specs=ins, out_specs=[VMEM] * len(outs), out_sh...  23.4 us
    ppermute x19, waiting for transfers between devices, across(): return lax.ppermute(x, axis, [(i, i ^ bit) for i in range(size)])  13.4 us
    ppermute x19, starting transfers between devices, across(): return lax.ppermute(x, axis, [(i, i ^ bit) for i in range(size)])  10.6 us
    ppermute x6, starting transfers between devices, turned(): return lax.ppermute(x, axis, [(i, (i + step) % size) for i in range(size)])  5.2 us
  transfers between devices with their start and end apart: 25, of which 13 were waited for; matrix products, arithmetic and copies ran while one was open for 0% of the time, Pallas kernels for 17%

profile of v3, /device:TPU:9, one launch (start us, length us, event | category | flops | bytes accessed | tf_op | source)
XLA Modules:
  0.0 77.0 jit_solution(3103493171121837810)
XLA Ops:
  0.6 1.7 %pack.1 = (bf16[80,1280]{1,0:T(8,128)(2,1)S(1)}, bf16[80,1280]{1,0:T(8,128)(2,1)S(1)}, bf16[80,1280]{1,0:T(8,128)(2,1)S(1)}, bf16[80,1280]{1,0:T(8,128)(2,1)S(1)}, bf16[80,1280]{1,0:T(8,128)(2,1)S(1)}) custom-call(s32[1,128]{1,0:T(1,128)} %bitcast.13, bf16[128,2560]{1,0:T(8,128)(2,1)} %tokens_hbm.1), custom_call_target="tpu_custom_call" | custom-call | flops 1 | bytes 1 | tf_op jit(solution)/shard_map/pack/pallas_call | solution.py:87
  2.3 1.3 %collective-permute-start.3 = (bf16[80,1280]{1,0:T(8,128)(2,1)S(1)}, bf16[80,1280]{1,0:T(8,128)(2,1)S(1)}, u32[]{:S(2)}, u32[]{:S(2)}) collective-permute-start(bf16[80,1280]{1,0:T(8,128)(2,1)S(1)} %get-tuple-element.58.refs_0_), channel_id=1, source_target_pairs={{0,8},{8,0},{16,24},{24,16},{1,9},{9,1},{17,25},{25,17},{2,10},{10... | collective-permute-start | bytes 614408 | tf_op jit(solution)/shard_map/ppermute | solution.py:73
  3.6 1.2 %collective-permute-start.4 = (bf16[4,80,384]{2,1,0:T(8,128)(2,1)}, bf16[4,80,384]{2,1,0:T(8,128)(2,1)S(1)}, u32[]{:S(2)}, u32[]{:S(2)}) collective-permute-start(bf16[4,80,384]{2,1,0:T(8,128)(2,1)} %bitcast.10), channel_id=1, source_target_pairs={{0,16},{8,24},{16,0},{24,8},{1,17},{9,25},{17,1},{25,9},{2,18},{10... | collective-permute-start | bytes 737288 | tf_op jit(solution)/shard_map/ppermute | solution.py:73
  4.8 1.3 %collective-permute-start = (bf16[80,1280]{1,0:T(8,128)(2,1)S(1)}, bf16[80,1280]{1,0:T(8,128)(2,1)S(1)}, u32[]{:S(2)}, u32[]{:S(2)}) collective-permute-start(bf16[80,1280]{1,0:T(8,128)(2,1)S(1)} %get-tuple-element.51), channel_id=1, source_target_pairs={{0,1},{1,2},{2,3},{3,0},{4,5},{5,6},{6,7},{7,4},{8,9},{9,10},{10,1... | collective-permute-start | bytes 614408 | tf_op jit(solution)/shard_map/ppermute | solution.py:78
  6.1 1.0 %collective-permute-start.1 = (bf16[80,1280]{1,0:T(8,128)(2,1)S(1)}, bf16[80,1280]{1,0:T(8,128)(2,1)S(1)}, u32[]{:S(2)}, u32[]{:S(2)}) collective-permute-start(bf16[80,1280]{1,0:T(8,128)(2,1)S(1)} %get-tuple-element.52), channel_id=1, source_target_pairs={{0,2},{1,3},{2,0},{3,1},{4,6},{5,7},{6,4},{7,5},{8,10},{9,11},{10,... | collective-permute-start | bytes 614408 | tf_op jit(solution)/shard_map/ppermute | solution.py:78
  7.1 1.5 %collective-permute-start.2 = (bf16[80,1280]{1,0:T(8,128)(2,1)S(1)}, bf16[80,1280]{1,0:T(8,128)(2,1)S(1)}, u32[]{:S(2)}, u32[]{:S(2)}) collective-permute-start(bf16[80,1280]{1,0:T(8,128)(2,1)S(1)} %get-tuple-element.53), channel_id=1, source_target_pairs={{0,3},{1,0},{2,1},{3,2},{4,7},{5,4},{6,5},{7,6},{8,11},{9,8},{10,9... | collective-permute-start | bytes 614408 | tf_op jit(solution)/shard_map/ppermute | solution.py:78
  8.6 2.2 %load.1 = (bf16[384,2560]{1,0:T(8,128)(2,1)S(1)}, bf16[384,2560]{1,0:T(8,128)(2,1)S(1)}) custom-call(bf16[384,2560]{1,0:T(8,128)(2,1)} %bitcast.15, bf16[384,2560]{1,0:T(8,128)(2,1)} %bitcast.16), custom_call_target="tpu_custom_call" | custom-call | flops 1 | bytes 1 | tf_op jit(solution)/shard_map/load/pallas_call | solution.py:87
  11.2 0.7 collective-permute-start.8
  12.0 10.4 %collective-permute-done.1.refs_2_ = bf16[80,1280]{1,0:T(8,128)(2,1)S(1)} collective-permute-done((bf16[80,1280]{1,0:T(8,128)(2,1)S(1)}, bf16[80,1280]{1,0:T(8,128)(2,1)S(1)}, u32[]{:S(2)}, u32[]{:S(2)}) %collective-permute-start.1) | collective-permute-done | bytes 204832 | tf_op jit(solution)/shard_map/ppermute | solution.py:78
  22.4 3.4 %collective-permute-done.2.refs_3_ = bf16[80,1280]{1,0:T(8,128)(2,1)S(1)} collective-permute-done((bf16[80,1280]{1,0:T(8,128)(2,1)S(1)}, bf16[80,1280]{1,0:T(8,128)(2,1)S(1)}, u32[]{:S(2)}, u32[]{:S(2)}) %collective-permute-start.2) | collective-permute-done | bytes 204832 | tf_op jit(solution)/shard_map/ppermute | solution.py:78
  25.8 0.5 collective-permute-start.5
  26.3 0.5 collective-permute-start.7
  26.8 0.6 collective-permute-done.5.refs_5_
  28.1 4.3 %own.1 = (bf16[320,2560]{1,0:T(8,128)(2,1)S(1)}, bf16[320,384]{1,0:T(8,128)(2,1)S(1)}, bf16[320,384]{1,0:T(8,128)(2,1)S(1)}, bf16[320,1280]{1,0:T(8,128)(2,1)S(1...) custom-call(bf16[80,1280]{1,0:T(8,128)(2,1)S(1)} %get-tuple-element., ...), custom_call_target="tpu_custom_call" | custom-call | flops 1 | bytes 1 | tf_op jit(solution)/shard_map/own/pallas_call | solution.py:87
  32.4 0.4 collective-permute-start.10
  34.2 0.7 collective-permute-done.11.refs_1_
  35.2 1.1 %collective-permute-start.20 = (bf16[240,1280]{1,0:T(8,128)(2,1)S(1)}, bf16[240,1280]{1,0:T(8,128)(2,1)S(1)}, u32[]{:S(2)}, u32[]{:S(2)}) collective-permute-start(bf16[240,1280]{1,0:T(8,128)(2,1)S(1)} %constant_dynamic-update-slice_fusion.2), channel_id=1, source_target_pairs={{0,16},{8,24},{16,0},{24,8},{1,17},{9,25},{17,1},{25,9},{2,18},{10... | collective-permute-start | bytes 1843208 | tf_op jit(solution)/shard_map/ppermute | solution.py:73
  36.3 1.2 %collective-permute-start.19 = (bf16[240,1280]{1,0:T(8,128)(2,1)S(1)}, bf16[240,1280]{1,0:T(8,128)(2,1)S(1)}, u32[]{:S(2)}, u32[]{:S(2)}) collective-permute-start(bf16[240,1280]{1,0:T(8,128)(2,1)S(1)} %constant_dynamic-update-slice_fusion.2), channel_id=1, source_target_pairs={{0,8},{8,0},{16,24},{24,16},{1,9},{9,1},{17,25},{25,17},{2,10},{10... | collective-permute-start | bytes 1843208 | tf_op jit(solution)/shard_map/ppermute | solution.py:73
  37.8 1.4 %collective-permute-start.15 = (bf16[80,1280]{1,0:T(8,128)(2,1)S(1)}, bf16[80,1280]{1,0:T(8,128)(2,1)S(1)}, u32[]{:S(2)}, u32[]{:S(2)}) collective-permute-start(bf16[80,1280]{1,0:T(8,128)(2,1)S(1)} %get-tuple-element.76), channel_id=1, source_target_pairs={{0,2},{1,3},{2,0},{3,1},{4,6},{5,7},{6,4},{7,5},{8,10},{9,11},{10,... | collective-permute-start | bytes 614408 | tf_op jit(solution)/shard_map/ppermute | solution.py:78
  39.2 8.0 %collective-permute-done.15.refs_2_ = bf16[80,1280]{1,0:T(8,128)(2,1)S(1)} collective-permute-done((bf16[80,1280]{1,0:T(8,128)(2,1)S(1)}, bf16[80,1280]{1,0:T(8,128)(2,1)S(1)}, u32[]{:S(2)}, u32[]{:S(2)}) %collective-permute-start.15) | collective-permute-done | bytes 204832 | tf_op jit(solution)/shard_map/ppermute | solution.py:78
  47.2 1.6 %part.2 = (bf16[240,2560]{1,0:T(8,128)(2,1)S(1)}, bf16[240,384]{1,0:T(8,128)(2,1)S(1)}, bf16[240,384]{1,0:T(8,128)(2,1)S(1)}) custom-call(bf16[80,1280]{1,0:T(8,128)(2,1)S(1)} %collective-permute-done.3.refs_0_, bf16[160,1280]{1,0:T(8,128)(2,1)S(1)} %collective-permute-done.8.refs_1_, bf16[80,1280]{1,0:T(8,128)(2,1)S(1)} %collective-permute-done.17.refs_2_, ...), custom_call_target="tpu_custom_call" | custom-call | flops 1 | bytes 1 | tf_op jit(solution)/shard_map/part/pallas_call | solution.py:87
  48.9 3.2 %grads_near.1 = (f32[384,2560]{1,0:T(8,128)S(1)}, f32[384,2560]{1,0:T(8,128)S(1)}) custom-call(bf16[320,2560]{1,0:T(8,128)(2,1)S(1)} %get-tuple-element.78.refs_0_, bf16[240,2560]{1,0:T(8,128)(2,1)S(1)} %get-tuple-element.79.refs_1_, bf16[320,384]{1,0:T(8,128)(2,1)S(1)} %get-tuple-element.80.refs_2_, bf16[240,384]{1,0:T(8,128)(2,1)S(1)} %get-tuple-element.81.refs_3_, ...), custom_call_target="tpu_custom_call" | custom-call | flops 1 | bytes 1 | tf_op jit(solution)/shard_map/grads_near/pallas_call | solution.py:87
  52.1 1.6 %collective-permute-done.14.refs_1_ = bf16[80,1280]{1,0:T(8,128)(2,1)S(1)} collective-permute-done((bf16[80,1280]{1,0:T(8,128)(2,1)S(1)}, bf16[80,1280]{1,0:T(8,128)(2,1)S(1)}, u32[]{:S(2)}, u32[]{:S(2)}) %collective-permute-start.14) | collective-permute-done | bytes 204832 | tf_op jit(solution)/shard_map/ppermute | solution.py:78
  53.7 1.3 %unpack.1 = bf16[128,1280]{1,0:T(8,128)(2,1)} custom-call(s32[1,128]{1,0:T(1,128)S(1)} %bitcast.14, bf16[80,1280]{1,0:T(8,128)(2,1)S(1)} %get-tuple-element.74.refs_0_, bf16[80,1280]{1,0:T(8,128)(2,1)S(1)} %collective-permute-done.14.refs_1_, bf16[80,1280]{1,0:T(8,128)(2,1)S(1)} %collective-permute-done.15.refs_2_, ...), custom_call_target="tpu_custom_call" | custom-call | flops 1 | bytes 1 | tf_op jit(solution)/shard_map/unpack/pallas_call | solution.py:87
  55.0 8.6 %collective-permute-done.20.refs_1_ = bf16[240,1280]{1,0:T(8,128)(2,1)S(1)} collective-permute-done((bf16[240,1280]{1,0:T(8,128)(2,1)S(1)}, bf16[240,1280]{1,0:T(8,128)(2,1)S(1)}, u32[]{:S(2)}, u32[]{:S(2)}) %collective-permute-start.20) | collective-permute-done | bytes 614432 | tf_op jit(solution)/shard_map/ppermute | solution.py:73
  63.5 1.1 %collective-permute-start.22 = (bf16[240,1280]{1,0:T(8,128)(2,1)S(1)}, bf16[240,1280]{1,0:T(8,128)(2,1)S(1)}, u32[]{:S(2)}, u32[]{:S(2)}) collective-permute-start(bf16[240,1280]{1,0:T(8,128)(2,1)S(1)} %collective-permute-done.19.refs_0_), channel_id=1, source_target_pairs={{0,4},{4,0},{1,5},{5,1},{2,6},{6,2},{3,7},{7,3},{8,12},{12,8},{9,1... | collective-permute-start | bytes 1843208 | tf_op jit(solution)/shard_map/ppermute | solution.py:73
  64.6 0.5 collective-permute-start.24
  65.1 1.2 %collective-permute-done.22.refs_3_ = bf16[240,1280]{1,0:T(8,128)(2,1)S(1)} collective-permute-done((bf16[240,1280]{1,0:T(8,128)(2,1)S(1)}, bf16[240,1280]{1,0:T(8,128)(2,1)S(1)}, u32[]{:S(2)}, u32[]{:S(2)}) %collective-permute-start.22) | collective-permute-done | bytes 614432 | tf_op jit(solution)/shard_map/ppermute | solution.py:73
  66.3 0.9 %collective-permute-done.23.refs_4_ = bf16[240,1280]{1,0:T(8,128)(2,1)S(1)} collective-permute-done((bf16[240,1280]{1,0:T(8,128)(2,1)S(1)}, bf16[240,1280]{1,0:T(8,128)(2,1)S(1)}, u32[]{:S(2)}, u32[]{:S(2)}) %collective-permute-start.23) | collective-permute-done | bytes 614432 | tf_op jit(solution)/shard_map/ppermute | solution.py:73
  67.2 0.9 %collective-permute-done.24.refs_5_ = bf16[240,1280]{1,0:T(8,128)(2,1)S(1)} collective-permute-done((bf16[240,1280]{1,0:T(8,128)(2,1)S(1)}, bf16[240,1280]{1,0:T(8,128)(2,1)S(1)}, u32[]{:S(2)}, u32[]{:S(2)}) %collective-permute-start.24) | collective-permute-done | bytes 614432 | tf_op jit(solution)/shard_map/ppermute | solution.py:73
  68.1 4.4 %part.3 = (bf16[720,2560]{1,0:T(8,128)(2,1)S(1)}, bf16[720,384]{1,0:T(8,128)(2,1)S(1)}, bf16[720,384]{1,0:T(8,128)(2,1)S(1)}) custom-call(bf16[240,1280]{1,0:T(8,128)(2,1)S(1)} %collective-permute-done.19.refs_0_, bf16[240,1280]{1,0:T(8,128)(2,1)S(1)} %collective-permute-done.20.refs_1_, bf16[240,1280]{1,0:T(8,128)(2,1)S(1)} %collective-permute-done.21.refs_2_, ...), custom_call_target="tpu_custom_call" | custom-call | flops 1 | bytes 1 | tf_op jit(solution)/shard_map/part/pallas_call | solution.py:87
  72.4 4.6 %grads.1 = (bf16[384,2560]{1,0:T(8,128)(2,1)}, bf16[384,2560]{1,0:T(8,128)(2,1)}) custom-call(bf16[720,2560]{1,0:T(8,128)(2,1)S(1)} %get-tuple-element.90.refs_0_, bf16[720,384]{1,0:T(8,128)(2,1)S(1)} %get-tuple-element.91.refs_1_, bf16[720,384]{1,0:T(8,128)(2,1)S(1)} %get-tuple-element.92.refs_2_, f32[384,2560]{1,0:T(8,128)S(1)} %get-tuple-element.84.refs_3_, ...), custom_call_target="tpu_custom_call" | custom-call | flops 1 | bytes 1 | tf_op jit(solution)/shard_map/grads/pallas_call | solution.py:87
  (37 shorter events, 3.1 us)
Async XLA Ops:
  2.3 8.5 %collective-permute-start.3 = (bf16[80,1280]{1,0:T(8,128)(2,1)S(1)}, bf16[80,1280]{1,0:T(8,128)(2,1)S(1)}, u32[]{:S(2)}, u32[]{:S(2)}) collective-permute-start(bf16[80,1280]{1,0:T(8,128)(2,1)S(1)} %get-tuple-element.58.refs_0_), channel_id=1, source_target_pairs={{0,8},{8,0},{16,24},{24,16},{1,9},{9,1},{17,25},{25,17},{2,10},{10... | collective-permute-start | bytes 614408 | tf_op jit(solution)/shard_map/ppermute | solution.py:73
  3.6 7.3 %collective-permute-start.4 = (bf16[4,80,384]{2,1,0:T(8,128)(2,1)}, bf16[4,80,384]{2,1,0:T(8,128)(2,1)S(1)}, u32[]{:S(2)}, u32[]{:S(2)}) collective-permute-start(bf16[4,80,384]{2,1,0:T(8,128)(2,1)} %bitcast.10), channel_id=1, source_target_pairs={{0,16},{8,24},{16,0},{24,8},{1,17},{9,25},{17,1},{25,9},{2,18},{10... | collective-permute-start | bytes 737288 | tf_op jit(solution)/shard_map/ppermute | solution.py:73
  4.8 7.2 %collective-permute-start = (bf16[80,1280]{1,0:T(8,128)(2,1)S(1)}, bf16[80,1280]{1,0:T(8,128)(2,1)S(1)}, u32[]{:S(2)}, u32[]{:S(2)}) collective-permute-start(bf16[80,1280]{1,0:T(8,128)(2,1)S(1)} %get-tuple-element.51), channel_id=1, source_target_pairs={{0,1},{1,2},{2,3},{3,0},{4,5},{5,6},{6,7},{7,4},{8,9},{9,10},{10,1... | collective-permute-start | bytes 614408 | tf_op jit(solution)/shard_map/ppermute | solution.py:78
  6.1 16.3 %collective-permute-start.1 = (bf16[80,1280]{1,0:T(8,128)(2,1)S(1)}, bf16[80,1280]{1,0:T(8,128)(2,1)S(1)}, u32[]{:S(2)}, u32[]{:S(2)}) collective-permute-start(bf16[80,1280]{1,0:T(8,128)(2,1)S(1)} %get-tuple-element.52), channel_id=1, source_target_pairs={{0,2},{1,3},{2,0},{3,1},{4,6},{5,7},{6,4},{7,5},{8,10},{9,11},{10,... | collective-permute-start | bytes 614408 | tf_op jit(solution)/shard_map/ppermute | solution.py:78
  7.1 18.7 %collective-permute-start.2 = (bf16[80,1280]{1,0:T(8,128)(2,1)S(1)}, bf16[80,1280]{1,0:T(8,128)(2,1)S(1)}, u32[]{:S(2)}, u32[]{:S(2)}) collective-permute-start(bf16[80,1280]{1,0:T(8,128)(2,1)S(1)} %get-tuple-element.53), channel_id=1, source_target_pairs={{0,3},{1,0},{2,1},{3,2},{4,7},{5,4},{6,5},{7,6},{8,11},{9,8},{10,9... | collective-permute-start | bytes 614408 | tf_op jit(solution)/shard_map/ppermute | solution.py:78
  8.6 2.3 %copy-start = (bf16[1,1,4,80,384]{4,3,2,1,0:T(8,128)(2,1)S(1)}, bf16[1,1,4,80,384]{4,3,2,1,0:T(8,128)(2,1)}, u32[]{:S(2)}) copy-start(bf16[1,1,4,80,384]{4,3,2,1,0:T(8,128)(2,1)} %param.9) | copy-start | bytes 737284
  10.9 17.2 %collective-permute-start.9 = (bf16[2,4,80,384]{3,2,1,0:T(8,128)(2,1)S(1)}, bf16[2,4,80,384]{3,2,1,0:T(8,128)(2,1)S(1)}, u32[]{:S(2)}, u32[]{:S(2)}) collective-permute-start(bf16[2,4,80,384]{3,2,1,0:T(8,128)(2,1)S(1)} %pad_maximum_fusion), channel_id=1, source_target_pairs={{0,8},{8,0},{16,24},{24,16},{1,9},{9,1},{17,25},{25,17},{2,10},{10... | collective-permute-start | bytes 1474568 | tf_op jit(solution)/shard_map/ppermute | solution.py:73
  11.2 16.8 %collective-permute-start.8 = (bf16[160,1280]{1,0:T(8,128)(2,1)S(1)}, bf16[160,1280]{1,0:T(8,128)(2,1)S(1)}, u32[]{:S(2)}, u32[]{:S(2)}) collective-permute-start(bf16[160,1280]{1,0:T(8,128)(2,1)S(1)} %constant_dynamic-update-slice_fusion), channel_id=1, source_target_pairs={{0,16},{8,24},{16,0},{24,8},{1,17},{9,25},{17,1},{25,9},{2,18},{10... | collective-permute-start | bytes 1228808 | tf_op jit(solution)/shard_map/ppermute | solution.py:73
  25.8 1.6 %collective-permute-start.5 = (bf16[80,1280]{1,0:T(8,128)(2,1)S(1)}, bf16[80,1280]{1,0:T(8,128)(2,1)S(1)}, u32[]{:S(2)}, u32[]{:S(2)}) collective-permute-start(bf16[80,1280]{1,0:T(8,128)(2,1)S(1)} %collective-permute-done.refs_1_), channel_id=1, source_target_pairs={{0,4},{4,0},{1,5},{5,1},{2,6},{6,2},{3,7},{7,3},{8,12},{12,8},{9,1... | collective-permute-start | bytes 614408 | tf_op jit(solution)/shard_map/ppermute | solution.py:73
  26.3 1.5 %collective-permute-start.6 = (bf16[80,1280]{1,0:T(8,128)(2,1)S(1)}, bf16[80,1280]{1,0:T(8,128)(2,1)S(1)}, u32[]{:S(2)}, u32[]{:S(2)}) collective-permute-start(bf16[80,1280]{1,0:T(8,128)(2,1)S(1)} %collective-permute-done.1.refs_2_), channel_id=1, source_target_pairs={{0,4},{4,0},{1,5},{5,1},{2,6},{6,2},{3,7},{7,3},{8,12},{12,8},{9,1... | collective-permute-start | bytes 614408 | tf_op jit(solution)/shard_map/ppermute | solution.py:73
  26.3 1.7 %collective-permute-start.7 = (bf16[80,1280]{1,0:T(8,128)(2,1)S(1)}, bf16[80,1280]{1,0:T(8,128)(2,1)S(1)}, u32[]{:S(2)}, u32[]{:S(2)}) collective-permute-start(bf16[80,1280]{1,0:T(8,128)(2,1)S(1)} %collective-permute-done.2.refs_3_), channel_id=1, source_target_pairs={{0,4},{4,0},{1,5},{5,1},{2,6},{6,2},{3,7},{7,3},{8,12},{12,8},{9,1... | collective-permute-start | bytes 614408 | tf_op jit(solution)/shard_map/ppermute | solution.py:73
  27.4 10.4 %collective-permute-start.17 = (bf16[80,1280]{1,0:T(8,128)(2,1)S(1)}, bf16[80,1280]{1,0:T(8,128)(2,1)S(1)}, u32[]{:S(2)}, u32[]{:S(2)}) collective-permute-start(bf16[80,1280]{1,0:T(8,128)(2,1)S(1)} %collective-permute-done.3.refs_0_), channel_id=1, source_target_pairs={{0,4},{4,0},{1,5},{5,1},{2,6},{6,2},{3,7},{7,3},{8,12},{12,8},{9,1... | collective-permute-start | bytes 614408 | tf_op jit(solution)/shard_map/ppermute | solution.py:73
  32.4 1.5 %collective-permute-start.10 = (bf16[80,1280]{1,0:T(8,128)(2,1)S(1)}, bf16[80,1280]{1,0:T(8,128)(2,1)S(1)}, u32[]{:S(2)}, u32[]{:S(2)}) collective-permute-start(bf16[80,1280]{1,0:T(8,128)(2,1)S(1)} %get-tuple-element.70), channel_id=1, source_target_pairs={{0,4},{4,0},{1,5},{5,1},{2,6},{6,2},{3,7},{7,3},{8,12},{12,8},{9,1... | collective-permute-start | bytes 614408 | tf_op jit(solution)/shard_map/ppermute | solution.py:73
  32.8 6.4 %collective-permute-start.18 = (bf16[160,1280]{1,0:T(8,128)(2,1)S(1)}, bf16[160,1280]{1,0:T(8,128)(2,1)S(1)}, u32[]{:S(2)}, u32[]{:S(2)}) collective-permute-start(bf16[160,1280]{1,0:T(8,128)(2,1)S(1)} %collective-permute-done.8.refs_1_), channel_id=1, source_target_pairs={{0,4},{4,0},{1,5},{5,1},{2,6},{6,2},{3,7},{7,3},{8,12},{12,8},{9,1... | collective-permute-start | bytes 1228808 | tf_op jit(solution)/shard_map/ppermute | solution.py:73
  33.1 1.8 %collective-permute-start.11 = (bf16[80,1280]{1,0:T(8,128)(2,1)S(1)}, bf16[80,1280]{1,0:T(8,128)(2,1)S(1)}, u32[]{:S(2)}, u32[]{:S(2)}) collective-permute-start(bf16[80,1280]{1,0:T(8,128)(2,1)S(1)} %get-tuple-element.71), channel_id=1, source_target_pairs={{0,4},{4,0},{1,5},{5,1},{2,6},{6,2},{3,7},{7,3},{8,12},{12,8},{9,1... | collective-permute-start | bytes 614408 | tf_op jit(solution)/shard_map/ppermute | solution.py:73
  33.4 1.8 %collective-permute-start.12 = (bf16[80,1280]{1,0:T(8,128)(2,1)S(1)}, bf16[80,1280]{1,0:T(8,128)(2,1)S(1)}, u32[]{:S(2)}, u32[]{:S(2)}) collective-permute-start(bf16[80,1280]{1,0:T(8,128)(2,1)S(1)} %get-tuple-element.72), channel_id=1, source_target_pairs={{0,4},{4,0},{1,5},{5,1},{2,6},{6,2},{3,7},{7,3},{8,12},{12,8},{9,1... | collective-permute-start | bytes 614408 | tf_op jit(solution)/shard_map/ppermute | solution.py:73
  33.9 2.4 %collective-permute-start.13 = (bf16[80,1280]{1,0:T(8,128)(2,1)S(1)}, bf16[80,1280]{1,0:T(8,128)(2,1)S(1)}, u32[]{:S(2)}, u32[]{:S(2)}) collective-permute-start(bf16[80,1280]{1,0:T(8,128)(2,1)S(1)} %get-tuple-element.73), channel_id=1, source_target_pairs={{0,4},{4,0},{1,5},{5,1},{2,6},{6,2},{3,7},{7,3},{8,12},{12,8},{9,1... | collective-permute-start | bytes 614408 | tf_op jit(solution)/shard_map/ppermute | solution.py:73
  34.9 20.1 %collective-permute-start.21 = (bf16[240,1280]{1,0:T(8,128)(2,1)S(1)}, bf16[240,1280]{1,0:T(8,128)(2,1)S(1)}, u32[]{:S(2)}, u32[]{:S(2)}) collective-permute-start(bf16[240,1280]{1,0:T(8,128)(2,1)S(1)} %constant_dynamic-update-slice_fusion.2), channel_id=1, source_target_pairs={{0,24},{8,16},{16,8},{24,0},{1,25},{9,17},{17,9},{25,1},{2,26},{10... | collective-permute-start | bytes 1843208 | tf_op jit(solution)/shard_map/ppermute | solution.py:73
  35.2 28.4 %collective-permute-start.20 = (bf16[240,1280]{1,0:T(8,128)(2,1)S(1)}, bf16[240,1280]{1,0:T(8,128)(2,1)S(1)}, u32[]{:S(2)}, u32[]{:S(2)}) collective-permute-start(bf16[240,1280]{1,0:T(8,128)(2,1)S(1)} %constant_dynamic-update-slice_fusion.2), channel_id=1, source_target_pairs={{0,16},{8,24},{16,0},{24,8},{1,17},{9,25},{17,1},{25,9},{2,18},{10... | collective-permute-start | bytes 1843208 | tf_op jit(solution)/shard_map/ppermute | solution.py:73
  36.3 27.2 %collective-permute-start.19 = (bf16[240,1280]{1,0:T(8,128)(2,1)S(1)}, bf16[240,1280]{1,0:T(8,128)(2,1)S(1)}, u32[]{:S(2)}, u32[]{:S(2)}) collective-permute-start(bf16[240,1280]{1,0:T(8,128)(2,1)S(1)} %constant_dynamic-update-slice_fusion.2), channel_id=1, source_target_pairs={{0,8},{8,0},{16,24},{24,16},{1,9},{9,1},{17,25},{25,17},{2,10},{10... | collective-permute-start | bytes 1843208 | tf_op jit(solution)/shard_map/ppermute | solution.py:73
  37.8 9.5 %collective-permute-start.15 = (bf16[80,1280]{1,0:T(8,128)(2,1)S(1)}, bf16[80,1280]{1,0:T(8,128)(2,1)S(1)}, u32[]{:S(2)}, u32[]{:S(2)}) collective-permute-start(bf16[80,1280]{1,0:T(8,128)(2,1)S(1)} %get-tuple-element.76), channel_id=1, source_target_pairs={{0,2},{1,3},{2,0},{3,1},{4,6},{5,7},{6,4},{7,5},{8,10},{9,11},{10,... | collective-permute-start | bytes 614408 | tf_op jit(solution)/shard_map/ppermute | solution.py:78
  39.2 12.9 %collective-permute-start.16 = (bf16[80,1280]{1,0:T(8,128)(2,1)S(1)}, bf16[80,1280]{1,0:T(8,128)(2,1)S(1)}, u32[]{:S(2)}, u32[]{:S(2)}) collective-permute-start(bf16[80,1280]{1,0:T(8,128)(2,1)S(1)} %get-tuple-element.77), channel_id=1, source_target_pairs={{0,1},{1,2},{2,3},{3,0},{4,5},{5,6},{6,7},{7,4},{8,9},{9,10},{10,1... | collective-permute-start | bytes 614408 | tf_op jit(solution)/shard_map/ppermute | solution.py:78
  47.2 6.5 %collective-permute-start.14 = (bf16[80,1280]{1,0:T(8,128)(2,1)S(1)}, bf16[80,1280]{1,0:T(8,128)(2,1)S(1)}, u32[]{:S(2)}, u32[]{:S(2)}) collective-permute-start(bf16[80,1280]{1,0:T(8,128)(2,1)S(1)} %get-tuple-element.75), channel_id=1, source_target_pairs={{0,3},{1,0},{2,1},{3,2},{4,7},{5,4},{6,5},{7,6},{8,11},{9,8},{10,9... | collective-permute-start | bytes 614408 | tf_op jit(solution)/shard_map/ppermute | solution.py:78
  48.8 4.9 %copy-start.1 = (s32[128,1]{0,1:T(1,128)S(1)}, s32[128,1]{0,1:T(1,128)}, u32[]{:S(2)}) copy-start(s32[128,1]{0,1:T(1,128)} %param.6) | copy-start | bytes 1540
  63.5 2.7 %collective-permute-start.22 = (bf16[240,1280]{1,0:T(8,128)(2,1)S(1)}, bf16[240,1280]{1,0:T(8,128)(2,1)S(1)}, u32[]{:S(2)}, u32[]{:S(2)}) collective-permute-start(bf16[240,1280]{1,0:T(8,128)(2,1)S(1)} %collective-permute-done.19.refs_0_), channel_id=1, source_target_pairs={{0,4},{4,0},{1,5},{5,1},{2,6},{6,2},{3,7},{7,3},{8,12},{12,8},{9,1... | collective-permute-start | bytes 1843208 | tf_op jit(solution)/shard_map/ppermute | solution.py:73
  64.6 2.5 %collective-permute-start.23 = (bf16[240,1280]{1,0:T(8,128)(2,1)S(1)}, bf16[240,1280]{1,0:T(8,128)(2,1)S(1)}, u32[]{:S(2)}, u32[]{:S(2)}) collective-permute-start(bf16[240,1280]{1,0:T(8,128)(2,1)S(1)} %collective-permute-done.20.refs_1_), channel_id=1, source_target_pairs={{0,4},{4,0},{1,5},{5,1},{2,6},{6,2},{3,7},{7,3},{8,12},{12,8},{9,1... | collective-permute-start | bytes 1843208 | tf_op jit(solution)/shard_map/ppermute | solution.py:73
  64.6 3.4 %collective-permute-start.24 = (bf16[240,1280]{1,0:T(8,128)(2,1)S(1)}, bf16[240,1280]{1,0:T(8,128)(2,1)S(1)}, u32[]{:S(2)}, u32[]{:S(2)}) collective-permute-start(bf16[240,1280]{1,0:T(8,128)(2,1)S(1)} %collective-permute-done.21.refs_2_), channel_id=1, source_target_pairs={{0,4},{4,0},{1,5},{5,1},{2,6},{6,2},{3,7},{7,3},{8,12},{12,8},{9,1... | collective-permute-start | bytes 1843208 | tf_op jit(solution)/shard_map/ppermute | solution.py:73

commit v4 on v3

--- a/solution.py
+++ b/solution.py
@@ -83,11 +83,11 @@
 HBM = pl.BlockSpec(memory_space=pltpu.HBM)
 
 
-def call(kernel, ins, outs, args, scratch=(), name=None, limit=24, flops=1):
+def call(kernel, ins, outs, args, scratch=(), name=None, limit=24, flops=1, out_spec=VMEM):
     return pl.pallas_call(
         kernel,
         in_specs=ins,
-        out_specs=[VMEM] * len(outs),
+        out_specs=[out_spec] * len(outs),
         out_shape=outs,
         scratch_shapes=list(scratch),
         compiler_params=pltpu.CompilerParams(vmem_limit_bytes=limit << 20),
@@ -124,10 +124,11 @@
     return pl.ds(pl.multiple_of(core * half, 128), half)
 
 
-def load_kernel(a_ref, b_ref, a_out, b_out, sem):
+def load_kernel(gate_ref, up_ref, out, sem):
+    units = gate_ref.shape[0]
     copies = [
-        pltpu.make_async_copy(a_ref, a_out, sem.at[0]),
-        pltpu.make_async_copy(b_ref, b_out, sem.at[1]),
+        pltpu.make_async_copy(gate_ref, out.at[:units], sem.at[0]),
+        pltpu.make_async_copy(up_ref, out.at[units:], sem.at[1]),
     ]
     for c in copies:
         c.start()
@@ -162,11 +163,11 @@
 
 
 def sum_kernel(kept_ref, *refs):
-    n = len(refs) // 2
-    capacity = refs[0].shape[0]
-    for k, (got, out) in enumerate(zip(refs[:n], refs[n:])):
+    got_ref, *outs = refs
+    capacity = outs[0].shape[0]
+    for k, out in enumerate(outs):
         at = pl.ds(k * capacity, capacity)
-        out[...] = (kept_ref[at].astype(F32) + got[...].astype(F32)).astype(BF16)
+        out[...] = (kept_ref[at].astype(F32) + got_ref[at].astype(F32)).astype(BF16)
 
 
 def fill(pieces, others, full, sem):
@@ -188,64 +189,64 @@
     return lax.rem(lax.axis_index("exp") - k + count, count)
 
 
-def own_kernel(blocks, earlier, n, *refs):
+def own_kernel(blocks, *refs):
+    n = len(blocks)
     pieces, others = refs[:n], refs[n : 2 * n]
-    cotan_ref, gate_ref, up_ref = refs[2 * n : 2 * n + 3]
-    refs = refs[2 * n + 3 :]
-    full, d_gate_ref, d_up_ref, kept_ref, *sent_refs = refs[len(refs) - 6 - len(blocks) : -2]
-    hidden_ref, sem = refs[-2:]
+    cotan_ref, rows_ref, full, d_ref, kept_ref, sent_ref, hidden_ref, sem = refs[2 * n :]
     core, half = lax.axis_index("shard"), full.shape[1] // 2
-    capacity = cotan_ref.shape[1]
+    capacity, units = cotan_ref.shape[1:]
     fill(pieces, others, full, sem)
-    rows = full[...]
-    gate_act, up_act = dot(rows, gate_ref[...], LAST), dot(rows, up_ref[...], LAST)
+    acts = dot(full[...], rows_ref[...], LAST)
     for i, k in enumerate(blocks):
         at = slice(i * capacity, (i + 1) * capacity)
-        gate, up = gate_act[at], up_act[at]
+        gate, up = acts[at, :units], acts[at, units:]
         sigma, d_gate, d_up = gradients(gate, up, cotan_ref[source_of(k)])
-        hidden = (gate * sigma * up).astype(BF16)
-        if len(blocks) + len(earlier) == lax.axis_size("exp"):
-            hidden_ref[source_of(k)] = hidden
-        else:
-            hidden_ref[i] = hidden
-        d_gate_ref[at] = d_gate
-        d_up_ref[at] = d_up
-    for i, k in enumerate(earlier):
-        hidden_ref[source_of(k)] = refs[0][i]
-    for side, outs in ((1 - core, sent_refs), (core, [kept_ref])):
-        term = dot(d_gate_ref[...], gate_ref[:, side_of(side, half)], MATMUL)
-        term += dot(d_up_ref[...], up_ref[:, side_of(side, half)], MATMUL)
-        start = 0
-        for out in outs:
-            out[...] = term[start : start + out.shape[0]].astype(BF16)
-            start += out.shape[0]
-
-
-def part_kernel(plan, *refs):
-    n = (len(refs) - 9) // 2
+        hidden_ref[source_of(k)] = (gate * sigma * up).astype(BF16)
+        d_ref[at, :units] = d_gate
+        d_ref[at, units:] = d_up
+    for side, out in ((1 - core, sent_ref), (core, kept_ref)):
+        out[...] = dot(d_ref[...], rows_ref[:, side_of(side, half)], MATMUL).astype(BF16)
+
+
+def part_kernel(plan, n, *refs):
     pieces, others = refs[:n], refs[n : 2 * n]
-    near, far, zero, gate_ref, up_ref, full, d_gate_ref, d_up_ref, sem = refs[2 * n :]
+    near, far, rows_ref, full, d_ref, sem = refs[2 * n :]
+    capacity, units = near.shape[1:]
     fill(pieces, others, full, sem)
-    rows = full[...]
-    gate_act, up_act = dot(rows, gate_ref[...], LAST), dot(rows, up_ref[...], LAST)
-    capacity = near.shape[1]
+    acts = dot(full[...], rows_ref[...], LAST)
     for i, (k, group) in enumerate(plan):
         at = slice(i * capacity, (i + 1) * capacity)
         source = source_of(k)
         cotan = near[source] if group == 2 else far[0 if group == 1 else 1, source]
-        _, d_gate, d_up = gradients(gate_act[at], up_act[at], cotan)
-        d_gate_ref[at] = d_gate
-        d_up_ref[at] = d_up
-
-
-def grad_kernel(scale, n, *refs):
-    fulls, gates, ups = refs[:n], refs[n : 2 * n], refs[2 * n : 3 * n]
-    *earlier, gate_out, up_out = refs[3 * n :]
-    for i, (parts, out) in enumerate(((gates, gate_out), (ups, up_out))):
-        total = sum(dot(d[...], full[...], FIRST) for d, full in zip(parts, fulls))
-        if earlier:
-            total += earlier[i][...]
-        out[...] = (total * scale).astype(out.dtype)
+        _, d_gate, d_up = gradients(acts[at, :units], acts[at, units:], cotan)
+        d_ref[at, :units] = d_gate
+        d_ref[at, units:] = d_up
+
+
+def grad_kernel(n, *refs):
+    fulls, ds, out = refs[:n], refs[n : 2 * n], refs[2 * n]
+    out[...] = sum(dot(d[...], full[...], FIRST) for d, full in zip(ds, fulls))
+
+
+def last_grad_kernel(scale, n, *refs):
+    fulls, ds = refs[:n], refs[n : 2 * n]
+    earlier, gate_out, up_out, staged, sem = refs[2 * n :]
+    units, quarter, copies = gate_out.shape[0], staged.shape[1] // 4, []
+    for i in range(4):
+        columns = slice(i * quarter, (i + 1) * quarter)
+        total = sum(dot(d[...], full[:, columns], FIRST) for d, full in zip(ds, fulls))
+        staged[:, columns] = ((total + earlier[:, columns]) * scale).astype(BF16)
+        for j, out in enumerate((gate_out, up_out)):
+            copies.append(
+                pltpu.make_async_copy(
+                    staged.at[j * units : (j + 1) * units, columns],
+                    out.at[:, columns],
+                    sem.at[i, j],
+                )
+            )
+            copies[-1].start()
+    for c in copies:
+        c.wait()
 
 
 def swap(x):
@@ -263,34 +264,32 @@
     sem = [pltpu.SemaphoreType.DMA((1,))]
     piece = like(capacity, half)
 
-    def own(pair, rows, others, earlier, hidden):
+    def own(pair, rows, others):
         n = len(pair) * capacity
         return call(
-            functools.partial(own_kernel, pair, earlier, len(rows)),
-            [ANY] * (2 * len(rows)) + [VMEM] * (3 + len(hidden)),
-            [like(n, width)]
-            + [like(n, hidden_width)] * 2
-            + [like(n, half)] + [piece] * len(pair)
-            + [like(len(pair) + len(earlier), capacity, hidden_width)],
-            [*rows, *others, cotan, gate_rows, up_rows, *hidden],
+            functools.partial(own_kernel, pair),
+            [ANY] * (2 * len(rows)) + [VMEM] * 2,
+            [like(n, width), like(n, 2 * hidden_width)]
+            + [like(n, half)] * 2
+            + [like(len(pair), capacity, hidden_width)],
+            [*rows, *others, cotan, both_rows],
             scratch=sem,
             name="own",
         )
 
-    def part(plan, pieces, near, far):
+    def part(plan, pieces, others, near, far):
         n = sum(p.shape[0] for p in pieces)
         return call(
-            functools.partial(part_kernel, plan),
-            [ANY] * (2 * len(pieces)) + [VMEM] * 5,
-            [like(n, width)] + [like(n, hidden_width)] * 2,
-            [*pieces, *[swap(p) for p in pieces], near, far, near, gate_rows, up_rows],
+            functools.partial(part_kernel, plan, len(pieces)),
+            [ANY] * (2 * len(pieces)) + [VMEM] * 3,
+            [like(n, width), like(n, 2 * hidden_width)],
+            [*pieces, *others, near, far, both_rows],
             scratch=sem,
             name="part",
         )
 
     def add(kept, got):
-        n = len(got)
-        return call(sum_kernel, [VMEM] * (1 + n), [piece] * n, [kept, *got], name="sum")
+        return call(sum_kernel, [VMEM] * 2, [piece] * count, [kept, got], name="sum")
 
     *blocks, other = call(
         functools.partial(pack_kernel, capacity),
@@ -310,15 +309,15 @@
     (cotan_sent,) = after([cotan], c0)
     c0_near = across(c0, "rep", 1)
     cotan_near = across(cotan_sent, "rep", 2)
-    gate_rows, up_rows = call(
+    (both_rows,) = call(
         load_kernel,
         [HBM] * 2,
-        [like(hidden_width, width)] * 2,
+        [like(2 * hidden_width, width)],
         after([pltpu.with_memory_space_constraint(x, pltpu.HBM) for x in (gate_rows, up_rows)], c0),
         scratch=[pltpu.SemaphoreType.DMA((2,))],
         name="load",
     )
-    c0_kept, c0_near_kept = after([c0, c0_near], gate_rows, up_rows)
+    c0_kept, c0_near_kept = after([c0, c0_near], both_rows)
     c0_both = jnp.concatenate([c0_kept, c0_near_kept])
     cotan_both = jnp.stack([cotan, cotan_near])
     c0_far = across(c0_both, "rep", 2)
@@ -327,42 +326,55 @@
     z1, z2, z3 = after([z1, z2, z3], c0_both, cotan_both)
     o1, o2, o3 = swap(z1), swap(z2), swap(z3)
     c123 = jnp.concatenate([z1, z2, z3])
-    c123_x, c123_y, c123_d = (across(c123, "rep", bit) for bit in (1, 2, 3))
     o1, o2, o3 = after([o1, o2, o3], c0_far, cotan_far)
-    full_a, d_gate_a, d_up_a, kept, *sent, hidden = own(
-        (0, 1, 2, 3), [c0, z1, z2, z3], [other, o1, o2, o3], (), ()
-    )
-    r0, r1, r2, r3 = add(kept, [swap(s) for s in sent])
+    full_a, d_a, kept, sent, hidden = own((0, 1, 2, 3), [c0, z1, z2, z3], [other, o1, o2, o3])
+    c123_sent, c0_near_sent, c0_far_sent = after([c123, c0_near, c0_far], kept)
+    c123_x, c123_y = across(c123_sent, "rep", 1), across(c123_sent, "rep", 2)
+    c0_others = [swap(c0_near_sent), swap(c0_far_sent)]
+    r0, r1, r2, r3 = add(kept, swap(sent))
+    r1, r2, r3 = after([r1, r2, r3], *c0_others)
     r1, r2, r3 = turned(r1, "exp", -1), turned(r2, "exp", -2), turned(r3, "exp", -3)
+
     plan = ((0, 1), (0, 2), (0, 3))
-    full_c, d_gate_c, d_up_c = part(plan, [c0_near, c0_far], cotan_near, cotan_far)
-    wide = like(hidden_width, width, dtype=F32)
-    total_gate, total_up = call(
-        functools.partial(grad_kernel, 1.0, 2),
-        [VMEM] * 6,
-        [wide] * 2,
-        [full_a, full_c, d_gate_a, d_gate_c, d_up_a, d_up_c],
+    full_c, d_c = part(plan, [c0_near, c0_far], c0_others, cotan_near, cotan_far)
+    (total,) = call(
+        functools.partial(grad_kernel, 2),
+        [VMEM] * 4,
+        [like(2 * hidden_width, width, dtype=F32)],
+        [full_a, full_c, d_a, d_c],
         name="grads_near",
         limit=32,
     )
-    r2, r3 = after([r2, r3], total_gate)
+    c123_x, c123_y = after([c123_x, c123_y], total)
+    cut = (c123.shape[0] // 2 + 15) // 16 * 16
+    far_sent = [across(c123_x[:cut], "rep", 2), across(c123_y[cut:], "rep", 1)]
     (d_tokens,) = call(
         functools.partial(unpack_kernel, capacity),
         [VMEM] * (1 + count),
         [like(tokens.shape[0], half)],
         [experts, r0, r1, r2, r3],
         name="unpack",
-    )
-    c123_x, c123_y, c123_d = after([c123_x, c123_y, c123_d], d_tokens)
-    plan = tuple((k, group) for group in (1, 2, 3) for k in (1, 2, 3))
-    full_d, d_gate_d, d_up_d = part(plan, [c123_x, c123_y, c123_d], cotan_near, cotan_far)
+        flops=6*10**9,
+    )
+    (c123_x,), (c123_y,) = after([c123_x], r1), after([c123_y], r2)
+    far_sent = after(far_sent, d_tokens)
+    plan = tuple((k, group) for group in (1, 2) for k in (1, 2, 3))
+    full_d, d_d = part(
+        plan, [c123_x, c123_y], [swap(c123_x), swap(c123_y)], cotan_near, cotan_far
+    )
+    plan = tuple((k, 3) for k in (1, 2, 3))
+    full_e, d_e = part(
+        plan, far_sent, after([swap(f) for f in far_sent], d_d), cotan_near, cotan_far
+    )
     grad_gate, grad_up = call(
-        functools.partial(grad_kernel, 1.0 / lax.axis_size("rep"), 1),
+        functools.partial(last_grad_kernel, 1.0 / lax.axis_size("rep"), 2),
         [VMEM] * 5,
         [like(hidden_width, width)] * 2,
-        [full_d, d_gate_d, d_up_d, total_gate, total_up],
+        [full_d, full_e, d_d, d_e, total],
+        scratch=[pltpu.VMEM((2 * hidden_width, width), BF16), pltpu.SemaphoreType.DMA((4, 2))],
         name="grads",
         limit=32,
+        out_spec=HBM,
     )
     return hidden.reshape(d_hidden.shape), d_tokens, grad_gate[None], grad_up[None]
 

time: 77.2 us -> 70.1 us (0.908)
  the two profiles are of different devices: /device:TPU:9 before, /device:TPU:0 now
where the time goes in v4:
time: 70.1 us; the launch traced here: 70 us
  waiting for transfers between devices  23.1 us (33%)
  Pallas kernels  22.8 us (33%)
  starting transfers between devices  22.8 us (33%)
  between operations  0.96 us (1%)
    pallas_call x10, Pallas kernels, call(): pl.pallas_call(kernel, in_specs=ins, out_specs=[out_spec] * len(outs), ou...  22.8 us
    ppermute x6, waiting for transfers between devices, turned(): return lax.ppermute(x, axis, [(i, (i + step) % size) for i in range(size)])  16.7 us
    ppermute x6, starting transfers between devices, turned(): return lax.ppermute(x, axis, [(i, (i + step) % size) for i in range(size)])  11.8 us
    ppermute x18, starting transfers between devices, across(): return lax.ppermute(x, axis, [(i, i ^ bit) for i in range(size)])  11 us
    ppermute x18, waiting for transfers between devices, across(): return lax.ppermute(x, axis, [(i, i ^ bit) for i in range(size)])  6.43 us
  transfers between devices with their start and end apart: 24, of which 12 were waited for; matrix products, arithmetic and copies ran while one was open for 0% of the time, Pallas kernels for 15%

profile of v4, /device:TPU:0, one launch (start us, length us, event | category | flops | bytes accessed | tf_op | source)
XLA Modules:
  0.0 70.0 jit_solution(8832406320239092708)
XLA Ops:
  0.6 1.7 %pack.1 = (bf16[80,1280]{1,0:T(8,128)(2,1)S(1)}, bf16[80,1280]{1,0:T(8,128)(2,1)S(1)}, bf16[80,1280]{1,0:T(8,128)(2,1)S(1)}, bf16[80,1280]{1,0:T(8,128)(2,1)S(1)}, bf16[80,1280]{1,0:T(8,128)(2,1)S(1)}) custom-call(s32[1,128]{1,0:T(1,128)} %bitcast.13, bf16[128,2560]{1,0:T(8,128)(2,1)} %tokens_hbm.1), custom_call_target="tpu_custom_call" | custom-call | flops 1 | bytes 1 | tf_op jit(solution)/shard_map/pack/pallas_call | solution.py:87
  2.3 3.0 %collective-permute-start.3 = (bf16[80,1280]{1,0:T(8,128)(2,1)S(1)}, bf16[80,1280]{1,0:T(8,128)(2,1)S(1)}, u32[]{:S(2)}, u32[]{:S(2)}) collective-permute-start(bf16[80,1280]{1,0:T(8,128)(2,1)S(1)} %get-tuple-element.57.refs_0_), channel_id=1, source_target_pairs={{0,8},{8,0},{16,24},{24,16},{1,9},{9,1},{17,25},{25,17},{2,10},{10... | collective-permute-start | bytes 614408 | tf_op jit(solution)/shard_map/ppermute | solution.py:73
  5.3 1.5 %collective-permute-start.4 = (bf16[4,80,384]{2,1,0:T(8,128)(2,1)}, bf16[4,80,384]{2,1,0:T(8,128)(2,1)S(1)}, u32[]{:S(2)}, u32[]{:S(2)}) collective-permute-start(bf16[4,80,384]{2,1,0:T(8,128)(2,1)} %bitcast.10), channel_id=1, source_target_pairs={{0,16},{8,24},{16,0},{24,8},{1,17},{9,25},{17,1},{25,9},{2,18},{10... | collective-permute-start | bytes 737288 | tf_op jit(solution)/shard_map/ppermute | solution.py:73
  6.8 1.6 %collective-permute-start = (bf16[80,1280]{1,0:T(8,128)(2,1)S(1)}, bf16[80,1280]{1,0:T(8,128)(2,1)S(1)}, u32[]{:S(2)}, u32[]{:S(2)}) collective-permute-start(bf16[80,1280]{1,0:T(8,128)(2,1)S(1)} %get-tuple-element.52), channel_id=1, source_target_pairs={{0,1},{1,2},{2,3},{3,0},{4,5},{5,6},{6,7},{7,4},{8,9},{9,10},{10,1... | collective-permute-start | bytes 614408 | tf_op jit(solution)/shard_map/ppermute | solution.py:78
  8.4 2.6 %collective-permute-start.1 = (bf16[80,1280]{1,0:T(8,128)(2,1)S(1)}, bf16[80,1280]{1,0:T(8,128)(2,1)S(1)}, u32[]{:S(2)}, u32[]{:S(2)}) collective-permute-start(bf16[80,1280]{1,0:T(8,128)(2,1)S(1)} %get-tuple-element.53), channel_id=1, source_target_pairs={{0,2},{1,3},{2,0},{3,1},{4,6},{5,7},{6,4},{7,5},{8,10},{9,11},{10,... | collective-permute-start | bytes 614408 | tf_op jit(solution)/shard_map/ppermute | solution.py:78
  11.0 1.3 %collective-permute-start.2 = (bf16[80,1280]{1,0:T(8,128)(2,1)S(1)}, bf16[80,1280]{1,0:T(8,128)(2,1)S(1)}, u32[]{:S(2)}, u32[]{:S(2)}) collective-permute-start(bf16[80,1280]{1,0:T(8,128)(2,1)S(1)} %get-tuple-element.54), channel_id=1, source_target_pairs={{0,3},{1,0},{2,1},{3,2},{4,7},{5,4},{6,5},{7,6},{8,11},{9,8},{10,9... | collective-permute-start | bytes 614408 | tf_op jit(solution)/shard_map/ppermute | solution.py:78
  12.3 2.2 %load.1.refs_9_.refs_6_ = bf16[768,2560]{1,0:T(8,128)(2,1)S(1)} custom-call(bf16[384,2560]{1,0:T(8,128)(2,1)} %bitcast.15, bf16[384,2560]{1,0:T(8,128)(2,1)} %bitcast.16), custom_call_target="tpu_custom_call" | custom-call | flops 1 | bytes 1 | tf_op jit(solution)/shard_map/load/pallas_call | solution.py:87
  14.7 0.6 collective-permute-start.9
  15.3 0.6 collective-permute-start.8
  15.8 0.9 %collective-permute-done.refs_1_ = bf16[80,1280]{1,0:T(8,128)(2,1)S(1)} collective-permute-done((bf16[80,1280]{1,0:T(8,128)(2,1)S(1)}, bf16[80,1280]{1,0:T(8,128)(2,1)S(1)}, u32[]{:S(2)}, u32[]{:S(2)}) %collective-permute-start) | collective-permute-done | bytes 204832 | tf_op jit(solution)/shard_map/ppermute | solution.py:78
  16.7 7.1 %collective-permute-done.1.refs_2_ = bf16[80,1280]{1,0:T(8,128)(2,1)S(1)} collective-permute-done((bf16[80,1280]{1,0:T(8,128)(2,1)S(1)}, bf16[80,1280]{1,0:T(8,128)(2,1)S(1)}, u32[]{:S(2)}, u32[]{:S(2)}) %collective-permute-start.1) | collective-permute-done | bytes 204832 | tf_op jit(solution)/shard_map/ppermute | solution.py:78
  23.8 0.5 collective-permute-start.6
  24.3 0.9 %collective-permute-done.5.refs_5_ = bf16[80,1280]{1,0:T(8,128)(2,1)S(1)} collective-permute-done((bf16[80,1280]{1,0:T(8,128)(2,1)S(1)}, bf16[80,1280]{1,0:T(8,128)(2,1)S(1)}, u32[]{:S(2)}, u32[]{:S(2)}) %collective-permute-start.5) | collective-permute-done | bytes 204832 | tf_op jit(solution)/shard_map/ppermute | solution.py:73
  26.3 4.1 %own.1 = (bf16[320,2560]{1,0:T(8,128)(2,1)S(1)}, bf16[320,768]{1,0:T(8,128)(2,1)S(1)}, bf16[320,1280]{1,0:T(8,128)(2,1)S(1)}, bf16[320,1280]{1,0:T(8,128)(2,1)S(1)}, bf16[4,80,384]{2,1,0:T(8,128)(2,1)}) custom-call(bf16[80,1280]{1,0:T(8,128)(2,1)S(1)} %get-tuple-element.57.refs_0_, bf16[80,1280]{1,0:T(8,128)(2,1)S(1)} %collective-permute-done.refs_1_, ...), custom_call_target="tpu_custom_call" | custom-call | flops 1 | bytes 1 | tf_op jit(solution)/shard_map/own/pallas_call | solution.py:87
  30.5 0.6 collective-permute-start.16
  31.1 0.5 collective-permute-start.17
  31.6 0.5 collective-permute-start.11
  32.1 0.7 collective-permute-done.10.refs_0_
  33.0 0.7 collective-permute-done.11.refs_2_
  33.7 5.7 %collective-permute-start.13 = (bf16[80,1280]{1,0:T(8,128)(2,1)S(1)}, bf16[80,1280]{1,0:T(8,128)(2,1)S(1)}, u32[]{:S(2)}, u32[]{:S(2)}) collective-permute-start(bf16[80,1280]{1,0:T(8,128)(2,1)S(1)} %get-tuple-element.76), channel_id=1, source_target_pairs={{0,3},{1,0},{2,1},{3,2},{4,7},{5,4},{6,5},{7,6},{8,11},{9,8},{10,9... | collective-permute-start | bytes 614408 | tf_op jit(solution)/shard_map/ppermute | solution.py:78
  39.9 1.4 %part.3 = (bf16[240,2560]{1,0:T(8,128)(2,1)S(1)}, bf16[240,768]{1,0:T(8,128)(2,1)S(1)}) custom-call(bf16[80,1280]{1,0:T(8,128)(2,1)S(1)} %collective-permute-done.3.refs_0_, bf16[160,1280]{1,0:T(8,128)(2,1)S(1)} %collective-permute-done.8.refs_1_, bf16[80,1280]{1,0:T(8,128)(2,1)S(1)} %collective-permute-done.11.refs_2_, ...), custom_call_target="tpu_custom_call" | custom-call | flops 1 | bytes 1 | tf_op jit(solution)/shard_map/part/pallas_call | solution.py:87
  41.3 3.3 %grads_near.1.refs_4_ = f32[768,2560]{1,0:T(8,128)S(1)} custom-call(bf16[320,2560]{1,0:T(8,128)(2,1)S(1)} %get-tuple-element.80.refs_0_, bf16[240,2560]{1,0:T(8,128)(2,1)S(1)} %get-tuple-element.81.refs_1_, bf16[320,768]{1,0:T(8,128)(2,1)S(1)} %get-tuple-element.82.refs_2_, bf16[240,768]{1,0:T(8,128)(2,1)S(1)} %get-tuple-element.83.refs_3_), custom_call_target="tpu_custom_call" | custom-call | flops 1 | bytes 1 | tf_op jit(solution)/shard_map/grads_near/pallas_call | solution.py:87
  44.6 2.2 %collective-permute-done.16.refs_0_ = bf16[240,1280]{1,0:T(8,128)(2,1)S(1)} collective-permute-done((bf16[240,1280]{1,0:T(8,128)(2,1)S(1)}, bf16[240,1280]{1,0:T(8,128)(2,1)S(1)}, u32[]{:S(2)}, u32[]{:S(2)}) %collective-permute-start.16) | collective-permute-done | bytes 614432 | tf_op jit(solution)/shard_map/ppermute | solution.py:73
  47.1 0.6 collective-permute-start.20
  47.7 1.6 %collective-permute-start.21 = (bf16[112,1280]{1,0:T(8,128)(2,1)S(1)}, bf16[112,1280]{1,0:T(8,128)(2,1)S(1)}, u32[]{:S(2)}, u32[]{:S(2)}) collective-permute-start(bf16[112,1280]{1,0:T(8,128)(2,1)S(1)} %slice.7), channel_id=1, source_target_pairs={{0,8},{8,0},{16,24},{24,16},{1,9},{9,1},{17,25},{25,17},{2,10},{10... | collective-permute-start | bytes 860168 | tf_op jit(solution)/shard_map/ppermute | solution.py:73
  49.3 8.8 %collective-permute-done.14.refs_2_ = bf16[80,1280]{1,0:T(8,128)(2,1)S(1)} collective-permute-done((bf16[80,1280]{1,0:T(8,128)(2,1)S(1)}, bf16[80,1280]{1,0:T(8,128)(2,1)S(1)}, u32[]{:S(2)}, u32[]{:S(2)}) %collective-permute-start.14) | collective-permute-done | bytes 204832 | tf_op jit(solution)/shard_map/ppermute | solution.py:78
  58.0 0.5 collective-permute-start.19
  58.5 1.3 %unpack.1 = bf16[128,1280]{1,0:T(8,128)(2,1)} custom-call(s32[1,128]{1,0:T(1,128)S(1)} %bitcast.14, bf16[80,1280]{1,0:T(8,128)(2,1)S(1)} %get-tuple-element.70.refs_0_, bf16[80,1280]{1,0:T(8,128)(2,1)S(1)} %collective-permute-done.13.refs_1_, bf16[80,1280]{1,0:T(8,128)(2,1)S(1)} %collective-permute-done.14.refs_2_, ...), custom_call_target="tpu_custom_call" | custom-call | flops 6000000000 | bytes 1 | tf_op jit(solution)/shard_map/unpack/pallas_call | solution.py:87
  60.3 0.6 collective-permute-done.19.refs_3_
  60.9 2.4 %part.4 = (bf16[480,2560]{1,0:T(8,128)(2,1)S(1)}, bf16[480,768]{1,0:T(8,128)(2,1)S(1)}) custom-call(bf16[240,1280]{1,0:T(8,128)(2,1)S(1)} %collective-permute-done.16.refs_0_, bf16[240,1280]{1,0:T(8,128)(2,1)S(1)} %collective-permute-done.17.refs_1_, bf16[240,1280]{1,0:T(8,128)(2,1)S(1)} %collective-permute-done.18.refs_2_, ...), custom_call_target="tpu_custom_call" | custom-call | flops 1 | bytes 1 | tf_op jit(solution)/shard_map/part/pallas_call | solution.py:87
  63.3 1.4 %part.5 = (bf16[240,2560]{1,0:T(8,128)(2,1)S(1)}, bf16[240,768]{1,0:T(8,128)(2,1)S(1)}) custom-call(bf16[128,1280]{1,0:T(8,128)(2,1)S(1)} %collective-permute-done.20.refs_0_, bf16[112,1280]{1,0:T(8,128)(2,1)S(1)} %collective-permute-done.21.refs_1_, bf16[128,1280]{1,0:T(8,128)(2,1)S(1)} %collective-permute-done.22.refs_2_, ...), custom_call_target="tpu_custom_call" | custom-call | flops 1 | bytes 1 | tf_op jit(solution)/shard_map/part/pallas_call | solution.py:87
  64.8 5.0 %grads.1 = (bf16[384,2560]{1,0:T(8,128)(2,1)}, bf16[384,2560]{1,0:T(8,128)(2,1)}) custom-call(bf16[480,2560]{1,0:T(8,128)(2,1)S(1)} %get-tuple-element.88.refs_0_, bf16[240,2560]{1,0:T(8,128)(2,1)S(1)} %get-tuple-element.94.refs_1_, bf16[480,768]{1,0:T(8,128)(2,1)S(1)} %get-tuple-element.91.refs_2_, bf16[240,768]{1,0:T(8,128)(2,1)S(1)} %get-tuple-element.95.refs_3_, ...), custom_call_target="tpu_custom_call" | custom-call | flops 1 | bytes 1 | tf_op jit(solution)/shard_map/grads/pallas_call | solution.py:87
  (36 shorter events, 2.8 us)
Async XLA Ops:
  2.3 12.2 %collective-permute-start.3 = (bf16[80,1280]{1,0:T(8,128)(2,1)S(1)}, bf16[80,1280]{1,0:T(8,128)(2,1)S(1)}, u32[]{:S(2)}, u32[]{:S(2)}) collective-permute-start(bf16[80,1280]{1,0:T(8,128)(2,1)S(1)} %get-tuple-element.57.refs_0_), channel_id=1, source_target_pairs={{0,8},{8,0},{16,24},{24,16},{1,9},{9,1},{17,25},{25,17},{2,10},{10... | collective-permute-start | bytes 614408 | tf_op jit(solution)/shard_map/ppermute | solution.py:73
  5.3 9.3 %collective-permute-start.4 = (bf16[4,80,384]{2,1,0:T(8,128)(2,1)}, bf16[4,80,384]{2,1,0:T(8,128)(2,1)S(1)}, u32[]{:S(2)}, u32[]{:S(2)}) collective-permute-start(bf16[4,80,384]{2,1,0:T(8,128)(2,1)} %bitcast.10), channel_id=1, source_target_pairs={{0,16},{8,24},{16,0},{24,8},{1,17},{9,25},{17,1},{25,9},{2,18},{10... | collective-permute-start | bytes 737288 | tf_op jit(solution)/shard_map/ppermute | solution.py:73
  6.8 9.9 %collective-permute-start = (bf16[80,1280]{1,0:T(8,128)(2,1)S(1)}, bf16[80,1280]{1,0:T(8,128)(2,1)S(1)}, u32[]{:S(2)}, u32[]{:S(2)}) collective-permute-start(bf16[80,1280]{1,0:T(8,128)(2,1)S(1)} %get-tuple-element.52), channel_id=1, source_target_pairs={{0,1},{1,2},{2,3},{3,0},{4,5},{5,6},{6,7},{7,4},{8,9},{9,10},{10,1... | collective-permute-start | bytes 614408 | tf_op jit(solution)/shard_map/ppermute | solution.py:78
  8.4 15.4 %collective-permute-start.1 = (bf16[80,1280]{1,0:T(8,128)(2,1)S(1)}, bf16[80,1280]{1,0:T(8,128)(2,1)S(1)}, u32[]{:S(2)}, u32[]{:S(2)}) collective-permute-start(bf16[80,1280]{1,0:T(8,128)(2,1)S(1)} %get-tuple-element.53), channel_id=1, source_target_pairs={{0,2},{1,3},{2,0},{3,1},{4,6},{5,7},{6,4},{7,5},{8,10},{9,11},{10,... | collective-permute-start | bytes 614408 | tf_op jit(solution)/shard_map/ppermute | solution.py:78
  11.0 12.8 %collective-permute-start.2 = (bf16[80,1280]{1,0:T(8,128)(2,1)S(1)}, bf16[80,1280]{1,0:T(8,128)(2,1)S(1)}, u32[]{:S(2)}, u32[]{:S(2)}) collective-permute-start(bf16[80,1280]{1,0:T(8,128)(2,1)S(1)} %get-tuple-element.54), channel_id=1, source_target_pairs={{0,3},{1,0},{2,1},{3,2},{4,7},{5,4},{6,5},{7,6},{8,11},{9,8},{10,9... | collective-permute-start | bytes 614408 | tf_op jit(solution)/shard_map/ppermute | solution.py:78
  12.3 2.3 %copy-start = (bf16[1,1,4,80,384]{4,3,2,1,0:T(8,128)(2,1)S(1)}, bf16[1,1,4,80,384]{4,3,2,1,0:T(8,128)(2,1)}, u32[]{:S(2)}) copy-start(bf16[1,1,4,80,384]{4,3,2,1,0:T(8,128)(2,1)} %param.9) | copy-start | bytes 737284
  14.7 11.6 %collective-permute-start.9 = (bf16[2,4,80,384]{3,2,1,0:T(8,128)(2,1)S(1)}, bf16[2,4,80,384]{3,2,1,0:T(8,128)(2,1)S(1)}, u32[]{:S(2)}, u32[]{:S(2)}) collective-permute-start(bf16[2,4,80,384]{3,2,1,0:T(8,128)(2,1)S(1)} %pad_maximum_fusion.1), channel_id=1, source_target_pairs={{0,8},{8,0},{16,24},{24,16},{1,9},{9,1},{17,25},{25,17},{2,10},{10... | collective-permute-start | bytes 1474568 | tf_op jit(solution)/shard_map/ppermute | solution.py:73
  15.3 10.6 %collective-permute-start.8 = (bf16[160,1280]{1,0:T(8,128)(2,1)S(1)}, bf16[160,1280]{1,0:T(8,128)(2,1)S(1)}, u32[]{:S(2)}, u32[]{:S(2)}) collective-permute-start(bf16[160,1280]{1,0:T(8,128)(2,1)S(1)} %constant_dynamic-update-slice_fusion), channel_id=1, source_target_pairs={{0,16},{8,24},{16,0},{24,8},{1,17},{9,25},{17,1},{25,9},{2,18},{10... | collective-permute-start | bytes 1228808 | tf_op jit(solution)/shard_map/ppermute | solution.py:73
  23.8 1.5 %collective-permute-start.5 = (bf16[80,1280]{1,0:T(8,128)(2,1)S(1)}, bf16[80,1280]{1,0:T(8,128)(2,1)S(1)}, u32[]{:S(2)}, u32[]{:S(2)}) collective-permute-start(bf16[80,1280]{1,0:T(8,128)(2,1)S(1)} %collective-permute-done.refs_1_), channel_id=1, source_target_pairs={{0,4},{4,0},{1,5},{5,1},{2,6},{6,2},{3,7},{7,3},{8,12},{12,8},{9,1... | collective-permute-start | bytes 614408 | tf_op jit(solution)/shard_map/ppermute | solution.py:73
  23.8 1.7 %collective-permute-start.6 = (bf16[80,1280]{1,0:T(8,128)(2,1)S(1)}, bf16[80,1280]{1,0:T(8,128)(2,1)S(1)}, u32[]{:S(2)}, u32[]{:S(2)}) collective-permute-start(bf16[80,1280]{1,0:T(8,128)(2,1)S(1)} %collective-permute-done.1.refs_2_), channel_id=1, source_target_pairs={{0,4},{4,0},{1,5},{5,1},{2,6},{6,2},{3,7},{7,3},{8,12},{12,8},{9,1... | collective-permute-start | bytes 614408 | tf_op jit(solution)/shard_map/ppermute | solution.py:73
  24.3 1.5 %collective-permute-start.7 = (bf16[80,1280]{1,0:T(8,128)(2,1)S(1)}, bf16[80,1280]{1,0:T(8,128)(2,1)S(1)}, u32[]{:S(2)}, u32[]{:S(2)}) collective-permute-start(bf16[80,1280]{1,0:T(8,128)(2,1)S(1)} %collective-permute-done.2.refs_3_), channel_id=1, source_target_pairs={{0,4},{4,0},{1,5},{5,1},{2,6},{6,2},{3,7},{7,3},{8,12},{12,8},{9,1... | collective-permute-start | bytes 614408 | tf_op jit(solution)/shard_map/ppermute | solution.py:73
  30.4 2.4 %collective-permute-start.10 = (bf16[320,1280]{1,0:T(8,128)(2,1)S(1)}, bf16[320,1280]{1,0:T(8,128)(2,1)S(1)}, u32[]{:S(2)}, u32[]{:S(2)}) collective-permute-start(bf16[320,1280]{1,0:T(8,128)(2,1)S(1)} %get-tuple-element.69), channel_id=1, source_target_pairs={{0,4},{4,0},{1,5},{5,1},{2,6},{6,2},{3,7},{7,3},{8,12},{12,8},{9,1... | collective-permute-start | bytes 2457608 | tf_op jit(solution)/shard_map/ppermute | solution.py:73
  30.5 16.3 %collective-permute-start.16 = (bf16[240,1280]{1,0:T(8,128)(2,1)S(1)}, bf16[240,1280]{1,0:T(8,128)(2,1)S(1)}, u32[]{:S(2)}, u32[]{:S(2)}) collective-permute-start(bf16[240,1280]{1,0:T(8,128)(2,1)S(1)} %pad_maximum_fusion), channel_id=1, source_target_pairs={{0,8},{8,0},{16,24},{24,16},{1,9},{9,1},{17,25},{25,17},{2,10},{10... | collective-permute-start | bytes 1843208 | tf_op jit(solution)/shard_map/ppermute | solution.py:73
  31.1 16.0 %collective-permute-start.17 = (bf16[240,1280]{1,0:T(8,128)(2,1)S(1)}, bf16[240,1280]{1,0:T(8,128)(2,1)S(1)}, u32[]{:S(2)}, u32[]{:S(2)}) collective-permute-start(bf16[240,1280]{1,0:T(8,128)(2,1)S(1)} %pad_maximum_fusion), channel_id=1, source_target_pairs={{0,16},{8,24},{16,0},{24,8},{1,17},{9,25},{17,1},{25,9},{2,18},{10... | collective-permute-start | bytes 1843208 | tf_op jit(solution)/shard_map/ppermute | solution.py:73
  31.6 2.0 %collective-permute-start.12 = (bf16[160,1280]{1,0:T(8,128)(2,1)S(1)}, bf16[160,1280]{1,0:T(8,128)(2,1)S(1)}, u32[]{:S(2)}, u32[]{:S(2)}) collective-permute-start(bf16[160,1280]{1,0:T(8,128)(2,1)S(1)} %collective-permute-done.8.refs_1_), channel_id=1, source_target_pairs={{0,4},{4,0},{1,5},{5,1},{2,6},{6,2},{3,7},{7,3},{8,12},{12,8},{9,1... | collective-permute-start | bytes 1228808 | tf_op jit(solution)/shard_map/ppermute | solution.py:73
  31.6 2.0 %collective-permute-start.11 = (bf16[80,1280]{1,0:T(8,128)(2,1)S(1)}, bf16[80,1280]{1,0:T(8,128)(2,1)S(1)}, u32[]{:S(2)}, u32[]{:S(2)}) collective-permute-start(bf16[80,1280]{1,0:T(8,128)(2,1)S(1)} %collective-permute-done.3.refs_0_), channel_id=1, source_target_pairs={{0,4},{4,0},{1,5},{5,1},{2,6},{6,2},{3,7},{7,3},{8,12},{12,8},{9,1... | collective-permute-start | bytes 614408 | tf_op jit(solution)/shard_map/ppermute | solution.py:73
  33.7 15.6 %collective-permute-start.13 = (bf16[80,1280]{1,0:T(8,128)(2,1)S(1)}, bf16[80,1280]{1,0:T(8,128)(2,1)S(1)}, u32[]{:S(2)}, u32[]{:S(2)}) collective-permute-start(bf16[80,1280]{1,0:T(8,128)(2,1)S(1)} %get-tuple-element.76), channel_id=1, source_target_pairs={{0,3},{1,0},{2,1},{3,2},{4,7},{5,4},{6,5},{7,6},{8,11},{9,8},{10,9... | collective-permute-start | bytes 614408 | tf_op jit(solution)/shard_map/ppermute | solution.py:78
  39.4 18.7 %collective-permute-start.14 = (bf16[80,1280]{1,0:T(8,128)(2,1)S(1)}, bf16[80,1280]{1,0:T(8,128)(2,1)S(1)}, u32[]{:S(2)}, u32[]{:S(2)}) collective-permute-start(bf16[80,1280]{1,0:T(8,128)(2,1)S(1)} %get-tuple-element.77), channel_id=1, source_target_pairs={{0,2},{1,3},{2,0},{3,1},{4,6},{5,7},{6,4},{7,5},{8,10},{9,11},{10,... | collective-permute-start | bytes 614408 | tf_op jit(solution)/shard_map/ppermute | solution.py:78
  39.8 18.8 %collective-permute-start.15 = (bf16[80,1280]{1,0:T(8,128)(2,1)S(1)}, bf16[80,1280]{1,0:T(8,128)(2,1)S(1)}, u32[]{:S(2)}, u32[]{:S(2)}) collective-permute-start(bf16[80,1280]{1,0:T(8,128)(2,1)S(1)} %get-tuple-element.78), channel_id=1, source_target_pairs={{0,1},{1,2},{2,3},{3,0},{4,5},{5,6},{6,7},{7,4},{8,9},{9,10},{10,1... | collective-permute-start | bytes 614408 | tf_op jit(solution)/shard_map/ppermute | solution.py:78
  41.3 17.2 %copy-start.1 = (s32[128,1]{0,1:T(1,128)S(1)}, s32[128,1]{0,1:T(1,128)}, u32[]{:S(2)}) copy-start(s32[128,1]{0,1:T(1,128)} %param.6) | copy-start | bytes 1540
  47.1 12.7 %collective-permute-start.20 = (bf16[128,1280]{1,0:T(8,128)(2,1)S(1)}, bf16[128,1280]{1,0:T(8,128)(2,1)S(1)}, u32[]{:S(2)}, u32[]{:S(2)}) collective-permute-start(bf16[128,1280]{1,0:T(8,128)(2,1)S(1)} %slice.6), channel_id=1, source_target_pairs={{0,16},{8,24},{16,0},{24,8},{1,17},{9,25},{17,1},{25,9},{2,18},{10... | collective-permute-start | bytes 983048 | tf_op jit(solution)/shard_map/ppermute | solution.py:73
  47.7 12.1 %collective-permute-start.21 = (bf16[112,1280]{1,0:T(8,128)(2,1)S(1)}, bf16[112,1280]{1,0:T(8,128)(2,1)S(1)}, u32[]{:S(2)}, u32[]{:S(2)}) collective-permute-start(bf16[112,1280]{1,0:T(8,128)(2,1)S(1)} %slice.7), channel_id=1, source_target_pairs={{0,8},{8,0},{16,24},{24,16},{1,9},{9,1},{17,25},{25,17},{2,10},{10... | collective-permute-start | bytes 860168 | tf_op jit(solution)/shard_map/ppermute | solution.py:73
  58.0 2.3 %collective-permute-start.18 = (bf16[240,1280]{1,0:T(8,128)(2,1)S(1)}, bf16[240,1280]{1,0:T(8,128)(2,1)S(1)}, u32[]{:S(2)}, u32[]{:S(2)}) collective-permute-start(bf16[240,1280]{1,0:T(8,128)(2,1)S(1)} %collective-permute-done.16.refs_0_), channel_id=1, source_target_pairs={{0,4},{4,0},{1,5},{5,1},{2,6},{6,2},{3,7},{7,3},{8,12},{12,8},{9,1... | collective-permute-start | bytes 1843208 | tf_op jit(solution)/shard_map/ppermute | solution.py:73
  58.0 2.9 %collective-permute-start.19 = (bf16[240,1280]{1,0:T(8,128)(2,1)S(1)}, bf16[240,1280]{1,0:T(8,128)(2,1)S(1)}, u32[]{:S(2)}, u32[]{:S(2)}) collective-permute-start(bf16[240,1280]{1,0:T(8,128)(2,1)S(1)} %collective-permute-done.17.refs_1_), channel_id=1, source_target_pairs={{0,4},{4,0},{1,5},{5,1},{2,6},{6,2},{3,7},{7,3},{8,12},{12,8},{9,1... | collective-permute-start | bytes 1843208 | tf_op jit(solution)/shard_map/ppermute | solution.py:73
  59.8 3.5 %collective-permute-start.22 = (bf16[128,1280]{1,0:T(8,128)(2,1)S(1)}, bf16[128,1280]{1,0:T(8,128)(2,1)S(1)}, u32[]{:S(2)}, u32[]{:S(2)}) collective-permute-start(bf16[128,1280]{1,0:T(8,128)(2,1)S(1)} %collective-permute-done.20.refs_0_), channel_id=1, source_target_pairs={{0,4},{4,0},{1,5},{5,1},{2,6},{6,2},{3,7},{7,3},{8,12},{12,8},{9,1... | collective-permute-start | bytes 983048 | tf_op jit(solution)/shard_map/ppermute | solution.py:73
  59.8 3.5 %collective-permute-start.23 = (bf16[112,1280]{1,0:T(8,128)(2,1)S(1)}, bf16[112,1280]{1,0:T(8,128)(2,1)S(1)}, u32[]{:S(2)}, u32[]{:S(2)}) collective-permute-start(bf16[112,1280]{1,0:T(8,128)(2,1)S(1)} %collective-permute-done.21.refs_1_), channel_id=1, source_target_pairs={{0,4},{4,0},{1,5},{5,1},{2,6},{6,2},{3,7},{7,3},{8,12},{12,8},{9,1... | collective-permute-start | bytes 860168 | tf_op jit(solution)/shard_map/ppermute | solution.py:73

commit v5 on v4

--- a/solution.py
+++ b/solution.py
@@ -156,10 +156,14 @@
     outs[count][...] = dot(placing[:capacity], theirs[...], MATMUL).astype(BF16)
 
 
-def unpack_kernel(capacity, expert_ref, *refs):
+def place_kernel(capacity, expert_ref, out):
+    out[...] = jnp.transpose(place_rows(expert_ref, capacity))
+
+
+def unpack_kernel(placing_ref, *refs):
     *pieces, out = refs
     rows = jnp.concatenate([p[...] for p in pieces])
-    out[...] = dot(place_rows(expert_ref, capacity), rows, FIRST).astype(BF16)
+    out[...] = dot(placing_ref[...], rows, MATMUL).astype(BF16)
 
 
 def sum_kernel(kept_ref, *refs):
@@ -192,7 +196,7 @@
 def own_kernel(blocks, *refs):
     n = len(blocks)
     pieces, others = refs[:n], refs[n : 2 * n]
-    cotan_ref, rows_ref, full, d_ref, kept_ref, sent_ref, hidden_ref, sem = refs[2 * n :]
+    cotan_ref, rows_ref, full, d_ref, sent_ref, hidden_ref, sem = refs[2 * n :]
     core, half = lax.axis_index("shard"), full.shape[1] // 2
     capacity, units = cotan_ref.shape[1:]
     fill(pieces, others, full, sem)
@@ -204,8 +208,13 @@
         hidden_ref[source_of(k)] = (gate * sigma * up).astype(BF16)
         d_ref[at, :units] = d_gate
         d_ref[at, units:] = d_up
-    for side, out in ((1 - core, sent_ref), (core, kept_ref)):
-        out[...] = dot(d_ref[...], rows_ref[:, side_of(side, half)], MATMUL).astype(BF16)
+    theirs = rows_ref[:, side_of(1 - core, half)]
+    sent_ref[...] = dot(d_ref[...], theirs, MATMUL).astype(BF16)
+
+
+def kept_kernel(d_ref, rows_ref, kept_ref):
+    mine = rows_ref[:, side_of(lax.axis_index("shard"), kept_ref.shape[1])]
+    kept_ref[...] = dot(d_ref[...], mine, MATMUL).astype(BF16)
 
 
 def part_kernel(plan, n, *refs):
@@ -230,11 +239,16 @@
 
 def last_grad_kernel(scale, n, *refs):
     fulls, ds = refs[:n], refs[n : 2 * n]
-    earlier, gate_out, up_out, staged, sem = refs[2 * n :]
-    units, quarter, copies = gate_out.shape[0], staged.shape[1] // 4, []
-    for i in range(4):
-        columns = slice(i * quarter, (i + 1) * quarter)
-        total = sum(dot(d[...], full[:, columns], FIRST) for d, full in zip(ds, fulls))
+    earlier, gate_out, up_out, staged, held, sem = refs[2 * n :]
+    units, copies, start = gate_out.shape[0], [], 0
+    for d in ds:
+        held[start : start + d.shape[0]] = d[...]
+        start += d.shape[0]
+    blocks = sem.shape[0]
+    wide = staged.shape[1] // blocks
+    for i in range(blocks):
+        columns = slice(i * wide, (i + 1) * wide)
+        total = dot(held[...], jnp.concatenate([full[:, columns] for full in fulls]), FIRST)
         staged[:, columns] = ((total + earlier[:, columns]) * scale).astype(BF16)
         for j, out in enumerate((gate_out, up_out)):
             copies.append(
@@ -270,7 +284,7 @@
             functools.partial(own_kernel, pair),
             [ANY] * (2 * len(rows)) + [VMEM] * 2,
             [like(n, width), like(n, 2 * hidden_width)]
-            + [like(n, half)] * 2
+            + [like(n, half)]
             + [like(len(pair), capacity, hidden_width)],
             [*rows, *others, cotan, both_rows],
             scratch=sem,
@@ -327,12 +341,14 @@
     o1, o2, o3 = swap(z1), swap(z2), swap(z3)
     c123 = jnp.concatenate([z1, z2, z3])
     o1, o2, o3 = after([o1, o2, o3], c0_far, cotan_far)
-    full_a, d_a, kept, sent, hidden = own((0, 1, 2, 3), [c0, z1, z2, z3], [other, o1, o2, o3])
-    c123_sent, c0_near_sent, c0_far_sent = after([c123, c0_near, c0_far], kept)
+    full_a, d_a, sent, hidden = own((0, 1, 2, 3), [c0, z1, z2, z3], [other, o1, o2, o3])
+    (kept,) = call(
+        kept_kernel, [VMEM] * 2, [like(count * capacity, half)], [d_a, both_rows], name="kept"
+    )
+    c123_sent, c0_near_sent, c0_far_sent = after([c123, c0_near, c0_far], sent)
     c123_x, c123_y = across(c123_sent, "rep", 1), across(c123_sent, "rep", 2)
     c0_others = [swap(c0_near_sent), swap(c0_far_sent)]
     r0, r1, r2, r3 = add(kept, swap(sent))
-    r1, r2, r3 = after([r1, r2, r3], *c0_others)
     r1, r2, r3 = turned(r1, "exp", -1), turned(r2, "exp", -2), turned(r3, "exp", -3)
 
     plan = ((0, 1), (0, 2), (0, 3))
@@ -345,14 +361,21 @@
         name="grads_near",
         limit=32,
     )
-    c123_x, c123_y = after([c123_x, c123_y], total)
+    (placing,) = call(
+        functools.partial(place_kernel, capacity),
+        [VMEM],
+        [like(tokens.shape[0], count * capacity)],
+        after([experts], d_c),
+        name="place",
+    )
+    c123_x, c123_y = after([c123_x, c123_y], total, placing)
     cut = (c123.shape[0] // 2 + 15) // 16 * 16
     far_sent = [across(c123_x[:cut], "rep", 2), across(c123_y[cut:], "rep", 1)]
     (d_tokens,) = call(
-        functools.partial(unpack_kernel, capacity),
+        unpack_kernel,
         [VMEM] * (1 + count),
         [like(tokens.shape[0], half)],
-        [experts, r0, r1, r2, r3],
+        [placing, r0, r1, r2, r3],
         name="unpack",
         flops=6*10**9,
     )
@@ -371,7 +394,11 @@
         [VMEM] * 5,
         [like(hidden_width, width)] * 2,
         [full_d, full_e, d_d, d_e, total],
-        scratch=[pltpu.VMEM((2 * hidden_width, width), BF16), pltpu.SemaphoreType.DMA((4, 2))],
+        scratch=[
+            pltpu.VMEM((2 * hidden_width, width), BF16),
+            pltpu.VMEM((d_d.shape[0] + d_e.shape[0], 2 * hidden_width), BF16),
+            pltpu.SemaphoreType.DMA((5, 2)),
+        ],
         name="grads",
         limit=32,
         out_spec=HBM,

time: 70.1 us -> 67.9 us (0.969)
  waiting for transfers between devices: 23.1 us -> 21.2 us
    ppermute x18, waiting for transfers between devices: 6.43 us -> 5.06 us  [across(): return lax.ppermute(x, axis, [(i, i ^ bit) for i in range(size)])]
    pallas_call x10 -> x12, Pallas kernels: 22.8 us -> 22.1 us  [call(): pl.pallas_call(kernel, in_specs=ins, out_specs=[out_spec] * len(outs), ou...]
  transfers between devices with their start and end apart: 24 -> 24, of which waited for: 12 -> 10; matrix products, arithmetic and copies ran while one was open for 0% -> 0% of each run, Pallas kernels for 15% -> 17%
where the time goes in v5:
time: 67.9 us; the launch traced here: 67.8 us
  starting transfers between devices  23.3 us (34%)
  Pallas kernels  22.1 us (33%)
  waiting for transfers between devices  21.2 us (31%)
  between operations  0.99 us (1%)
    pallas_call x12, Pallas kernels, call(): pl.pallas_call(kernel, in_specs=ins, out_specs=[out_spec] * len(outs), ou...  22.1 us
    ppermute x6, waiting for transfers between devices, turned(): return lax.ppermute(x, axis, [(i, (i + step) % size) for i in range(size)])  16.1 us
    ppermute x6, starting transfers between devices, turned(): return lax.ppermute(x, axis, [(i, (i + step) % size) for i in range(size)])  12.3 us
    ppermute x18, starting transfers between devices, across(): return lax.ppermute(x, axis, [(i, i ^ bit) for i in range(size)])  11 us
    ppermute x18, waiting for transfers between devices, across(): return lax.ppermute(x, axis, [(i, i ^ bit) for i in range(size)])  5.06 us
  transfers between devices with their start and end apart: 24, of which 10 were waited for; matrix products, arithmetic and copies ran while one was open for 0% of the time, Pallas kernels for 17%

profile of v5, /device:TPU:0, one launch (start us, length us, event | category | flops | bytes accessed | tf_op | source)
XLA Modules:
  0.0 67.8 jit_solution(13741288075995710973)
XLA Ops:
  0.6 1.7 %pack.1 = (bf16[80,1280]{1,0:T(8,128)(2,1)S(1)}, bf16[80,1280]{1,0:T(8,128)(2,1)S(1)}, bf16[80,1280]{1,0:T(8,128)(2,1)S(1)}, bf16[80,1280]{1,0:T(8,128)(2,1)S(1)}, bf16[80,1280]{1,0:T(8,128)(2,1)S(1)}) custom-call(s32[1,128]{1,0:T(1,128)} %bitcast.13, bf16[128,2560]{1,0:T(8,128)(2,1)} %tokens_hbm.1), custom_call_target="tpu_custom_call" | custom-call | flops 1 | bytes 1 | tf_op jit(solution)/shard_map/pack/pallas_call | solution.py:87
  2.3 3.0 %collective-permute-start.3 = (bf16[80,1280]{1,0:T(8,128)(2,1)S(1)}, bf16[80,1280]{1,0:T(8,128)(2,1)S(1)}, u32[]{:S(2)}, u32[]{:S(2)}) collective-permute-start(bf16[80,1280]{1,0:T(8,128)(2,1)S(1)} %get-tuple-element.54.refs_0_), channel_id=1, source_target_pairs={{0,8},{8,0},{16,24},{24,16},{1,9},{9,1},{17,25},{25,17},{2,10},{10... | collective-permute-start | bytes 614408 | tf_op jit(solution)/shard_map/ppermute | solution.py:73
  5.3 1.5 %collective-permute-start.4 = (bf16[4,80,384]{2,1,0:T(8,128)(2,1)}, bf16[4,80,384]{2,1,0:T(8,128)(2,1)S(1)}, u32[]{:S(2)}, u32[]{:S(2)}) collective-permute-start(bf16[4,80,384]{2,1,0:T(8,128)(2,1)} %bitcast.10), channel_id=1, source_target_pairs={{0,16},{8,24},{16,0},{24,8},{1,17},{9,25},{17,1},{25,9},{2,18},{10... | collective-permute-start | bytes 737288 | tf_op jit(solution)/shard_map/ppermute | solution.py:73
  6.8 1.6 %collective-permute-start = (bf16[80,1280]{1,0:T(8,128)(2,1)S(1)}, bf16[80,1280]{1,0:T(8,128)(2,1)S(1)}, u32[]{:S(2)}, u32[]{:S(2)}) collective-permute-start(bf16[80,1280]{1,0:T(8,128)(2,1)S(1)} %get-tuple-element.49), channel_id=1, source_target_pairs={{0,1},{1,2},{2,3},{3,0},{4,5},{5,6},{6,7},{7,4},{8,9},{9,10},{10,1... | collective-permute-start | bytes 614408 | tf_op jit(solution)/shard_map/ppermute | solution.py:78
  8.4 2.6 %collective-permute-start.1 = (bf16[80,1280]{1,0:T(8,128)(2,1)S(1)}, bf16[80,1280]{1,0:T(8,128)(2,1)S(1)}, u32[]{:S(2)}, u32[]{:S(2)}) collective-permute-start(bf16[80,1280]{1,0:T(8,128)(2,1)S(1)} %get-tuple-element.50), channel_id=1, source_target_pairs={{0,2},{1,3},{2,0},{3,1},{4,6},{5,7},{6,4},{7,5},{8,10},{9,11},{10,... | collective-permute-start | bytes 614408 | tf_op jit(solution)/shard_map/ppermute | solution.py:78
  11.0 1.3 %collective-permute-start.2 = (bf16[80,1280]{1,0:T(8,128)(2,1)S(1)}, bf16[80,1280]{1,0:T(8,128)(2,1)S(1)}, u32[]{:S(2)}, u32[]{:S(2)}) collective-permute-start(bf16[80,1280]{1,0:T(8,128)(2,1)S(1)} %get-tuple-element.51), channel_id=1, source_target_pairs={{0,3},{1,0},{2,1},{3,2},{4,7},{5,4},{6,5},{7,6},{8,11},{9,8},{10,9... | collective-permute-start | bytes 614408 | tf_op jit(solution)/shard_map/ppermute | solution.py:78
  12.3 2.2 %load.1.refs_9_.refs_6_.rows_ref = bf16[768,2560]{1,0:T(8,128)(2,1)S(1)} custom-call(bf16[384,2560]{1,0:T(8,128)(2,1)} %bitcast.15, bf16[384,2560]{1,0:T(8,128)(2,1)} %bitcast.16), custom_call_target="tpu_custom_call" | custom-call | flops 1 | bytes 1 | tf_op jit(solution)/shard_map/load/pallas_call | solution.py:87
  14.7 0.6 collective-permute-start.9
  15.3 0.6 collective-permute-start.8
  15.8 0.9 %collective-permute-done.refs_1_ = bf16[80,1280]{1,0:T(8,128)(2,1)S(1)} collective-permute-done((bf16[80,1280]{1,0:T(8,128)(2,1)S(1)}, bf16[80,1280]{1,0:T(8,128)(2,1)S(1)}, u32[]{:S(2)}, u32[]{:S(2)}) %collective-permute-start) | collective-permute-done | bytes 204832 | tf_op jit(solution)/shard_map/ppermute | solution.py:78
  16.7 7.1 %collective-permute-done.1.refs_2_ = bf16[80,1280]{1,0:T(8,128)(2,1)S(1)} collective-permute-done((bf16[80,1280]{1,0:T(8,128)(2,1)S(1)}, bf16[80,1280]{1,0:T(8,128)(2,1)S(1)}, u32[]{:S(2)}, u32[]{:S(2)}) %collective-permute-start.1) | collective-permute-done | bytes 204832 | tf_op jit(solution)/shard_map/ppermute | solution.py:78
  23.8 0.5 collective-permute-start.6
  24.3 0.9 %collective-permute-done.5.refs_5_ = bf16[80,1280]{1,0:T(8,128)(2,1)S(1)} collective-permute-done((bf16[80,1280]{1,0:T(8,128)(2,1)S(1)}, bf16[80,1280]{1,0:T(8,128)(2,1)S(1)}, u32[]{:S(2)}, u32[]{:S(2)}) %collective-permute-start.5) | collective-permute-done | bytes 204832 | tf_op jit(solution)/shard_map/ppermute | solution.py:73
  26.3 3.3 %own.1 = (bf16[320,2560]{1,0:T(8,128)(2,1)S(1)}, bf16[320,768]{1,0:T(8,128)(2,1)S(1)}, bf16[320,1280]{1,0:T(8,128)(2,1)S(1)}, bf16[4,80,384]{2,1,0:T(8,128)(2,1)}) custom-call(bf16[80,1280]{1,0:T(8,128)(2,1)S(1)} %get-tuple-element.54.refs_0_, bf16[80,1280]{1,0:T(8,128)(2,1)S(1)} %collective-permute-done.refs_1_, ...), custom_call_target="tpu_custom_call" | custom-call | flops 1 | bytes 1 | tf_op jit(solution)/shard_map/own/pallas_call | solution.py:87
  29.7 0.6 collective-permute-start.16
  30.3 0.5 collective-permute-start.17
  30.8 0.5 collective-permute-start.10
  31.3 0.8 %kept.1.kept_ref = bf16[320,1280]{1,0:T(8,128)(2,1)S(1)} custom-call(bf16[320,768]{1,0:T(8,128)(2,1)S(1)} %get-tuple-element.70.d_ref.refs_2_, bf16[768,2560]{1,0:T(8,128)(2,1)S(1)} %load.1.refs_9_.refs_6_.rows_ref), custom_call_target="tpu_custom_call" | custom-call | flops 1 | bytes 1 | tf_op jit(solution)/shard_map/kept/pallas_call | solution.py:87
  32.3 5.7 %collective-permute-start.13 = (bf16[80,1280]{1,0:T(8,128)(2,1)S(1)}, bf16[80,1280]{1,0:T(8,128)(2,1)S(1)}, u32[]{:S(2)}, u32[]{:S(2)}) collective-permute-start(bf16[80,1280]{1,0:T(8,128)(2,1)S(1)} %get-tuple-element.72), channel_id=1, source_target_pairs={{0,3},{1,0},{2,1},{3,2},{4,7},{5,4},{6,5},{7,6},{8,11},{9,8},{10,9... | collective-permute-start | bytes 614408 | tf_op jit(solution)/shard_map/ppermute | solution.py:78
  38.4 0.6 collective-permute-start.15
  39.1 1.4 %part.3 = (bf16[240,2560]{1,0:T(8,128)(2,1)S(1)}, bf16[240,768]{1,0:T(8,128)(2,1)S(1)}) custom-call(bf16[80,1280]{1,0:T(8,128)(2,1)S(1)} %collective-permute-done.3.refs_0_, bf16[160,1280]{1,0:T(8,128)(2,1)S(1)} %collective-permute-done.8.refs_1_, bf16[80,1280]{1,0:T(8,128)(2,1)S(1)} %collective-permute-done.10.refs_2_, ...), custom_call_target="tpu_custom_call" | custom-call | flops 1 | bytes 1 | tf_op jit(solution)/shard_map/part/pallas_call | solution.py:87
  40.7 3.3 %grads_near.1.refs_4_ = f32[768,2560]{1,0:T(8,128)S(1)} custom-call(bf16[320,2560]{1,0:T(8,128)(2,1)S(1)} %get-tuple-element.76.refs_0_, bf16[240,2560]{1,0:T(8,128)(2,1)S(1)} %get-tuple-element.77.refs_1_, bf16[320,768]{1,0:T(8,128)(2,1)S(1)} %get-tuple-element.70.d_ref.refs_2_, bf16[240,768]{1,0:T(8,128)(2,1)S(1)} %get-tuple-element.68.refs_3_), custom_call_target="tpu_custom_call" | custom-call | flops 1 | bytes 1 | tf_op jit(solution)/shard_map/grads_near/pallas_call | solution.py:87
  44.0 2.0 %collective-permute-done.16.refs_0_ = bf16[240,1280]{1,0:T(8,128)(2,1)S(1)} collective-permute-done((bf16[240,1280]{1,0:T(8,128)(2,1)S(1)}, bf16[240,1280]{1,0:T(8,128)(2,1)S(1)}, u32[]{:S(2)}, u32[]{:S(2)}) %collective-permute-start.16) | collective-permute-done | bytes 614432 | tf_op jit(solution)/shard_map/ppermute | solution.py:73
  46.3 0.6 collective-permute-start.20
  46.9 1.6 %collective-permute-start.21 = (bf16[112,1280]{1,0:T(8,128)(2,1)S(1)}, bf16[112,1280]{1,0:T(8,128)(2,1)S(1)}, u32[]{:S(2)}, u32[]{:S(2)}) collective-permute-start(bf16[112,1280]{1,0:T(8,128)(2,1)S(1)} %slice.7), channel_id=1, source_target_pairs={{0,8},{8,0},{16,24},{24,16},{1,9},{9,1},{17,25},{25,17},{2,10},{10... | collective-permute-start | bytes 860168 | tf_op jit(solution)/shard_map/ppermute | solution.py:73
  48.4 8.1 %collective-permute-done.14.refs_2_ = bf16[80,1280]{1,0:T(8,128)(2,1)S(1)} collective-permute-done((bf16[80,1280]{1,0:T(8,128)(2,1)S(1)}, bf16[80,1280]{1,0:T(8,128)(2,1)S(1)}, u32[]{:S(2)}, u32[]{:S(2)}) %collective-permute-start.14) | collective-permute-done | bytes 204832 | tf_op jit(solution)/shard_map/ppermute | solution.py:78
  56.6 0.5 collective-permute-start.19
  57.1 1.1 %unpack.1 = bf16[128,1280]{1,0:T(8,128)(2,1)} custom-call(bf16[128,320]{1,0:T(8,128)(2,1)S(1)} %place.1.placing_ref, bf16[80,1280]{1,0:T(8,128)(2,1)S(1)} %get-tuple-element.71.refs_0_, bf16[80,1280]{1,0:T(8,128)(2,1)S(1)} %collective-permute-done.13.refs_1_, bf16[80,1280]{1,0:T(8,128)(2,1)S(1)} %collective-permute-done.14.refs_2_, ...), custom_call_target="tpu_custom_call" | custom-call | flops 6000000000 | bytes 1 | tf_op jit(solution)/shard_map/unpack/pallas_call | solution.py:87
  58.7 0.8 %collective-permute-done.19.refs_3_ = bf16[240,1280]{1,0:T(8,128)(2,1)S(1)} collective-permute-done((bf16[240,1280]{1,0:T(8,128)(2,1)S(1)}, bf16[240,1280]{1,0:T(8,128)(2,1)S(1)}, u32[]{:S(2)}, u32[]{:S(2)}) %collective-permute-start.19) | collective-permute-done | bytes 614432 | tf_op jit(solution)/shard_map/ppermute | solution.py:73
  59.5 2.4 %part.4 = (bf16[480,2560]{1,0:T(8,128)(2,1)S(1)}, bf16[480,768]{1,0:T(8,128)(2,1)S(1)}) custom-call(bf16[240,1280]{1,0:T(8,128)(2,1)S(1)} %collective-permute-done.16.refs_0_, bf16[240,1280]{1,0:T(8,128)(2,1)S(1)} %collective-permute-done.17.refs_1_, bf16[240,1280]{1,0:T(8,128)(2,1)S(1)} %collective-permute-done.18.refs_2_, ...), custom_call_target="tpu_custom_call" | custom-call | flops 1 | bytes 1 | tf_op jit(solution)/shard_map/part/pallas_call | solution.py:87
  61.9 1.4 %part.5 = (bf16[240,2560]{1,0:T(8,128)(2,1)S(1)}, bf16[240,768]{1,0:T(8,128)(2,1)S(1)}) custom-call(bf16[128,1280]{1,0:T(8,128)(2,1)S(1)} %collective-permute-done.20.refs_0_, bf16[112,1280]{1,0:T(8,128)(2,1)S(1)} %collective-permute-done.21.refs_1_, bf16[128,1280]{1,0:T(8,128)(2,1)S(1)} %collective-permute-done.22.refs_2_, ...), custom_call_target="tpu_custom_call" | custom-call | flops 1 | bytes 1 | tf_op jit(solution)/shard_map/part/pallas_call | solution.py:87
  63.3 4.3 %grads.1 = (bf16[384,2560]{1,0:T(8,128)(2,1)}, bf16[384,2560]{1,0:T(8,128)(2,1)}) custom-call(bf16[480,2560]{1,0:T(8,128)(2,1)S(1)} %get-tuple-element.82.refs_0_, bf16[240,2560]{1,0:T(8,128)(2,1)S(1)} %get-tuple-element.88.refs_1_, bf16[480,768]{1,0:T(8,128)(2,1)S(1)} %get-tuple-element.85.refs_2_, bf16[240,768]{1,0:T(8,128)(2,1)S(1)} %get-tuple-element.89.refs_3_, ...), custom_call_target="tpu_custom_call" | custom-call | flops 1 | bytes 1 | tf_op jit(solution)/shard_map/grads/pallas_call | solution.py:87
  (38 shorter events, 2.9 us)
Async XLA Ops:
  2.3 12.2 %collective-permute-start.3 = (bf16[80,1280]{1,0:T(8,128)(2,1)S(1)}, bf16[80,1280]{1,0:T(8,128)(2,1)S(1)}, u32[]{:S(2)}, u32[]{:S(2)}) collective-permute-start(bf16[80,1280]{1,0:T(8,128)(2,1)S(1)} %get-tuple-element.54.refs_0_), channel_id=1, source_target_pairs={{0,8},{8,0},{16,24},{24,16},{1,9},{9,1},{17,25},{25,17},{2,10},{10... | collective-permute-start | bytes 614408 | tf_op jit(solution)/shard_map/ppermute | solution.py:73
  5.3 9.3 %collective-permute-start.4 = (bf16[4,80,384]{2,1,0:T(8,128)(2,1)}, bf16[4,80,384]{2,1,0:T(8,128)(2,1)S(1)}, u32[]{:S(2)}, u32[]{:S(2)}) collective-permute-start(bf16[4,80,384]{2,1,0:T(8,128)(2,1)} %bitcast.10), channel_id=1, source_target_pairs={{0,16},{8,24},{16,0},{24,8},{1,17},{9,25},{17,1},{25,9},{2,18},{10... | collective-permute-start | bytes 737288 | tf_op jit(solution)/shard_map/ppermute | solution.py:73
  6.8 9.9 %collective-permute-start = (bf16[80,1280]{1,0:T(8,128)(2,1)S(1)}, bf16[80,1280]{1,0:T(8,128)(2,1)S(1)}, u32[]{:S(2)}, u32[]{:S(2)}) collective-permute-start(bf16[80,1280]{1,0:T(8,128)(2,1)S(1)} %get-tuple-element.49), channel_id=1, source_target_pairs={{0,1},{1,2},{2,3},{3,0},{4,5},{5,6},{6,7},{7,4},{8,9},{9,10},{10,1... | collective-permute-start | bytes 614408 | tf_op jit(solution)/shard_map/ppermute | solution.py:78
  8.4 15.4 %collective-permute-start.1 = (bf16[80,1280]{1,0:T(8,128)(2,1)S(1)}, bf16[80,1280]{1,0:T(8,128)(2,1)S(1)}, u32[]{:S(2)}, u32[]{:S(2)}) collective-permute-start(bf16[80,1280]{1,0:T(8,128)(2,1)S(1)} %get-tuple-element.50), channel_id=1, source_target_pairs={{0,2},{1,3},{2,0},{3,1},{4,6},{5,7},{6,4},{7,5},{8,10},{9,11},{10,... | collective-permute-start | bytes 614408 | tf_op jit(solution)/shard_map/ppermute | solution.py:78
  11.0 12.8 %collective-permute-start.2 = (bf16[80,1280]{1,0:T(8,128)(2,1)S(1)}, bf16[80,1280]{1,0:T(8,128)(2,1)S(1)}, u32[]{:S(2)}, u32[]{:S(2)}) collective-permute-start(bf16[80,1280]{1,0:T(8,128)(2,1)S(1)} %get-tuple-element.51), channel_id=1, source_target_pairs={{0,3},{1,0},{2,1},{3,2},{4,7},{5,4},{6,5},{7,6},{8,11},{9,8},{10,9... | collective-permute-start | bytes 614408 | tf_op jit(solution)/shard_map/ppermute | solution.py:78
  12.3 2.3 %copy-start = (bf16[1,1,4,80,384]{4,3,2,1,0:T(8,128)(2,1)S(1)}, bf16[1,1,4,80,384]{4,3,2,1,0:T(8,128)(2,1)}, u32[]{:S(2)}) copy-start(bf16[1,1,4,80,384]{4,3,2,1,0:T(8,128)(2,1)} %param.9) | copy-start | bytes 737284
  14.7 11.6 %collective-permute-start.9 = (bf16[2,4,80,384]{3,2,1,0:T(8,128)(2,1)S(1)}, bf16[2,4,80,384]{3,2,1,0:T(8,128)(2,1)S(1)}, u32[]{:S(2)}, u32[]{:S(2)}) collective-permute-start(bf16[2,4,80,384]{3,2,1,0:T(8,128)(2,1)S(1)} %pad_maximum_fusion.1), channel_id=1, source_target_pairs={{0,8},{8,0},{16,24},{24,16},{1,9},{9,1},{17,25},{25,17},{2,10},{10... | collective-permute-start | bytes 1474568 | tf_op jit(solution)/shard_map/ppermute | solution.py:73
  15.3 10.6 %collective-permute-start.8 = (bf16[160,1280]{1,0:T(8,128)(2,1)S(1)}, bf16[160,1280]{1,0:T(8,128)(2,1)S(1)}, u32[]{:S(2)}, u32[]{:S(2)}) collective-permute-start(bf16[160,1280]{1,0:T(8,128)(2,1)S(1)} %constant_dynamic-update-slice_fusion), channel_id=1, source_target_pairs={{0,16},{8,24},{16,0},{24,8},{1,17},{9,25},{17,1},{25,9},{2,18},{10... | collective-permute-start | bytes 1228808 | tf_op jit(solution)/shard_map/ppermute | solution.py:73
  23.8 1.5 %collective-permute-start.5 = (bf16[80,1280]{1,0:T(8,128)(2,1)S(1)}, bf16[80,1280]{1,0:T(8,128)(2,1)S(1)}, u32[]{:S(2)}, u32[]{:S(2)}) collective-permute-start(bf16[80,1280]{1,0:T(8,128)(2,1)S(1)} %collective-permute-done.refs_1_), channel_id=1, source_target_pairs={{0,4},{4,0},{1,5},{5,1},{2,6},{6,2},{3,7},{7,3},{8,12},{12,8},{9,1... | collective-permute-start | bytes 614408 | tf_op jit(solution)/shard_map/ppermute | solution.py:73
  23.8 1.7 %collective-permute-start.6 = (bf16[80,1280]{1,0:T(8,128)(2,1)S(1)}, bf16[80,1280]{1,0:T(8,128)(2,1)S(1)}, u32[]{:S(2)}, u32[]{:S(2)}) collective-permute-start(bf16[80,1280]{1,0:T(8,128)(2,1)S(1)} %collective-permute-done.1.refs_2_), channel_id=1, source_target_pairs={{0,4},{4,0},{1,5},{5,1},{2,6},{6,2},{3,7},{7,3},{8,12},{12,8},{9,1... | collective-permute-start | bytes 614408 | tf_op jit(solution)/shard_map/ppermute | solution.py:73
  24.3 1.5 %collective-permute-start.7 = (bf16[80,1280]{1,0:T(8,128)(2,1)S(1)}, bf16[80,1280]{1,0:T(8,128)(2,1)S(1)}, u32[]{:S(2)}, u32[]{:S(2)}) collective-permute-start(bf16[80,1280]{1,0:T(8,128)(2,1)S(1)} %collective-permute-done.2.refs_3_), channel_id=1, source_target_pairs={{0,4},{4,0},{1,5},{5,1},{2,6},{6,2},{3,7},{7,3},{8,12},{12,8},{9,1... | collective-permute-start | bytes 614408 | tf_op jit(solution)/shard_map/ppermute | solution.py:73
  29.6 2.6 %collective-permute-start.12 = (bf16[320,1280]{1,0:T(8,128)(2,1)S(1)}, bf16[320,1280]{1,0:T(8,128)(2,1)S(1)}, u32[]{:S(2)}, u32[]{:S(2)}) collective-permute-start(bf16[320,1280]{1,0:T(8,128)(2,1)S(1)} %get-tuple-element.65), channel_id=1, source_target_pairs={{0,4},{4,0},{1,5},{5,1},{2,6},{6,2},{3,7},{7,3},{8,12},{12,8},{9,1... | collective-permute-start | bytes 2457608 | tf_op jit(solution)/shard_map/ppermute | solution.py:73
  29.7 16.3 %collective-permute-start.16 = (bf16[240,1280]{1,0:T(8,128)(2,1)S(1)}, bf16[240,1280]{1,0:T(8,128)(2,1)S(1)}, u32[]{:S(2)}, u32[]{:S(2)}) collective-permute-start(bf16[240,1280]{1,0:T(8,128)(2,1)S(1)} %pad_maximum_fusion), channel_id=1, source_target_pairs={{0,8},{8,0},{16,24},{24,16},{1,9},{9,1},{17,25},{25,17},{2,10},{10... | collective-permute-start | bytes 1843208 | tf_op jit(solution)/shard_map/ppermute | solution.py:73
  30.3 16.0 %collective-permute-start.17 = (bf16[240,1280]{1,0:T(8,128)(2,1)S(1)}, bf16[240,1280]{1,0:T(8,128)(2,1)S(1)}, u32[]{:S(2)}, u32[]{:S(2)}) collective-permute-start(bf16[240,1280]{1,0:T(8,128)(2,1)S(1)} %pad_maximum_fusion), channel_id=1, source_target_pairs={{0,16},{8,24},{16,0},{24,8},{1,17},{9,25},{17,1},{25,9},{2,18},{10... | collective-permute-start | bytes 1843208 | tf_op jit(solution)/shard_map/ppermute | solution.py:73
  30.8 7.7 %collective-permute-start.11 = (bf16[160,1280]{1,0:T(8,128)(2,1)S(1)}, bf16[160,1280]{1,0:T(8,128)(2,1)S(1)}, u32[]{:S(2)}, u32[]{:S(2)}) collective-permute-start(bf16[160,1280]{1,0:T(8,128)(2,1)S(1)} %collective-permute-done.8.refs_1_), channel_id=1, source_target_pairs={{0,4},{4,0},{1,5},{5,1},{2,6},{6,2},{3,7},{7,3},{8,12},{12,8},{9,1... | collective-permute-start | bytes 1228808 | tf_op jit(solution)/shard_map/ppermute | solution.py:73
  30.8 7.3 %collective-permute-start.10 = (bf16[80,1280]{1,0:T(8,128)(2,1)S(1)}, bf16[80,1280]{1,0:T(8,128)(2,1)S(1)}, u32[]{:S(2)}, u32[]{:S(2)}) collective-permute-start(bf16[80,1280]{1,0:T(8,128)(2,1)S(1)} %collective-permute-done.3.refs_0_), channel_id=1, source_target_pairs={{0,4},{4,0},{1,5},{5,1},{2,6},{6,2},{3,7},{7,3},{8,12},{12,8},{9,1... | collective-permute-start | bytes 614408 | tf_op jit(solution)/shard_map/ppermute | solution.py:73
  32.3 16.1 %collective-permute-start.13 = (bf16[80,1280]{1,0:T(8,128)(2,1)S(1)}, bf16[80,1280]{1,0:T(8,128)(2,1)S(1)}, u32[]{:S(2)}, u32[]{:S(2)}) collective-permute-start(bf16[80,1280]{1,0:T(8,128)(2,1)S(1)} %get-tuple-element.72), channel_id=1, source_target_pairs={{0,3},{1,0},{2,1},{3,2},{4,7},{5,4},{6,5},{7,6},{8,11},{9,8},{10,9... | collective-permute-start | bytes 614408 | tf_op jit(solution)/shard_map/ppermute | solution.py:78
  38.1 18.5 %collective-permute-start.14 = (bf16[80,1280]{1,0:T(8,128)(2,1)S(1)}, bf16[80,1280]{1,0:T(8,128)(2,1)S(1)}, u32[]{:S(2)}, u32[]{:S(2)}) collective-permute-start(bf16[80,1280]{1,0:T(8,128)(2,1)S(1)} %get-tuple-element.73), channel_id=1, source_target_pairs={{0,2},{1,3},{2,0},{3,1},{4,6},{5,7},{6,4},{7,5},{8,10},{9,11},{10,... | collective-permute-start | bytes 614408 | tf_op jit(solution)/shard_map/ppermute | solution.py:78
  38.4 2.0 %copy-start.1 = (s32[128,1]{0,1:T(1,128)S(1)}, s32[128,1]{0,1:T(1,128)}, u32[]{:S(2)}) copy-start(s32[128,1]{0,1:T(1,128)} %param.6) | copy-start | bytes 1540
  38.4 18.6 %collective-permute-start.15 = (bf16[80,1280]{1,0:T(8,128)(2,1)S(1)}, bf16[80,1280]{1,0:T(8,128)(2,1)S(1)}, u32[]{:S(2)}, u32[]{:S(2)}) collective-permute-start(bf16[80,1280]{1,0:T(8,128)(2,1)S(1)} %get-tuple-element.74), channel_id=1, source_target_pairs={{0,1},{1,2},{2,3},{3,0},{4,5},{5,6},{6,7},{7,4},{8,9},{9,10},{10,1... | collective-permute-start | bytes 614408 | tf_op jit(solution)/shard_map/ppermute | solution.py:78
  46.3 11.9 %collective-permute-start.20 = (bf16[128,1280]{1,0:T(8,128)(2,1)S(1)}, bf16[128,1280]{1,0:T(8,128)(2,1)S(1)}, u32[]{:S(2)}, u32[]{:S(2)}) collective-permute-start(bf16[128,1280]{1,0:T(8,128)(2,1)S(1)} %slice.6), channel_id=1, source_target_pairs={{0,16},{8,24},{16,0},{24,8},{1,17},{9,25},{17,1},{25,9},{2,18},{10... | collective-permute-start | bytes 983048 | tf_op jit(solution)/shard_map/ppermute | solution.py:73
  46.9 11.3 %collective-permute-start.21 = (bf16[112,1280]{1,0:T(8,128)(2,1)S(1)}, bf16[112,1280]{1,0:T(8,128)(2,1)S(1)}, u32[]{:S(2)}, u32[]{:S(2)}) collective-permute-start(bf16[112,1280]{1,0:T(8,128)(2,1)S(1)} %slice.7), channel_id=1, source_target_pairs={{0,8},{8,0},{16,24},{24,16},{1,9},{9,1},{17,25},{25,17},{2,10},{10... | collective-permute-start | bytes 860168 | tf_op jit(solution)/shard_map/ppermute | solution.py:73
  56.6 2.1 %collective-permute-start.18 = (bf16[240,1280]{1,0:T(8,128)(2,1)S(1)}, bf16[240,1280]{1,0:T(8,128)(2,1)S(1)}, u32[]{:S(2)}, u32[]{:S(2)}) collective-permute-start(bf16[240,1280]{1,0:T(8,128)(2,1)S(1)} %collective-permute-done.16.refs_0_), channel_id=1, source_target_pairs={{0,4},{4,0},{1,5},{5,1},{2,6},{6,2},{3,7},{7,3},{8,12},{12,8},{9,1... | collective-permute-start | bytes 1843208 | tf_op jit(solution)/shard_map/ppermute | solution.py:73
  56.6 2.9 %collective-permute-start.19 = (bf16[240,1280]{1,0:T(8,128)(2,1)S(1)}, bf16[240,1280]{1,0:T(8,128)(2,1)S(1)}, u32[]{:S(2)}, u32[]{:S(2)}) collective-permute-start(bf16[240,1280]{1,0:T(8,128)(2,1)S(1)} %collective-permute-done.17.refs_1_), channel_id=1, source_target_pairs={{0,4},{4,0},{1,5},{5,1},{2,6},{6,2},{3,7},{7,3},{8,12},{12,8},{9,1... | collective-permute-start | bytes 1843208 | tf_op jit(solution)/shard_map/ppermute | solution.py:73
  58.2 3.7 %collective-permute-start.22 = (bf16[128,1280]{1,0:T(8,128)(2,1)S(1)}, bf16[128,1280]{1,0:T(8,128)(2,1)S(1)}, u32[]{:S(2)}, u32[]{:S(2)}) collective-permute-start(bf16[128,1280]{1,0:T(8,128)(2,1)S(1)} %collective-permute-done.20.refs_0_), channel_id=1, source_target_pairs={{0,4},{4,0},{1,5},{5,1},{2,6},{6,2},{3,7},{7,3},{8,12},{12,8},{9,1... | collective-permute-start | bytes 983048 | tf_op jit(solution)/shard_map/ppermute | solution.py:73
  58.2 3.7 %collective-permute-start.23 = (bf16[112,1280]{1,0:T(8,128)(2,1)S(1)}, bf16[112,1280]{1,0:T(8,128)(2,1)S(1)}, u32[]{:S(2)}, u32[]{:S(2)}) collective-permute-start(bf16[112,1280]{1,0:T(8,128)(2,1)S(1)} %collective-permute-done.21.refs_1_), channel_id=1, source_target_pairs={{0,4},{4,0},{1,5},{5,1},{2,6},{6,2},{3,7},{7,3},{8,12},{12,8},{9,1... | collective-permute-start | bytes 860168 | tf_op jit(solution)/shard_map/ppermute | solution.py:73

commit v6 on v5

--- a/solution.py
+++ b/solution.py
@@ -125,11 +125,12 @@
 
 
 def load_kernel(gate_ref, up_ref, out, sem):
-    units = gate_ref.shape[0]
-    copies = [
-        pltpu.make_async_copy(gate_ref, out.at[:units], sem.at[0]),
-        pltpu.make_async_copy(up_ref, out.at[units:], sem.at[1]),
-    ]
+    core, (units, width) = lax.axis_index("shard"), gate_ref.shape
+    half, copies = width // 2, []
+    for i, ref in enumerate((gate_ref, up_ref)):
+        for j, side in enumerate((core, 1 - core)):
+            to = out.at[i * units : (i + 1) * units, j * half : (j + 1) * half]
+            copies.append(pltpu.make_async_copy(ref.at[:, side_of(side, half)], to, sem.at[i, j]))
     for c in copies:
         c.start()
     for c in copies:
@@ -174,18 +175,14 @@
         out[...] = (kept_ref[at].astype(F32) + got_ref[at].astype(F32)).astype(BF16)
 
 
-def fill(pieces, others, full, sem):
-    core, half = lax.axis_index("shard"), full.shape[1] // 2
-    copies, start = [], 0
-    for piece, other in zip(pieces, others):
-        at = pl.ds(start, piece.shape[0])
-        for ref, side in ((piece, core), (other, 1 - core)):
-            copies.append(pltpu.make_async_copy(ref, full.at[at, side_of(side, half)], sem.at[0]))
-        start += piece.shape[0]
-    for c in copies:
-        c.start()
-    for c in copies:
-        c.wait()
+def joined(refs, columns=slice(None)):
+    return jnp.concatenate([r[:, columns] for r in refs])
+
+
+def activations(pieces, others, rows_ref):
+    half = rows_ref.shape[1] // 2
+    acts = dot(joined(pieces), rows_ref[:, :half], LAST)
+    return acts + dot(joined(others), rows_ref[:, half:], LAST)
 
 
 def source_of(k):
@@ -196,11 +193,9 @@
 def own_kernel(blocks, *refs):
     n = len(blocks)
     pieces, others = refs[:n], refs[n : 2 * n]
-    cotan_ref, rows_ref, full, d_ref, sent_ref, hidden_ref, sem = refs[2 * n :]
-    core, half = lax.axis_index("shard"), full.shape[1] // 2
+    cotan_ref, rows_ref, d_ref, sent_ref, hidden_ref = refs[2 * n :]
     capacity, units = cotan_ref.shape[1:]
-    fill(pieces, others, full, sem)
-    acts = dot(full[...], rows_ref[...], LAST)
+    acts = activations(pieces, others, rows_ref)
     for i, k in enumerate(blocks):
         at = slice(i * capacity, (i + 1) * capacity)
         gate, up = acts[at, :units], acts[at, units:]
@@ -208,21 +203,19 @@
         hidden_ref[source_of(k)] = (gate * sigma * up).astype(BF16)
         d_ref[at, :units] = d_gate
         d_ref[at, units:] = d_up
-    theirs = rows_ref[:, side_of(1 - core, half)]
-    sent_ref[...] = dot(d_ref[...], theirs, MATMUL).astype(BF16)
+    sent_ref[...] = dot(d_ref[...], rows_ref[:, sent_ref.shape[1] :], MATMUL).astype(BF16)
 
 
 def kept_kernel(d_ref, rows_ref, kept_ref):
-    mine = rows_ref[:, side_of(lax.axis_index("shard"), kept_ref.shape[1])]
+    mine = rows_ref[:, : kept_ref.shape[1]]
     kept_ref[...] = dot(d_ref[...], mine, MATMUL).astype(BF16)
 
 
 def part_kernel(plan, n, *refs):
     pieces, others = refs[:n], refs[n : 2 * n]
-    near, far, rows_ref, full, d_ref, sem = refs[2 * n :]
+    near, far, rows_ref, d_ref = refs[2 * n :]
     capacity, units = near.shape[1:]
-    fill(pieces, others, full, sem)
-    acts = dot(full[...], rows_ref[...], LAST)
+    acts = activations(pieces, others, rows_ref)
     for i, (k, group) in enumerate(plan):
         at = slice(i * capacity, (i + 1) * capacity)
         source = source_of(k)
@@ -232,33 +225,42 @@
         d_ref[at, units:] = d_up
 
 
-def grad_kernel(n, *refs):
-    fulls, ds, out = refs[:n], refs[n : 2 * n], refs[2 * n]
-    out[...] = sum(dot(d[...], full[...], FIRST) for d, full in zip(ds, fulls))
-
-
-def last_grad_kernel(scale, n, *refs):
-    fulls, ds = refs[:n], refs[n : 2 * n]
-    earlier, gate_out, up_out, staged, held, sem = refs[2 * n :]
-    units, copies, start = gate_out.shape[0], [], 0
+def hold(ds, held):
+    start = 0
     for d in ds:
         held[start : start + d.shape[0]] = d[...]
         start += d.shape[0]
-    blocks = sem.shape[0]
-    wide = staged.shape[1] // blocks
-    for i in range(blocks):
-        columns = slice(i * wide, (i + 1) * wide)
-        total = dot(held[...], jnp.concatenate([full[:, columns] for full in fulls]), FIRST)
-        staged[:, columns] = ((total + earlier[:, columns]) * scale).astype(BF16)
-        for j, out in enumerate((gate_out, up_out)):
-            copies.append(
-                pltpu.make_async_copy(
-                    staged.at[j * units : (j + 1) * units, columns],
-                    out.at[:, columns],
-                    sem.at[i, j],
+
+
+def grad_kernel(n, *refs):
+    pieces, others = refs[:n], refs[n : 2 * n]
+    *ds, out, held = refs[2 * n :]
+    hold(ds, held)
+    half = out.shape[1] // 2
+    for j, rows in enumerate((pieces, others)):
+        out[:, j * half : (j + 1) * half] = dot(held[...], joined(rows), FIRST)
+
+
+def last_grad_kernel(scale, n, *refs):
+    pieces, others = refs[:n], refs[n : 2 * n]
+    *ds, earlier, gate_out, up_out, staged, held, sem = refs[2 * n :]
+    hold(ds, held)
+    core, units, half = lax.axis_index("shard"), gate_out.shape[0], staged.shape[1] // 2
+    wide, copies = half // 5, []
+    for j, (rows, side) in enumerate(((pieces, core), (others, 1 - core))):
+        for i, (start, stop) in enumerate(((0, 2), (2, 4), (4, 5))):
+            columns = slice(start * wide, stop * wide)
+            at = slice(j * half + start * wide, j * half + stop * wide)
+            total = dot(held[...], joined(rows, columns), FIRST)
+            staged[:, at] = ((total + earlier[:, at]) * scale).astype(BF16)
+            to = pl.ds(pl.multiple_of(side * half + start * wide, 128), (stop - start) * wide)
+            for h, out in enumerate((gate_out, up_out)):
+                copies.append(
+                    pltpu.make_async_copy(
+                        staged.at[h * units : (h + 1) * units, at], out.at[:, to], sem.at[j, i, h]
+                    )
                 )
-            )
-            copies[-1].start()
+                copies[-1].start()
     for c in copies:
         c.wait()
 
@@ -275,32 +277,28 @@
     hidden_width = w_gate.shape[1]
     gate_rows, up_rows, cotan = w_gate[0], w_up[0], d_hidden[0, 0]
     experts = expert_of.reshape(1, -1)
-    sem = [pltpu.SemaphoreType.DMA((1,))]
     piece = like(capacity, half)
 
     def own(pair, rows, others):
         n = len(pair) * capacity
         return call(
             functools.partial(own_kernel, pair),
-            [ANY] * (2 * len(rows)) + [VMEM] * 2,
-            [like(n, width), like(n, 2 * hidden_width)]
-            + [like(n, half)]
-            + [like(len(pair), capacity, hidden_width)],
+            [VMEM] * (2 * len(rows) + 2),
+            [like(n, 2 * hidden_width), like(n, half), like(len(pair), capacity, hidden_width)],
             [*rows, *others, cotan, both_rows],
-            scratch=sem,
             name="own",
         )
 
     def part(plan, pieces, others, near, far):
         n = sum(p.shape[0] for p in pieces)
-        return call(
+        (d,) = call(
             functools.partial(part_kernel, plan, len(pieces)),
-            [ANY] * (2 * len(pieces)) + [VMEM] * 3,
-            [like(n, width), like(n, 2 * hidden_width)],
+            [VMEM] * (2 * len(pieces) + 3),
+            [like(n, 2 * hidden_width)],
             [*pieces, *others, near, far, both_rows],
-            scratch=sem,
             name="part",
         )
+        return d
 
     def add(kept, got):
         return call(sum_kernel, [VMEM] * 2, [piece] * count, [kept, got], name="sum")
@@ -328,7 +326,7 @@
         [HBM] * 2,
         [like(2 * hidden_width, width)],
         after([pltpu.with_memory_space_constraint(x, pltpu.HBM) for x in (gate_rows, up_rows)], c0),
-        scratch=[pltpu.SemaphoreType.DMA((2,))],
+        scratch=[pltpu.SemaphoreType.DMA((2, 2))],
         name="load",
     )
     c0_kept, c0_near_kept = after([c0, c0_near], both_rows)
@@ -341,7 +339,7 @@
     o1, o2, o3 = swap(z1), swap(z2), swap(z3)
     c123 = jnp.concatenate([z1, z2, z3])
     o1, o2, o3 = after([o1, o2, o3], c0_far, cotan_far)
-    full_a, d_a, sent, hidden = own((0, 1, 2, 3), [c0, z1, z2, z3], [other, o1, o2, o3])
+    d_a, sent, hidden = own((0, 1, 2, 3), [c0, z1, z2, z3], [other, o1, o2, o3])
     (kept,) = call(
         kept_kernel, [VMEM] * 2, [like(count * capacity, half)], [d_a, both_rows], name="kept"
     )
@@ -352,12 +350,13 @@
     r1, r2, r3 = turned(r1, "exp", -1), turned(r2, "exp", -2), turned(r3, "exp", -3)
 
     plan = ((0, 1), (0, 2), (0, 3))
-    full_c, d_c = part(plan, [c0_near, c0_far], c0_others, cotan_near, cotan_far)
+    d_c = part(plan, [c0_near, c0_far], c0_others, cotan_near, cotan_far)
     (total,) = call(
-        functools.partial(grad_kernel, 2),
-        [VMEM] * 4,
+        functools.partial(grad_kernel, 6),
+        [VMEM] * 14,
         [like(2 * hidden_width, width, dtype=F32)],
-        [full_a, full_c, d_a, d_c],
+        [c0, z1, z2, z3, c0_near, c0_far, other, o1, o2, o3, *c0_others, d_a, d_c],
+        scratch=[pltpu.VMEM((d_a.shape[0] + d_c.shape[0], 2 * hidden_width), BF16)],
         name="grads_near",
         limit=32,
     )
@@ -382,22 +381,20 @@
     (c123_x,), (c123_y,) = after([c123_x], r1), after([c123_y], r2)
     far_sent = after(far_sent, d_tokens)
     plan = tuple((k, group) for group in (1, 2) for k in (1, 2, 3))
-    full_d, d_d = part(
-        plan, [c123_x, c123_y], [swap(c123_x), swap(c123_y)], cotan_near, cotan_far
-    )
+    pieces, others = [c123_x, c123_y], [swap(c123_x), swap(c123_y)]
+    d_d = part(plan, pieces, others, cotan_near, cotan_far)
     plan = tuple((k, 3) for k in (1, 2, 3))
-    full_e, d_e = part(
-        plan, far_sent, after([swap(f) for f in far_sent], d_d), cotan_near, cotan_far
-    )
+    far_others = after([swap(f) for f in far_sent], d_d)
+    d_e = part(plan, far_sent, far_others, cotan_near, cotan_far)
     grad_gate, grad_up = call(
-        functools.partial(last_grad_kernel, 1.0 / lax.axis_size("rep"), 2),
-        [VMEM] * 5,
+        functools.partial(last_grad_kernel, 1.0 / lax.axis_size("rep"), 4),
+        [VMEM] * 11,
         [like(hidden_width, width)] * 2,
-        [full_d, full_e, d_d, d_e, total],
+        [*pieces, *far_sent, *others, *far_others, d_d, d_e, total],
         scratch=[
             pltpu.VMEM((2 * hidden_width, width), BF16),
             pltpu.VMEM((d_d.shape[0] + d_e.shape[0], 2 * hidden_width), BF16),
-            pltpu.SemaphoreType.DMA((5, 2)),
+            pltpu.SemaphoreType.DMA((2, 3, 2)),
         ],
         name="grads",
         limit=32,

time: 67.9 us -> 65.5 us (0.965)
  the two profiles are of different devices: /device:TPU:0 before, /device:TPU:9 now
where the time goes in v6:
time: 65.5 us; the launch traced here: 65.3 us
  waiting for transfers between devices  22.8 us (35%)
  Pallas kernels  21.8 us (33%)
  starting transfers between devices  19.6 us (30%)
  between operations  0.98 us (1%)
    pallas_call x12, Pallas kernels, call(): pl.pallas_call(kernel, in_specs=ins, out_specs=[out_spec] * len(outs), ou...  21.8 us
    ppermute x6, waiting for transfers between devices, turned(): return lax.ppermute(x, axis, [(i, (i + step) % size) for i in range(size)])  14.9 us
    ppermute x18, starting transfers between devices, across(): return lax.ppermute(x, axis, [(i, i ^ bit) for i in range(size)])  12.9 us
    ppermute x18, waiting for transfers between devices, across(): return lax.ppermute(x, axis, [(i, i ^ bit) for i in range(size)])  7.91 us
    ppermute x6, starting transfers between devices, turned(): return lax.ppermute(x, axis, [(i, (i + step) % size) for i in range(size)])  6.64 us
  transfers between devices with their start and end apart: 24, of which 9 were waited for; matrix products, arithmetic and copies ran while one was open for 0% of the time, Pallas kernels for 17%

profile of v6, /device:TPU:9, one launch (start us, length us, event | category | flops | bytes accessed | tf_op | source)
XLA Modules:
  0.0 65.3 jit_solution(3874636508285593007)
XLA Ops:
  0.6 1.7 %pack.1 = (bf16[80,1280]{1,0:T(8,128)(2,1)S(1)}, bf16[80,1280]{1,0:T(8,128)(2,1)S(1)}, bf16[80,1280]{1,0:T(8,128)(2,1)S(1)}, bf16[80,1280]{1,0:T(8,128)(2,1)S(1)}, bf16[80,1280]{1,0:T(8,128)(2,1)S(1)}) custom-call(s32[1,128]{1,0:T(1,128)} %bitcast.13, bf16[128,2560]{1,0:T(8,128)(2,1)} %tokens_hbm.1), custom_call_target="tpu_custom_call" | custom-call | flops 1 | bytes 1 | tf_op jit(solution)/shard_map/pack/pallas_call | solution.py:87
  2.3 1.3 %collective-permute-start.3 = (bf16[80,1280]{1,0:T(8,128)(2,1)S(1)}, bf16[80,1280]{1,0:T(8,128)(2,1)S(1)}, u32[]{:S(2)}, u32[]{:S(2)}) collective-permute-start(bf16[80,1280]{1,0:T(8,128)(2,1)S(1)} %get-tuple-element.47.refs_0_), channel_id=1, source_target_pairs={{0,8},{8,0},{16,24},{24,16},{1,9},{9,1},{17,25},{25,17},{2,10},{10... | collective-permute-start | bytes 614408 | tf_op jit(solution)/shard_map/ppermute | solution.py:73
  3.6 1.2 %collective-permute-start.4 = (bf16[4,80,384]{2,1,0:T(8,128)(2,1)}, bf16[4,80,384]{2,1,0:T(8,128)(2,1)S(1)}, u32[]{:S(2)}, u32[]{:S(2)}) collective-permute-start(bf16[4,80,384]{2,1,0:T(8,128)(2,1)} %bitcast.10), channel_id=1, source_target_pairs={{0,16},{8,24},{16,0},{24,8},{1,17},{9,25},{17,1},{25,9},{2,18},{10... | collective-permute-start | bytes 737288 | tf_op jit(solution)/shard_map/ppermute | solution.py:73
  4.8 1.3 %collective-permute-start = (bf16[80,1280]{1,0:T(8,128)(2,1)S(1)}, bf16[80,1280]{1,0:T(8,128)(2,1)S(1)}, u32[]{:S(2)}, u32[]{:S(2)}) collective-permute-start(bf16[80,1280]{1,0:T(8,128)(2,1)S(1)} %get-tuple-element.42), channel_id=1, source_target_pairs={{0,1},{1,2},{2,3},{3,0},{4,5},{5,6},{6,7},{7,4},{8,9},{9,10},{10,1... | collective-permute-start | bytes 614408 | tf_op jit(solution)/shard_map/ppermute | solution.py:78
  6.1 1.0 %collective-permute-start.1 = (bf16[80,1280]{1,0:T(8,128)(2,1)S(1)}, bf16[80,1280]{1,0:T(8,128)(2,1)S(1)}, u32[]{:S(2)}, u32[]{:S(2)}) collective-permute-start(bf16[80,1280]{1,0:T(8,128)(2,1)S(1)} %get-tuple-element.43), channel_id=1, source_target_pairs={{0,2},{1,3},{2,0},{3,1},{4,6},{5,7},{6,4},{7,5},{8,10},{9,11},{10,... | collective-permute-start | bytes 614408 | tf_op jit(solution)/shard_map/ppermute | solution.py:78
  7.1 1.5 %collective-permute-start.2 = (bf16[80,1280]{1,0:T(8,128)(2,1)S(1)}, bf16[80,1280]{1,0:T(8,128)(2,1)S(1)}, u32[]{:S(2)}, u32[]{:S(2)}) collective-permute-start(bf16[80,1280]{1,0:T(8,128)(2,1)S(1)} %get-tuple-element.44), channel_id=1, source_target_pairs={{0,3},{1,0},{2,1},{3,2},{4,7},{5,4},{6,5},{7,6},{8,11},{9,8},{10,9... | collective-permute-start | bytes 614408 | tf_op jit(solution)/shard_map/ppermute | solution.py:78
  8.6 2.2 %load.1.refs_9_.refs_6_.rows_ref = bf16[768,2560]{1,0:T(8,128)(2,1)S(1)} custom-call(bf16[384,2560]{1,0:T(8,128)(2,1)} %bitcast.15, bf16[384,2560]{1,0:T(8,128)(2,1)} %bitcast.16), custom_call_target="tpu_custom_call" | custom-call | flops 1 | bytes 1 | tf_op jit(solution)/shard_map/load/pallas_call | solution.py:87
  11.2 0.8 %collective-permute-start.8 = (bf16[160,1280]{1,0:T(8,128)(2,1)S(1)}, bf16[160,1280]{1,0:T(8,128)(2,1)S(1)}, u32[]{:S(2)}, u32[]{:S(2)}) collective-permute-start(bf16[160,1280]{1,0:T(8,128)(2,1)S(1)} %constant_dynamic-update-slice_fusion), channel_id=1, source_target_pairs={{0,16},{8,24},{16,0},{24,8},{1,17},{9,25},{17,1},{25,9},{2,18},{10... | collective-permute-start | bytes 1228808 | tf_op jit(solution)/shard_map/ppermute | solution.py:73
  12.0 10.4 %collective-permute-done.1.refs_2_ = bf16[80,1280]{1,0:T(8,128)(2,1)S(1)} collective-permute-done((bf16[80,1280]{1,0:T(8,128)(2,1)S(1)}, bf16[80,1280]{1,0:T(8,128)(2,1)S(1)}, u32[]{:S(2)}, u32[]{:S(2)}) %collective-permute-start.1) | collective-permute-done | bytes 204832 | tf_op jit(solution)/shard_map/ppermute | solution.py:78
  22.4 3.4 %collective-permute-done.2.refs_3_ = bf16[80,1280]{1,0:T(8,128)(2,1)S(1)} collective-permute-done((bf16[80,1280]{1,0:T(8,128)(2,1)S(1)}, bf16[80,1280]{1,0:T(8,128)(2,1)S(1)}, u32[]{:S(2)}, u32[]{:S(2)}) %collective-permute-start.2) | collective-permute-done | bytes 204832 | tf_op jit(solution)/shard_map/ppermute | solution.py:78
  25.8 0.5 collective-permute-start.5
  26.3 0.5 collective-permute-start.7
  26.8 0.6 collective-permute-done.5.refs_5_.refs_7_
  28.1 3.0 %own.1 = (bf16[320,768]{1,0:T(8,128)(2,1)S(1)}, bf16[320,1280]{1,0:T(8,128)(2,1)S(1)}, bf16[4,80,384]{2,1,0:T(8,128)(2,1)}) custom-call(bf16[80,1280]{1,0:T(8,128)(2,1)S(1)} %get-tuple-element.47.refs_0_, bf16[80,1280]{1,0:T(8,128)(2,1)S(1)} %collective-permute-done.refs_1_, bf16[80,1280]{1,0:T(8,128)(2,1)S(1)} %collective-permute-done.1.refs_2_, ...), custom_call_target="tpu_custom_call" | custom-call | flops 1 | bytes 1 | tf_op jit(solution)/shard_map/own/pallas_call | solution.py:87
  32.1 0.8 %collective-permute-start.11 = (bf16[160,1280]{1,0:T(8,128)(2,1)S(1)}, bf16[160,1280]{1,0:T(8,128)(2,1)S(1)}, u32[]{:S(2)}, u32[]{:S(2)}) collective-permute-start(bf16[160,1280]{1,0:T(8,128)(2,1)S(1)} %collective-permute-done.8.refs_1_.refs_5_), channel_id=1, source_target_pairs={{0,4},{4,0},{1,5},{5,1},{2,6},{6,2},{3,7},{7,3},{8,12},{12,8},{9,1... | collective-permute-start | bytes 1228808 | tf_op jit(solution)/shard_map/ppermute | solution.py:73
  32.8 0.8 %kept.1.kept_ref = bf16[320,1280]{1,0:T(8,128)(2,1)S(1)} custom-call(bf16[320,768]{1,0:T(8,128)(2,1)S(1)} %get-tuple-element.62.d_ref.refs_12_, bf16[768,2560]{1,0:T(8,128)(2,1)S(1)} %load.1.refs_9_.refs_6_.rows_ref), custom_call_target="tpu_custom_call" | custom-call | flops 1 | bytes 1 | tf_op jit(solution)/shard_map/kept/pallas_call | solution.py:87
  33.9 1.4 %collective-permute-start.14 = (bf16[80,1280]{1,0:T(8,128)(2,1)S(1)}, bf16[80,1280]{1,0:T(8,128)(2,1)S(1)}, u32[]{:S(2)}, u32[]{:S(2)}) collective-permute-start(bf16[80,1280]{1,0:T(8,128)(2,1)S(1)} %get-tuple-element.65), channel_id=1, source_target_pairs={{0,2},{1,3},{2,0},{3,1},{4,6},{5,7},{6,4},{7,5},{8,10},{9,11},{10,... | collective-permute-start | bytes 614408 | tf_op jit(solution)/shard_map/ppermute | solution.py:78
  35.3 1.5 %collective-permute-start.15 = (bf16[80,1280]{1,0:T(8,128)(2,1)S(1)}, bf16[80,1280]{1,0:T(8,128)(2,1)S(1)}, u32[]{:S(2)}, u32[]{:S(2)}) collective-permute-start(bf16[80,1280]{1,0:T(8,128)(2,1)S(1)} %get-tuple-element.66), channel_id=1, source_target_pairs={{0,1},{1,2},{2,3},{3,0},{4,5},{5,6},{6,7},{7,4},{8,9},{9,10},{10,1... | collective-permute-start | bytes 614408 | tf_op jit(solution)/shard_map/ppermute | solution.py:78
  36.8 1.3 %part.3.refs_13_ = bf16[240,768]{1,0:T(8,128)(2,1)S(1)} custom-call(bf16[80,1280]{1,0:T(8,128)(2,1)S(1)} %collective-permute-done.3.refs_0_.refs_4_, bf16[160,1280]{1,0:T(8,128)(2,1)S(1)} %collective-permute-done.8.refs_1_.refs_5_, bf16[80,1280]{1,0:T(8,128)(2,1)S(1)} %collective-permute-done.10.refs_2_.refs_10_, ...), custom_call_target="tpu_custom_call" | custom-call | flops 1 | bytes 1 | tf_op jit(solution)/shard_map/part/pallas_call | solution.py:87
  38.3 3.3 %grads_near.1.refs_10_ = f32[768,2560]{1,0:T(8,128)S(1)} custom-call(bf16[80,1280]{1,0:T(8,128)(2,1)S(1)} %get-tuple-element.47.refs_0_, bf16[80,1280]{1,0:T(8,128)(2,1)S(1)} %collective-permute-done.refs_1_, bf16[80,1280]{1,0:T(8,128)(2,1)S(1)} %collective-permute-done.1.refs_2_, bf16[80,1280]{1,0:T(8,128)(2,1)S(1)} %collective-permute-done.2.refs_3_, ...), custom_call_target="tpu_custom_call" | custom-call | flops 1 | bytes 1 | tf_op jit(solution)/shard_map/grads_near/pallas_call | solution.py:87
  41.5 5.3 %collective-permute-done.16.refs_0_ = bf16[240,1280]{1,0:T(8,128)(2,1)S(1)} collective-permute-done((bf16[240,1280]{1,0:T(8,128)(2,1)S(1)}, bf16[240,1280]{1,0:T(8,128)(2,1)S(1)}, u32[]{:S(2)}, u32[]{:S(2)}) %collective-permute-start.16) | collective-permute-done | bytes 614432 | tf_op jit(solution)/shard_map/ppermute | solution.py:73
  47.2 1.2 %collective-permute-start.19 = (bf16[112,1280]{1,0:T(8,128)(2,1)S(1)}, bf16[112,1280]{1,0:T(8,128)(2,1)S(1)}, u32[]{:S(2)}, u32[]{:S(2)}) collective-permute-start(bf16[112,1280]{1,0:T(8,128)(2,1)S(1)} %slice.7), channel_id=1, source_target_pairs={{0,8},{8,0},{16,24},{24,16},{1,9},{9,1},{17,25},{25,17},{2,10},{10... | collective-permute-start | bytes 860168 | tf_op jit(solution)/shard_map/ppermute | solution.py:73
  48.4 1.9 %collective-permute-start.21 = (bf16[240,1280]{1,0:T(8,128)(2,1)S(1)}, bf16[240,1280]{1,0:T(8,128)(2,1)S(1)}, u32[]{:S(2)}, u32[]{:S(2)}) collective-permute-start(bf16[240,1280]{1,0:T(8,128)(2,1)S(1)} %collective-permute-done.17.refs_1_), channel_id=1, source_target_pairs={{0,4},{4,0},{1,5},{5,1},{2,6},{6,2},{3,7},{7,3},{8,12},{12,8},{9,1... | collective-permute-start | bytes 1843208 | tf_op jit(solution)/shard_map/ppermute | solution.py:73
  50.3 1.1 %collective-permute-done.13.refs_1_ = bf16[80,1280]{1,0:T(8,128)(2,1)S(1)} collective-permute-done((bf16[80,1280]{1,0:T(8,128)(2,1)S(1)}, bf16[80,1280]{1,0:T(8,128)(2,1)S(1)}, u32[]{:S(2)}, u32[]{:S(2)}) %collective-permute-start.13) | collective-permute-done | bytes 204832 | tf_op jit(solution)/shard_map/ppermute | solution.py:78
  51.4 1.0 %collective-permute-start.20 = (bf16[240,1280]{1,0:T(8,128)(2,1)S(1)}, bf16[240,1280]{1,0:T(8,128)(2,1)S(1)}, u32[]{:S(2)}, u32[]{:S(2)}) collective-permute-start(bf16[240,1280]{1,0:T(8,128)(2,1)S(1)} %collective-permute-done.16.refs_0_), channel_id=1, source_target_pairs={{0,4},{4,0},{1,5},{5,1},{2,6},{6,2},{3,7},{7,3},{8,12},{12,8},{9,1... | collective-permute-start | bytes 1843208 | tf_op jit(solution)/shard_map/ppermute | solution.py:73
  52.4 1.1 %unpack.1 = bf16[128,1280]{1,0:T(8,128)(2,1)} custom-call(bf16[128,320]{1,0:T(8,128)(2,1)S(1)} %place.1.placing_ref, bf16[80,1280]{1,0:T(8,128)(2,1)S(1)} %get-tuple-element.63.refs_0_, bf16[80,1280]{1,0:T(8,128)(2,1)S(1)} %collective-permute-done.13.refs_1_, bf16[80,1280]{1,0:T(8,128)(2,1)S(1)} %collective-permute-done.14.refs_2_, ...), custom_call_target="tpu_custom_call" | custom-call | flops 6000000000 | bytes 1 | tf_op jit(solution)/shard_map/unpack/pallas_call | solution.py:87
  53.5 0.5 collective-permute-done.19.refs_1_.refs_3_
  54.0 0.9 %collective-permute-done.18.refs_0_.refs_2_ = bf16[128,1280]{1,0:T(8,128)(2,1)S(1)} collective-permute-done((bf16[128,1280]{1,0:T(8,128)(2,1)S(1)}, bf16[128,1280]{1,0:T(8,128)(2,1)S(1)}, u32[]{:S(2)}, u32[]{:S(2)}) %collective-permute-start.18) | collective-permute-done | bytes 327712 | tf_op jit(solution)/shard_map/ppermute | solution.py:73
  54.8 2.2 %collective-permute-start.22 = (bf16[128,1280]{1,0:T(8,128)(2,1)S(1)}, bf16[128,1280]{1,0:T(8,128)(2,1)S(1)}, u32[]{:S(2)}, u32[]{:S(2)}) collective-permute-start(bf16[128,1280]{1,0:T(8,128)(2,1)S(1)} %collective-permute-done.18.refs_0_.refs_2_), channel_id=1, source_target_pairs={{0,4},{4,0},{1,5},{5,1},{2,6},{6,2},{3,7},{7,3},{8,12},{12,8},{9,1... | collective-permute-start | bytes 983048 | tf_op jit(solution)/shard_map/ppermute | solution.py:73
  57.1 2.2 %part.4.refs_8_ = bf16[480,768]{1,0:T(8,128)(2,1)S(1)} custom-call(bf16[240,1280]{1,0:T(8,128)(2,1)S(1)} %collective-permute-done.16.refs_0_, bf16[240,1280]{1,0:T(8,128)(2,1)S(1)} %collective-permute-done.17.refs_1_, bf16[240,1280]{1,0:T(8,128)(2,1)S(1)} %collective-permute-done.20.refs_2_.refs_4_, ...), custom_call_target="tpu_custom_call" | custom-call | flops 1 | bytes 1 | tf_op jit(solution)/shard_map/part/pallas_call | solution.py:87
  59.3 1.3 %part.5.refs_9_ = bf16[240,768]{1,0:T(8,128)(2,1)S(1)} custom-call(bf16[128,1280]{1,0:T(8,128)(2,1)S(1)} %collective-permute-done.18.refs_0_.refs_2_, bf16[112,1280]{1,0:T(8,128)(2,1)S(1)} %collective-permute-done.19.refs_1_.refs_3_, bf16[128,1280]{1,0:T(8,128)(2,1)S(1)} %collective-permute-done.22.refs_2_.refs_6_, ...), custom_call_target="tpu_custom_call" | custom-call | flops 1 | bytes 1 | tf_op jit(solution)/shard_map/part/pallas_call | solution.py:87
  60.6 4.6 %grads.1 = (bf16[384,2560]{1,0:T(8,128)(2,1)}, bf16[384,2560]{1,0:T(8,128)(2,1)}) custom-call(bf16[240,1280]{1,0:T(8,128)(2,1)S(1)} %collective-permute-done.16.refs_0_, bf16[240,1280]{1,0:T(8,128)(2,1)S(1)} %collective-permute-done.17.refs_1_, bf16[128,1280]{1,0:T(8,128)(2,1)S(1)} %collective-permute-done.18.refs_0_.refs_2_, ...), custom_call_target="tpu_custom_call" | custom-call | flops 1 | bytes 1 | tf_op jit(solution)/shard_map/grads/pallas_call | solution.py:87
  (38 shorter events, 2.8 us)
Async XLA Ops:
  2.3 8.5 %collective-permute-start.3 = (bf16[80,1280]{1,0:T(8,128)(2,1)S(1)}, bf16[80,1280]{1,0:T(8,128)(2,1)S(1)}, u32[]{:S(2)}, u32[]{:S(2)}) collective-permute-start(bf16[80,1280]{1,0:T(8,128)(2,1)S(1)} %get-tuple-element.47.refs_0_), channel_id=1, source_target_pairs={{0,8},{8,0},{16,24},{24,16},{1,9},{9,1},{17,25},{25,17},{2,10},{10... | collective-permute-start | bytes 614408 | tf_op jit(solution)/shard_map/ppermute | solution.py:73
  3.6 7.2 %collective-permute-start.4 = (bf16[4,80,384]{2,1,0:T(8,128)(2,1)}, bf16[4,80,384]{2,1,0:T(8,128)(2,1)S(1)}, u32[]{:S(2)}, u32[]{:S(2)}) collective-permute-start(bf16[4,80,384]{2,1,0:T(8,128)(2,1)} %bitcast.10), channel_id=1, source_target_pairs={{0,16},{8,24},{16,0},{24,8},{1,17},{9,25},{17,1},{25,9},{2,18},{10... | collective-permute-start | bytes 737288 | tf_op jit(solution)/shard_map/ppermute | solution.py:73
  4.8 7.2 %collective-permute-start = (bf16[80,1280]{1,0:T(8,128)(2,1)S(1)}, bf16[80,1280]{1,0:T(8,128)(2,1)S(1)}, u32[]{:S(2)}, u32[]{:S(2)}) collective-permute-start(bf16[80,1280]{1,0:T(8,128)(2,1)S(1)} %get-tuple-element.42), channel_id=1, source_target_pairs={{0,1},{1,2},{2,3},{3,0},{4,5},{5,6},{6,7},{7,4},{8,9},{9,10},{10,1... | collective-permute-start | bytes 614408 | tf_op jit(solution)/shard_map/ppermute | solution.py:78
  6.1 16.3 %collective-permute-start.1 = (bf16[80,1280]{1,0:T(8,128)(2,1)S(1)}, bf16[80,1280]{1,0:T(8,128)(2,1)S(1)}, u32[]{:S(2)}, u32[]{:S(2)}) collective-permute-start(bf16[80,1280]{1,0:T(8,128)(2,1)S(1)} %get-tuple-element.43), channel_id=1, source_target_pairs={{0,2},{1,3},{2,0},{3,1},{4,6},{5,7},{6,4},{7,5},{8,10},{9,11},{10,... | collective-permute-start | bytes 614408 | tf_op jit(solution)/shard_map/ppermute | solution.py:78
  7.1 18.7 %collective-permute-start.2 = (bf16[80,1280]{1,0:T(8,128)(2,1)S(1)}, bf16[80,1280]{1,0:T(8,128)(2,1)S(1)}, u32[]{:S(2)}, u32[]{:S(2)}) collective-permute-start(bf16[80,1280]{1,0:T(8,128)(2,1)S(1)} %get-tuple-element.44), channel_id=1, source_target_pairs={{0,3},{1,0},{2,1},{3,2},{4,7},{5,4},{6,5},{7,6},{8,11},{9,8},{10,9... | collective-permute-start | bytes 614408 | tf_op jit(solution)/shard_map/ppermute | solution.py:78
  8.6 2.2 %copy-start = (bf16[1,1,4,80,384]{4,3,2,1,0:T(8,128)(2,1)S(1)}, bf16[1,1,4,80,384]{4,3,2,1,0:T(8,128)(2,1)}, u32[]{:S(2)}) copy-start(bf16[1,1,4,80,384]{4,3,2,1,0:T(8,128)(2,1)} %param.9) | copy-start | bytes 737284
  10.9 17.2 %collective-permute-start.9 = (bf16[2,4,80,384]{3,2,1,0:T(8,128)(2,1)S(1)}, bf16[2,4,80,384]{3,2,1,0:T(8,128)(2,1)S(1)}, u32[]{:S(2)}, u32[]{:S(2)}) collective-permute-start(bf16[2,4,80,384]{3,2,1,0:T(8,128)(2,1)S(1)} %pad_maximum_fusion.1), channel_id=1, source_target_pairs={{0,8},{8,0},{16,24},{24,16},{1,9},{9,1},{17,25},{25,17},{2,10},{10... | collective-permute-start | bytes 1474568 | tf_op jit(solution)/shard_map/ppermute | solution.py:73
  11.2 16.9 %collective-permute-start.8 = (bf16[160,1280]{1,0:T(8,128)(2,1)S(1)}, bf16[160,1280]{1,0:T(8,128)(2,1)S(1)}, u32[]{:S(2)}, u32[]{:S(2)}) collective-permute-start(bf16[160,1280]{1,0:T(8,128)(2,1)S(1)} %constant_dynamic-update-slice_fusion), channel_id=1, source_target_pairs={{0,16},{8,24},{16,0},{24,8},{1,17},{9,25},{17,1},{25,9},{2,18},{10... | collective-permute-start | bytes 1228808 | tf_op jit(solution)/shard_map/ppermute | solution.py:73
  25.8 1.6 %collective-permute-start.5 = (bf16[80,1280]{1,0:T(8,128)(2,1)S(1)}, bf16[80,1280]{1,0:T(8,128)(2,1)S(1)}, u32[]{:S(2)}, u32[]{:S(2)}) collective-permute-start(bf16[80,1280]{1,0:T(8,128)(2,1)S(1)} %collective-permute-done.refs_1_), channel_id=1, source_target_pairs={{0,4},{4,0},{1,5},{5,1},{2,6},{6,2},{3,7},{7,3},{8,12},{12,8},{9,1... | collective-permute-start | bytes 614408 | tf_op jit(solution)/shard_map/ppermute | solution.py:73
  26.3 1.5 %collective-permute-start.6 = (bf16[80,1280]{1,0:T(8,128)(2,1)S(1)}, bf16[80,1280]{1,0:T(8,128)(2,1)S(1)}, u32[]{:S(2)}, u32[]{:S(2)}) collective-permute-start(bf16[80,1280]{1,0:T(8,128)(2,1)S(1)} %collective-permute-done.1.refs_2_), channel_id=1, source_target_pairs={{0,4},{4,0},{1,5},{5,1},{2,6},{6,2},{3,7},{7,3},{8,12},{12,8},{9,1... | collective-permute-start | bytes 614408 | tf_op jit(solution)/shard_map/ppermute | solution.py:73
  26.3 1.7 %collective-permute-start.7 = (bf16[80,1280]{1,0:T(8,128)(2,1)S(1)}, bf16[80,1280]{1,0:T(8,128)(2,1)S(1)}, u32[]{:S(2)}, u32[]{:S(2)}) collective-permute-start(bf16[80,1280]{1,0:T(8,128)(2,1)S(1)} %collective-permute-done.2.refs_3_), channel_id=1, source_target_pairs={{0,4},{4,0},{1,5},{5,1},{2,6},{6,2},{3,7},{7,3},{8,12},{12,8},{9,1... | collective-permute-start | bytes 614408 | tf_op jit(solution)/shard_map/ppermute | solution.py:73
  31.1 2.5 %collective-permute-start.12 = (bf16[320,1280]{1,0:T(8,128)(2,1)S(1)}, bf16[320,1280]{1,0:T(8,128)(2,1)S(1)}, u32[]{:S(2)}, u32[]{:S(2)}) collective-permute-start(bf16[320,1280]{1,0:T(8,128)(2,1)S(1)} %get-tuple-element.58), channel_id=1, source_target_pairs={{0,4},{4,0},{1,5},{5,1},{2,6},{6,2},{3,7},{7,3},{8,12},{12,8},{9,1... | collective-permute-start | bytes 2457608 | tf_op jit(solution)/shard_map/ppermute | solution.py:73
  31.5 15.3 %collective-permute-start.16 = (bf16[240,1280]{1,0:T(8,128)(2,1)S(1)}, bf16[240,1280]{1,0:T(8,128)(2,1)S(1)}, u32[]{:S(2)}, u32[]{:S(2)}) collective-permute-start(bf16[240,1280]{1,0:T(8,128)(2,1)S(1)} %pad_maximum_fusion), channel_id=1, source_target_pairs={{0,8},{8,0},{16,24},{24,16},{1,9},{9,1},{17,25},{25,17},{2,10},{10... | collective-permute-start | bytes 1843208 | tf_op jit(solution)/shard_map/ppermute | solution.py:73
  31.8 15.0 %collective-permute-start.17 = (bf16[240,1280]{1,0:T(8,128)(2,1)S(1)}, bf16[240,1280]{1,0:T(8,128)(2,1)S(1)}, u32[]{:S(2)}, u32[]{:S(2)}) collective-permute-start(bf16[240,1280]{1,0:T(8,128)(2,1)S(1)} %pad_maximum_fusion), channel_id=1, source_target_pairs={{0,16},{8,24},{16,0},{24,8},{1,17},{9,25},{17,1},{25,9},{2,18},{10... | collective-permute-start | bytes 1843208 | tf_op jit(solution)/shard_map/ppermute | solution.py:73
  32.1 3.2 %collective-permute-start.11 = (bf16[160,1280]{1,0:T(8,128)(2,1)S(1)}, bf16[160,1280]{1,0:T(8,128)(2,1)S(1)}, u32[]{:S(2)}, u32[]{:S(2)}) collective-permute-start(bf16[160,1280]{1,0:T(8,128)(2,1)S(1)} %collective-permute-done.8.refs_1_.refs_5_), channel_id=1, source_target_pairs={{0,4},{4,0},{1,5},{5,1},{2,6},{6,2},{3,7},{7,3},{8,12},{12,8},{9,1... | collective-permute-start | bytes 1228808 | tf_op jit(solution)/shard_map/ppermute | solution.py:73
  32.8 2.4 %collective-permute-start.10 = (bf16[80,1280]{1,0:T(8,128)(2,1)S(1)}, bf16[80,1280]{1,0:T(8,128)(2,1)S(1)}, u32[]{:S(2)}, u32[]{:S(2)}) collective-permute-start(bf16[80,1280]{1,0:T(8,128)(2,1)S(1)} %collective-permute-done.3.refs_0_.refs_4_), channel_id=1, source_target_pairs={{0,4},{4,0},{1,5},{5,1},{2,6},{6,2},{3,7},{7,3},{8,12},{12,8},{9,1... | collective-permute-start | bytes 614408 | tf_op jit(solution)/shard_map/ppermute | solution.py:73
  33.9 14.5 %collective-permute-start.14 = (bf16[80,1280]{1,0:T(8,128)(2,1)S(1)}, bf16[80,1280]{1,0:T(8,128)(2,1)S(1)}, u32[]{:S(2)}, u32[]{:S(2)}) collective-permute-start(bf16[80,1280]{1,0:T(8,128)(2,1)S(1)} %get-tuple-element.65), channel_id=1, source_target_pairs={{0,2},{1,3},{2,0},{3,1},{4,6},{5,7},{6,4},{7,5},{8,10},{9,11},{10,... | collective-permute-start | bytes 614408 | tf_op jit(solution)/shard_map/ppermute | solution.py:78
  35.3 16.1 %collective-permute-start.13 = (bf16[80,1280]{1,0:T(8,128)(2,1)S(1)}, bf16[80,1280]{1,0:T(8,128)(2,1)S(1)}, u32[]{:S(2)}, u32[]{:S(2)}) collective-permute-start(bf16[80,1280]{1,0:T(8,128)(2,1)S(1)} %get-tuple-element.64), channel_id=1, source_target_pairs={{0,3},{1,0},{2,1},{3,2},{4,7},{5,4},{6,5},{7,6},{8,11},{9,8},{10,9... | collective-permute-start | bytes 614408 | tf_op jit(solution)/shard_map/ppermute | solution.py:78
  35.3 2.7 %copy-start.1 = (s32[128,1]{0,1:T(1,128)S(1)}, s32[128,1]{0,1:T(1,128)}, u32[]{:S(2)}) copy-start(s32[128,1]{0,1:T(1,128)} %param.6) | copy-start | bytes 1540
  35.3 17.1 %collective-permute-start.15 = (bf16[80,1280]{1,0:T(8,128)(2,1)S(1)}, bf16[80,1280]{1,0:T(8,128)(2,1)S(1)}, u32[]{:S(2)}, u32[]{:S(2)}) collective-permute-start(bf16[80,1280]{1,0:T(8,128)(2,1)S(1)} %get-tuple-element.66), channel_id=1, source_target_pairs={{0,1},{1,2},{2,3},{3,0},{4,5},{5,6},{6,7},{7,4},{8,9},{9,10},{10,1... | collective-permute-start | bytes 614408 | tf_op jit(solution)/shard_map/ppermute | solution.py:78
  46.9 8.0 %collective-permute-start.18 = (bf16[128,1280]{1,0:T(8,128)(2,1)S(1)}, bf16[128,1280]{1,0:T(8,128)(2,1)S(1)}, u32[]{:S(2)}, u32[]{:S(2)}) collective-permute-start(bf16[128,1280]{1,0:T(8,128)(2,1)S(1)} %slice.6), channel_id=1, source_target_pairs={{0,16},{8,24},{16,0},{24,8},{1,17},{9,25},{17,1},{25,9},{2,18},{10... | collective-permute-start | bytes 983048 | tf_op jit(solution)/shard_map/ppermute | solution.py:73
  47.2 6.8 %collective-permute-start.19 = (bf16[112,1280]{1,0:T(8,128)(2,1)S(1)}, bf16[112,1280]{1,0:T(8,128)(2,1)S(1)}, u32[]{:S(2)}, u32[]{:S(2)}) collective-permute-start(bf16[112,1280]{1,0:T(8,128)(2,1)S(1)} %slice.7), channel_id=1, source_target_pairs={{0,8},{8,0},{16,24},{24,16},{1,9},{9,1},{17,25},{25,17},{2,10},{10... | collective-permute-start | bytes 860168 | tf_op jit(solution)/shard_map/ppermute | solution.py:73
  48.4 8.7 %collective-permute-start.21 = (bf16[240,1280]{1,0:T(8,128)(2,1)S(1)}, bf16[240,1280]{1,0:T(8,128)(2,1)S(1)}, u32[]{:S(2)}, u32[]{:S(2)}) collective-permute-start(bf16[240,1280]{1,0:T(8,128)(2,1)S(1)} %collective-permute-done.17.refs_1_), channel_id=1, source_target_pairs={{0,4},{4,0},{1,5},{5,1},{2,6},{6,2},{3,7},{7,3},{8,12},{12,8},{9,1... | collective-permute-start | bytes 1843208 | tf_op jit(solution)/shard_map/ppermute | solution.py:73
  51.4 5.7 %collective-permute-start.20 = (bf16[240,1280]{1,0:T(8,128)(2,1)S(1)}, bf16[240,1280]{1,0:T(8,128)(2,1)S(1)}, u32[]{:S(2)}, u32[]{:S(2)}) collective-permute-start(bf16[240,1280]{1,0:T(8,128)(2,1)S(1)} %collective-permute-done.16.refs_0_), channel_id=1, source_target_pairs={{0,4},{4,0},{1,5},{5,1},{2,6},{6,2},{3,7},{7,3},{8,12},{12,8},{9,1... | collective-permute-start | bytes 1843208 | tf_op jit(solution)/shard_map/ppermute | solution.py:73
  54.8 4.4 %collective-permute-start.22 = (bf16[128,1280]{1,0:T(8,128)(2,1)S(1)}, bf16[128,1280]{1,0:T(8,128)(2,1)S(1)}, u32[]{:S(2)}, u32[]{:S(2)}) collective-permute-start(bf16[128,1280]{1,0:T(8,128)(2,1)S(1)} %collective-permute-done.18.refs_0_.refs_2_), channel_id=1, source_target_pairs={{0,4},{4,0},{1,5},{5,1},{2,6},{6,2},{3,7},{7,3},{8,12},{12,8},{9,1... | collective-permute-start | bytes 983048 | tf_op jit(solution)/shard_map/ppermute | solution.py:73
  57.0 2.2 %collective-permute-start.23 = (bf16[112,1280]{1,0:T(8,128)(2,1)S(1)}, bf16[112,1280]{1,0:T(8,128)(2,1)S(1)}, u32[]{:S(2)}, u32[]{:S(2)}) collective-permute-start(bf16[112,1280]{1,0:T(8,128)(2,1)S(1)} %collective-permute-done.19.refs_1_.refs_3_), channel_id=1, source_target_pairs={{0,4},{4,0},{1,5},{5,1},{2,6},{6,2},{3,7},{7,3},{8,12},{12,8},{9,1... | collective-permute-start | bytes 860168 | tf_op jit(solution)/shard_map/ppermute | solution.py:73

commit v7 on v6

--- a/solution.py
+++ b/solution.py
@@ -213,9 +213,13 @@
 
 def part_kernel(plan, n, *refs):
     pieces, others = refs[:n], refs[n : 2 * n]
-    near, far, rows_ref, d_ref = refs[2 * n :]
+    near, far, rows_ref, *begun, d_ref = refs[2 * n :]
     capacity, units = near.shape[1:]
-    acts = activations(pieces, others, rows_ref)
+    if begun:
+        half = rows_ref.shape[1] // 2
+        acts = begun[0][...] + dot(joined(others), rows_ref[:, half:], LAST)
+    else:
+        acts = activations(pieces, others, rows_ref)
     for i, (k, group) in enumerate(plan):
         at = slice(i * capacity, (i + 1) * capacity)
         source = source_of(k)
@@ -223,6 +227,11 @@
         _, d_gate, d_up = gradients(acts[at, :units], acts[at, units:], cotan)
         d_ref[at, :units] = d_gate
         d_ref[at, units:] = d_up
+
+
+def begin_kernel(*refs):
+    *pieces, rows_ref, out = refs
+    out[...] = dot(joined(pieces), rows_ref[:, : rows_ref.shape[1] // 2], LAST)
 
 
 def hold(ds, held):
@@ -289,13 +298,13 @@
             name="own",
         )
 
-    def part(plan, pieces, others, near, far):
+    def part(plan, pieces, others, near, far, begun=()):
         n = sum(p.shape[0] for p in pieces)
         (d,) = call(
             functools.partial(part_kernel, plan, len(pieces)),
-            [VMEM] * (2 * len(pieces) + 3),
+            [VMEM] * (2 * len(pieces) + 3 + len(begun)),
             [like(n, 2 * hidden_width)],
-            [*pieces, *others, near, far, both_rows],
+            [*pieces, *others, near, far, both_rows, *begun],
             name="part",
         )
         return d
@@ -370,6 +379,15 @@
     c123_x, c123_y = after([c123_x, c123_y], total, placing)
     cut = (c123.shape[0] // 2 + 15) // 16 * 16
     far_sent = [across(c123_x[:cut], "rep", 2), across(c123_y[cut:], "rep", 1)]
+    (c123_x,), (c123_y,) = after([c123_x], r1), after([c123_y], r2)
+    (begun,) = call(
+        begin_kernel,
+        [VMEM] * 3,
+        [like(2 * c123.shape[0], 2 * hidden_width, dtype=F32)],
+        [c123_x, c123_y, both_rows],
+        name="begin",
+    )
+    (r3,) = after([r3], begun)
     (d_tokens,) = call(
         unpack_kernel,
         [VMEM] * (1 + count),
@@ -378,11 +396,10 @@
         name="unpack",
         flops=6*10**9,
     )
-    (c123_x,), (c123_y,) = after([c123_x], r1), after([c123_y], r2)
     far_sent = after(far_sent, d_tokens)
     plan = tuple((k, group) for group in (1, 2) for k in (1, 2, 3))
     pieces, others = [c123_x, c123_y], [swap(c123_x), swap(c123_y)]
-    d_d = part(plan, pieces, others, cotan_near, cotan_far)
+    d_d = part(plan, pieces, others, cotan_near, cotan_far, [begun])
     plan = tuple((k, 3) for k in (1, 2, 3))
     far_others = after([swap(f) for f in far_sent], d_d)
     d_e = part(plan, far_sent, far_others, cotan_near, cotan_far)

time: 65.5 us -> 64.9 us (level)
  starting transfers between devices: 19.6 us -> 17.7 us
  waiting for transfers between devices: 22.8 us -> 23.8 us
    ppermute x6, waiting for transfers between devices: 14.9 us -> 16.8 us  [turned(): return lax.ppermute(x, axis, [(i, (i + step) % size) for i in range(size)])]
    ppermute x18, starting transfers between devices: 12.9 us -> 11.1 us  [across(): return lax.ppermute(x, axis, [(i, i ^ bit) for i in range(size)])]
    ppermute x18, waiting for transfers between devices: 7.91 us -> 6.94 us  [across(): return lax.ppermute(x, axis, [(i, i ^ bit) for i in range(size)])]
    pallas_call x12 -> x13, Pallas kernels: 21.8 us -> 22.1 us  [call(): pl.pallas_call(kernel, in_specs=ins, out_specs=[out_spec] * len(outs), ou...]
  transfers between devices with their start and end apart: 24 -> 24, of which waited for: 9 -> 9; matrix products, arithmetic and copies ran while one was open for 0% -> 0% of each run, Pallas kernels for 17% -> 18%
where the time goes in v7:
time: 64.9 us; the launch traced here: 64.8 us
  waiting for transfers between devices  23.8 us (37%)
  Pallas kernels  22.1 us (34%)
  starting transfers between devices  17.7 us (27%)
  between operations  0.99 us (2%)
    pallas_call x13, Pallas kernels, call(): pl.pallas_call(kernel, in_specs=ins, out_specs=[out_spec] * len(outs), ou...  22.1 us
    ppermute x6, waiting for transfers between devices, turned(): return lax.ppermute(x, axis, [(i, (i + step) % size) for i in range(size)])  16.8 us
    ppermute x18, starting transfers between devices, across(): return lax.ppermute(x, axis, [(i, i ^ bit) for i in range(size)])  11.1 us
    ppermute x18, waiting for transfers between devices, across(): return lax.ppermute(x, axis, [(i, i ^ bit) for i in range(size)])  6.94 us
    ppermute x6, starting transfers between devices, turned(): return lax.ppermute(x, axis, [(i, (i + step) % size) for i in range(size)])  6.64 us
  transfers between devices with their start and end apart: 24, of which 9 were waited for; matrix products, arithmetic and copies ran while one was open for 0% of the time, Pallas kernels for 18%

profile of v7, /device:TPU:9, one launch (start us, length us, event | category | flops | bytes accessed | tf_op | source)
XLA Modules:
  0.0 64.8 jit_solution(17162065730701050879)
XLA Ops:
  0.6 1.7 %pack.1 = (bf16[80,1280]{1,0:T(8,128)(2,1)S(1)}, bf16[80,1280]{1,0:T(8,128)(2,1)S(1)}, bf16[80,1280]{1,0:T(8,128)(2,1)S(1)}, bf16[80,1280]{1,0:T(8,128)(2,1)S(1)}, bf16[80,1280]{1,0:T(8,128)(2,1)S(1)}) custom-call(s32[1,128]{1,0:T(1,128)} %bitcast.13, bf16[128,2560]{1,0:T(8,128)(2,1)} %tokens_hbm.1), custom_call_target="tpu_custom_call" | custom-call | flops 1 | bytes 1 | tf_op jit(solution)/shard_map/pack/pallas_call | solution.py:87
  2.3 1.3 %collective-permute-start.3 = (bf16[80,1280]{1,0:T(8,128)(2,1)S(1)}, bf16[80,1280]{1,0:T(8,128)(2,1)S(1)}, u32[]{:S(2)}, u32[]{:S(2)}) collective-permute-start(bf16[80,1280]{1,0:T(8,128)(2,1)S(1)} %get-tuple-element.48.refs_0_), channel_id=1, source_target_pairs={{0,8},{8,0},{16,24},{24,16},{1,9},{9,1},{17,25},{25,17},{2,10},{10... | collective-permute-start | bytes 614408 | tf_op jit(solution)/shard_map/ppermute | solution.py:73
  3.6 1.2 %collective-permute-start.4 = (bf16[4,80,384]{2,1,0:T(8,128)(2,1)}, bf16[4,80,384]{2,1,0:T(8,128)(2,1)S(1)}, u32[]{:S(2)}, u32[]{:S(2)}) collective-permute-start(bf16[4,80,384]{2,1,0:T(8,128)(2,1)} %bitcast.10), channel_id=1, source_target_pairs={{0,16},{8,24},{16,0},{24,8},{1,17},{9,25},{17,1},{25,9},{2,18},{10... | collective-permute-start | bytes 737288 | tf_op jit(solution)/shard_map/ppermute | solution.py:73
  4.8 1.3 %collective-permute-start = (bf16[80,1280]{1,0:T(8,128)(2,1)S(1)}, bf16[80,1280]{1,0:T(8,128)(2,1)S(1)}, u32[]{:S(2)}, u32[]{:S(2)}) collective-permute-start(bf16[80,1280]{1,0:T(8,128)(2,1)S(1)} %get-tuple-element.43), channel_id=1, source_target_pairs={{0,1},{1,2},{2,3},{3,0},{4,5},{5,6},{6,7},{7,4},{8,9},{9,10},{10,1... | collective-permute-start | bytes 614408 | tf_op jit(solution)/shard_map/ppermute | solution.py:78
  6.1 1.0 %collective-permute-start.1 = (bf16[80,1280]{1,0:T(8,128)(2,1)S(1)}, bf16[80,1280]{1,0:T(8,128)(2,1)S(1)}, u32[]{:S(2)}, u32[]{:S(2)}) collective-permute-start(bf16[80,1280]{1,0:T(8,128)(2,1)S(1)} %get-tuple-element.44), channel_id=1, source_target_pairs={{0,2},{1,3},{2,0},{3,1},{4,6},{5,7},{6,4},{7,5},{8,10},{9,11},{10,... | collective-permute-start | bytes 614408 | tf_op jit(solution)/shard_map/ppermute | solution.py:78
  7.1 1.5 %collective-permute-start.2 = (bf16[80,1280]{1,0:T(8,128)(2,1)S(1)}, bf16[80,1280]{1,0:T(8,128)(2,1)S(1)}, u32[]{:S(2)}, u32[]{:S(2)}) collective-permute-start(bf16[80,1280]{1,0:T(8,128)(2,1)S(1)} %get-tuple-element.45), channel_id=1, source_target_pairs={{0,3},{1,0},{2,1},{3,2},{4,7},{5,4},{6,5},{7,6},{8,11},{9,8},{10,9... | collective-permute-start | bytes 614408 | tf_op jit(solution)/shard_map/ppermute | solution.py:78
  8.6 2.2 %load.1.refs_9_.refs_6_.rows_ref.refs_2_ = bf16[768,2560]{1,0:T(8,128)(2,1)S(1)} custom-call(bf16[384,2560]{1,0:T(8,128)(2,1)} %bitcast.15, bf16[384,2560]{1,0:T(8,128)(2,1)} %bitcast.16), custom_call_target="tpu_custom_call" | custom-call | flops 1 | bytes 1 | tf_op jit(solution)/shard_map/load/pallas_call | solution.py:87
  11.2 0.8 %collective-permute-start.8 = (bf16[160,1280]{1,0:T(8,128)(2,1)S(1)}, bf16[160,1280]{1,0:T(8,128)(2,1)S(1)}, u32[]{:S(2)}, u32[]{:S(2)}) collective-permute-start(bf16[160,1280]{1,0:T(8,128)(2,1)S(1)} %constant_dynamic-update-slice_fusion), channel_id=1, source_target_pairs={{0,16},{8,24},{16,0},{24,8},{1,17},{9,25},{17,1},{25,9},{2,18},{10... | collective-permute-start | bytes 1228808 | tf_op jit(solution)/shard_map/ppermute | solution.py:73
  12.0 10.4 %collective-permute-done.1.refs_2_ = bf16[80,1280]{1,0:T(8,128)(2,1)S(1)} collective-permute-done((bf16[80,1280]{1,0:T(8,128)(2,1)S(1)}, bf16[80,1280]{1,0:T(8,128)(2,1)S(1)}, u32[]{:S(2)}, u32[]{:S(2)}) %collective-permute-start.1) | collective-permute-done | bytes 204832 | tf_op jit(solution)/shard_map/ppermute | solution.py:78
  22.4 3.4 %collective-permute-done.2.refs_3_ = bf16[80,1280]{1,0:T(8,128)(2,1)S(1)} collective-permute-done((bf16[80,1280]{1,0:T(8,128)(2,1)S(1)}, bf16[80,1280]{1,0:T(8,128)(2,1)S(1)}, u32[]{:S(2)}, u32[]{:S(2)}) %collective-permute-start.2) | collective-permute-done | bytes 204832 | tf_op jit(solution)/shard_map/ppermute | solution.py:78
  25.8 0.5 collective-permute-start.5
  26.3 0.5 collective-permute-start.7
  26.8 0.6 collective-permute-done.5.refs_5_.refs_7_
  27.4 0.4 collective-permute-done.6.refs_6_.refs_8_
  28.1 3.0 %own.1 = (bf16[320,768]{1,0:T(8,128)(2,1)S(1)}, bf16[320,1280]{1,0:T(8,128)(2,1)S(1)}, bf16[4,80,384]{2,1,0:T(8,128)(2,1)}) custom-call(bf16[80,1280]{1,0:T(8,128)(2,1)S(1)} %get-tuple-element.48.refs_0_, bf16[80,1280]{1,0:T(8,128)(2,1)S(1)} %collective-permute-done.refs_1_, bf16[80,1280]{1,0:T(8,128)(2,1)S(1)} %collective-permute-done.1.refs_2_, ...), custom_call_target="tpu_custom_call" | custom-call | flops 1 | bytes 1 | tf_op jit(solution)/shard_map/own/pallas_call | solution.py:87
  31.1 0.4 collective-permute-start.12
  32.1 0.8 %collective-permute-start.11 = (bf16[160,1280]{1,0:T(8,128)(2,1)S(1)}, bf16[160,1280]{1,0:T(8,128)(2,1)S(1)}, u32[]{:S(2)}, u32[]{:S(2)}) collective-permute-start(bf16[160,1280]{1,0:T(8,128)(2,1)S(1)} %collective-permute-done.8.refs_1_.refs_5_), channel_id=1, source_target_pairs={{0,4},{4,0},{1,5},{5,1},{2,6},{6,2},{3,7},{7,3},{8,12},{12,8},{9,1... | collective-permute-start | bytes 1228808 | tf_op jit(solution)/shard_map/ppermute | solution.py:73
  32.8 0.8 %kept.1.kept_ref = bf16[320,1280]{1,0:T(8,128)(2,1)S(1)} custom-call(bf16[320,768]{1,0:T(8,128)(2,1)S(1)} %get-tuple-element.63.d_ref.refs_12_, bf16[768,2560]{1,0:T(8,128)(2,1)S(1)} %load.1.refs_9_.refs_6_.rows_ref.refs_2_), custom_call_target="tpu_custom_call" | custom-call | flops 1 | bytes 1 | tf_op jit(solution)/shard_map/kept/pallas_call | solution.py:87
  33.9 1.4 %collective-permute-start.14 = (bf16[80,1280]{1,0:T(8,128)(2,1)S(1)}, bf16[80,1280]{1,0:T(8,128)(2,1)S(1)}, u32[]{:S(2)}, u32[]{:S(2)}) collective-permute-start(bf16[80,1280]{1,0:T(8,128)(2,1)S(1)} %get-tuple-element.66), channel_id=1, source_target_pairs={{0,2},{1,3},{2,0},{3,1},{4,6},{5,7},{6,4},{7,5},{8,10},{9,11},{10,... | collective-permute-start | bytes 614408 | tf_op jit(solution)/shard_map/ppermute | solution.py:78
  35.3 1.5 %collective-permute-start.15 = (bf16[80,1280]{1,0:T(8,128)(2,1)S(1)}, bf16[80,1280]{1,0:T(8,128)(2,1)S(1)}, u32[]{:S(2)}, u32[]{:S(2)}) collective-permute-start(bf16[80,1280]{1,0:T(8,128)(2,1)S(1)} %get-tuple-element.67), channel_id=1, source_target_pairs={{0,1},{1,2},{2,3},{3,0},{4,5},{5,6},{6,7},{7,4},{8,9},{9,10},{10,1... | collective-permute-start | bytes 614408 | tf_op jit(solution)/shard_map/ppermute | solution.py:78
  36.8 1.3 %part.3.refs_13_ = bf16[240,768]{1,0:T(8,128)(2,1)S(1)} custom-call(bf16[80,1280]{1,0:T(8,128)(2,1)S(1)} %collective-permute-done.3.refs_0_.refs_4_, bf16[160,1280]{1,0:T(8,128)(2,1)S(1)} %collective-permute-done.8.refs_1_.refs_5_, bf16[80,1280]{1,0:T(8,128)(2,1)S(1)} %collective-permute-done.10.refs_2_.refs_10_, ...), custom_call_target="tpu_custom_call" | custom-call | flops 1 | bytes 1 | tf_op jit(solution)/shard_map/part/pallas_call | solution.py:87
  38.3 3.3 %grads_near.1.refs_10_ = f32[768,2560]{1,0:T(8,128)S(1)} custom-call(bf16[80,1280]{1,0:T(8,128)(2,1)S(1)} %get-tuple-element.48.refs_0_, bf16[80,1280]{1,0:T(8,128)(2,1)S(1)} %collective-permute-done.refs_1_, bf16[80,1280]{1,0:T(8,128)(2,1)S(1)} %collective-permute-done.1.refs_2_, bf16[80,1280]{1,0:T(8,128)(2,1)S(1)} %collective-permute-done.2.refs_3_, ...), custom_call_target="tpu_custom_call" | custom-call | flops 1 | bytes 1 | tf_op jit(solution)/shard_map/grads_near/pallas_call | solution.py:87
  41.5 5.3 %collective-permute-done.16.refs_0_ = bf16[240,1280]{1,0:T(8,128)(2,1)S(1)} collective-permute-done((bf16[240,1280]{1,0:T(8,128)(2,1)S(1)}, bf16[240,1280]{1,0:T(8,128)(2,1)S(1)}, u32[]{:S(2)}, u32[]{:S(2)}) %collective-permute-start.16) | collective-permute-done | bytes 614432 | tf_op jit(solution)/shard_map/ppermute | solution.py:73
  47.2 1.2 %collective-permute-start.19 = (bf16[112,1280]{1,0:T(8,128)(2,1)S(1)}, bf16[112,1280]{1,0:T(8,128)(2,1)S(1)}, u32[]{:S(2)}, u32[]{:S(2)}) collective-permute-start(bf16[112,1280]{1,0:T(8,128)(2,1)S(1)} %slice.7), channel_id=1, source_target_pairs={{0,8},{8,0},{16,24},{24,16},{1,9},{9,1},{17,25},{25,17},{2,10},{10... | collective-permute-start | bytes 860168 | tf_op jit(solution)/shard_map/ppermute | solution.py:73
  48.4 3.0 %collective-permute-done.13.refs_1_ = bf16[80,1280]{1,0:T(8,128)(2,1)S(1)} collective-permute-done((bf16[80,1280]{1,0:T(8,128)(2,1)S(1)}, bf16[80,1280]{1,0:T(8,128)(2,1)S(1)}, u32[]{:S(2)}, u32[]{:S(2)}) %collective-permute-start.13) | collective-permute-done | bytes 204832 | tf_op jit(solution)/shard_map/ppermute | solution.py:78
  51.4 1.0 %collective-permute-start.21 = (bf16[240,1280]{1,0:T(8,128)(2,1)S(1)}, bf16[240,1280]{1,0:T(8,128)(2,1)S(1)}, u32[]{:S(2)}, u32[]{:S(2)}) collective-permute-start(bf16[240,1280]{1,0:T(8,128)(2,1)S(1)} %collective-permute-done.17.refs_1_), channel_id=1, source_target_pairs={{0,4},{4,0},{1,5},{5,1},{2,6},{6,2},{3,7},{7,3},{8,12},{12,8},{9,1... | collective-permute-start | bytes 1843208 | tf_op jit(solution)/shard_map/ppermute | solution.py:73
  52.4 1.2 %begin.1.refs_7_ = f32[480,768]{1,0:T(8,128)S(1)} custom-call(bf16[240,1280]{1,0:T(8,128)(2,1)S(1)} %collective-permute-done.16.refs_0_, bf16[240,1280]{1,0:T(8,128)(2,1)S(1)} %collective-permute-done.17.refs_1_, bf16[768,2560]{1,0:T(8,128)(2,1)S(1)} %load.1.refs_9_.refs_6_.rows_ref.refs_2_), custom_call_target="tpu_custom_call" | custom-call | flops 1 | bytes 1 | tf_op jit(solution)/shard_map/begin/pallas_call | solution.py:87
  53.6 1.1 %unpack.1 = bf16[128,1280]{1,0:T(8,128)(2,1)} custom-call(bf16[128,320]{1,0:T(8,128)(2,1)S(1)} %place.1.placing_ref, bf16[80,1280]{1,0:T(8,128)(2,1)S(1)} %get-tuple-element.64.refs_0_, bf16[80,1280]{1,0:T(8,128)(2,1)S(1)} %collective-permute-done.13.refs_1_, bf16[80,1280]{1,0:T(8,128)(2,1)S(1)} %collective-permute-done.14.refs_2_, ...), custom_call_target="tpu_custom_call" | custom-call | flops 6000000000 | bytes 1 | tf_op jit(solution)/shard_map/unpack/pallas_call | solution.py:87
  54.8 2.2 %collective-permute-start.22 = (bf16[128,1280]{1,0:T(8,128)(2,1)S(1)}, bf16[128,1280]{1,0:T(8,128)(2,1)S(1)}, u32[]{:S(2)}, u32[]{:S(2)}) collective-permute-start(bf16[128,1280]{1,0:T(8,128)(2,1)S(1)} %collective-permute-done.18.refs_0_.refs_2_), channel_id=1, source_target_pairs={{0,4},{4,0},{1,5},{5,1},{2,6},{6,2},{3,7},{7,3},{8,12},{12,8},{9,1... | collective-permute-start | bytes 983048 | tf_op jit(solution)/shard_map/ppermute | solution.py:73
  57.1 1.4 %part.4.refs_8_ = bf16[480,768]{1,0:T(8,128)(2,1)S(1)} custom-call(bf16[240,1280]{1,0:T(8,128)(2,1)S(1)} %collective-permute-done.16.refs_0_, bf16[240,1280]{1,0:T(8,128)(2,1)S(1)} %collective-permute-done.17.refs_1_, bf16[240,1280]{1,0:T(8,128)(2,1)S(1)} %collective-permute-done.20.refs_2_.refs_4_, ...), custom_call_target="tpu_custom_call" | custom-call | flops 1 | bytes 1 | tf_op jit(solution)/shard_map/part/pallas_call | solution.py:87
  58.7 1.3 %part.5.refs_9_ = bf16[240,768]{1,0:T(8,128)(2,1)S(1)} custom-call(bf16[128,1280]{1,0:T(8,128)(2,1)S(1)} %collective-permute-done.18.refs_0_.refs_2_, bf16[112,1280]{1,0:T(8,128)(2,1)S(1)} %collective-permute-done.19.refs_1_.refs_3_, bf16[128,1280]{1,0:T(8,128)(2,1)S(1)} %collective-permute-done.22.refs_2_.refs_6_, ...), custom_call_target="tpu_custom_call" | custom-call | flops 1 | bytes 1 | tf_op jit(solution)/shard_map/part/pallas_call | solution.py:87
  60.0 4.6 %grads.1 = (bf16[384,2560]{1,0:T(8,128)(2,1)}, bf16[384,2560]{1,0:T(8,128)(2,1)}) custom-call(bf16[240,1280]{1,0:T(8,128)(2,1)S(1)} %collective-permute-done.16.refs_0_, bf16[240,1280]{1,0:T(8,128)(2,1)S(1)} %collective-permute-done.17.refs_1_, bf16[128,1280]{1,0:T(8,128)(2,1)S(1)} %collective-permute-done.18.refs_0_.refs_2_, ...), custom_call_target="tpu_custom_call" | custom-call | flops 1 | bytes 1 | tf_op jit(solution)/shard_map/grads/pallas_call | solution.py:87
  (39 shorter events, 2.6 us)
Async XLA Ops:
  2.3 8.5 %collective-permute-start.3 = (bf16[80,1280]{1,0:T(8,128)(2,1)S(1)}, bf16[80,1280]{1,0:T(8,128)(2,1)S(1)}, u32[]{:S(2)}, u32[]{:S(2)}) collective-permute-start(bf16[80,1280]{1,0:T(8,128)(2,1)S(1)} %get-tuple-element.48.refs_0_), channel_id=1, source_target_pairs={{0,8},{8,0},{16,24},{24,16},{1,9},{9,1},{17,25},{25,17},{2,10},{10... | collective-permute-start | bytes 614408 | tf_op jit(solution)/shard_map/ppermute | solution.py:73
  3.6 7.2 %collective-permute-start.4 = (bf16[4,80,384]{2,1,0:T(8,128)(2,1)}, bf16[4,80,384]{2,1,0:T(8,128)(2,1)S(1)}, u32[]{:S(2)}, u32[]{:S(2)}) collective-permute-start(bf16[4,80,384]{2,1,0:T(8,128)(2,1)} %bitcast.10), channel_id=1, source_target_pairs={{0,16},{8,24},{16,0},{24,8},{1,17},{9,25},{17,1},{25,9},{2,18},{10... | collective-permute-start | bytes 737288 | tf_op jit(solution)/shard_map/ppermute | solution.py:73
  4.8 7.2 %collective-permute-start = (bf16[80,1280]{1,0:T(8,128)(2,1)S(1)}, bf16[80,1280]{1,0:T(8,128)(2,1)S(1)}, u32[]{:S(2)}, u32[]{:S(2)}) collective-permute-start(bf16[80,1280]{1,0:T(8,128)(2,1)S(1)} %get-tuple-element.43), channel_id=1, source_target_pairs={{0,1},{1,2},{2,3},{3,0},{4,5},{5,6},{6,7},{7,4},{8,9},{9,10},{10,1... | collective-permute-start | bytes 614408 | tf_op jit(solution)/shard_map/ppermute | solution.py:78
  6.1 16.3 %collective-permute-start.1 = (bf16[80,1280]{1,0:T(8,128)(2,1)S(1)}, bf16[80,1280]{1,0:T(8,128)(2,1)S(1)}, u32[]{:S(2)}, u32[]{:S(2)}) collective-permute-start(bf16[80,1280]{1,0:T(8,128)(2,1)S(1)} %get-tuple-element.44), channel_id=1, source_target_pairs={{0,2},{1,3},{2,0},{3,1},{4,6},{5,7},{6,4},{7,5},{8,10},{9,11},{10,... | collective-permute-start | bytes 614408 | tf_op jit(solution)/shard_map/ppermute | solution.py:78
  7.1 18.7 %collective-permute-start.2 = (bf16[80,1280]{1,0:T(8,128)(2,1)S(1)}, bf16[80,1280]{1,0:T(8,128)(2,1)S(1)}, u32[]{:S(2)}, u32[]{:S(2)}) collective-permute-start(bf16[80,1280]{1,0:T(8,128)(2,1)S(1)} %get-tuple-element.45), channel_id=1, source_target_pairs={{0,3},{1,0},{2,1},{3,2},{4,7},{5,4},{6,5},{7,6},{8,11},{9,8},{10,9... | collective-permute-start | bytes 614408 | tf_op jit(solution)/shard_map/ppermute | solution.py:78
  8.6 2.2 %copy-start = (bf16[1,1,4,80,384]{4,3,2,1,0:T(8,128)(2,1)S(1)}, bf16[1,1,4,80,384]{4,3,2,1,0:T(8,128)(2,1)}, u32[]{:S(2)}) copy-start(bf16[1,1,4,80,384]{4,3,2,1,0:T(8,128)(2,1)} %param.9) | copy-start | bytes 737284
  10.9 17.2 %collective-permute-start.9 = (bf16[2,4,80,384]{3,2,1,0:T(8,128)(2,1)S(1)}, bf16[2,4,80,384]{3,2,1,0:T(8,128)(2,1)S(1)}, u32[]{:S(2)}, u32[]{:S(2)}) collective-permute-start(bf16[2,4,80,384]{3,2,1,0:T(8,128)(2,1)S(1)} %pad_maximum_fusion.1), channel_id=1, source_target_pairs={{0,8},{8,0},{16,24},{24,16},{1,9},{9,1},{17,25},{25,17},{2,10},{10... | collective-permute-start | bytes 1474568 | tf_op jit(solution)/shard_map/ppermute | solution.py:73
  11.2 16.9 %collective-permute-start.8 = (bf16[160,1280]{1,0:T(8,128)(2,1)S(1)}, bf16[160,1280]{1,0:T(8,128)(2,1)S(1)}, u32[]{:S(2)}, u32[]{:S(2)}) collective-permute-start(bf16[160,1280]{1,0:T(8,128)(2,1)S(1)} %constant_dynamic-update-slice_fusion), channel_id=1, source_target_pairs={{0,16},{8,24},{16,0},{24,8},{1,17},{9,25},{17,1},{25,9},{2,18},{10... | collective-permute-start | bytes 1228808 | tf_op jit(solution)/shard_map/ppermute | solution.py:73
  25.8 1.6 %collective-permute-start.5 = (bf16[80,1280]{1,0:T(8,128)(2,1)S(1)}, bf16[80,1280]{1,0:T(8,128)(2,1)S(1)}, u32[]{:S(2)}, u32[]{:S(2)}) collective-permute-start(bf16[80,1280]{1,0:T(8,128)(2,1)S(1)} %collective-permute-done.refs_1_), channel_id=1, source_target_pairs={{0,4},{4,0},{1,5},{5,1},{2,6},{6,2},{3,7},{7,3},{8,12},{12,8},{9,1... | collective-permute-start | bytes 614408 | tf_op jit(solution)/shard_map/ppermute | solution.py:73
  26.3 1.5 %collective-permute-start.6 = (bf16[80,1280]{1,0:T(8,128)(2,1)S(1)}, bf16[80,1280]{1,0:T(8,128)(2,1)S(1)}, u32[]{:S(2)}, u32[]{:S(2)}) collective-permute-start(bf16[80,1280]{1,0:T(8,128)(2,1)S(1)} %collective-permute-done.1.refs_2_), channel_id=1, source_target_pairs={{0,4},{4,0},{1,5},{5,1},{2,6},{6,2},{3,7},{7,3},{8,12},{12,8},{9,1... | collective-permute-start | bytes 614408 | tf_op jit(solution)/shard_map/ppermute | solution.py:73
  26.3 1.7 %collective-permute-start.7 = (bf16[80,1280]{1,0:T(8,128)(2,1)S(1)}, bf16[80,1280]{1,0:T(8,128)(2,1)S(1)}, u32[]{:S(2)}, u32[]{:S(2)}) collective-permute-start(bf16[80,1280]{1,0:T(8,128)(2,1)S(1)} %collective-permute-done.2.refs_3_), channel_id=1, source_target_pairs={{0,4},{4,0},{1,5},{5,1},{2,6},{6,2},{3,7},{7,3},{8,12},{12,8},{9,1... | collective-permute-start | bytes 614408 | tf_op jit(solution)/shard_map/ppermute | solution.py:73
  31.1 2.5 %collective-permute-start.12 = (bf16[320,1280]{1,0:T(8,128)(2,1)S(1)}, bf16[320,1280]{1,0:T(8,128)(2,1)S(1)}, u32[]{:S(2)}, u32[]{:S(2)}) collective-permute-start(bf16[320,1280]{1,0:T(8,128)(2,1)S(1)} %get-tuple-element.59), channel_id=1, source_target_pairs={{0,4},{4,0},{1,5},{5,1},{2,6},{6,2},{3,7},{7,3},{8,12},{12,8},{9,1... | collective-permute-start | bytes 2457608 | tf_op jit(solution)/shard_map/ppermute | solution.py:73
  31.5 15.3 %collective-permute-start.16 = (bf16[240,1280]{1,0:T(8,128)(2,1)S(1)}, bf16[240,1280]{1,0:T(8,128)(2,1)S(1)}, u32[]{:S(2)}, u32[]{:S(2)}) collective-permute-start(bf16[240,1280]{1,0:T(8,128)(2,1)S(1)} %pad_maximum_fusion), channel_id=1, source_target_pairs={{0,8},{8,0},{16,24},{24,16},{1,9},{9,1},{17,25},{25,17},{2,10},{10... | collective-permute-start | bytes 1843208 | tf_op jit(solution)/shard_map/ppermute | solution.py:73
  31.8 15.0 %collective-permute-start.17 = (bf16[240,1280]{1,0:T(8,128)(2,1)S(1)}, bf16[240,1280]{1,0:T(8,128)(2,1)S(1)}, u32[]{:S(2)}, u32[]{:S(2)}) collective-permute-start(bf16[240,1280]{1,0:T(8,128)(2,1)S(1)} %pad_maximum_fusion), channel_id=1, source_target_pairs={{0,16},{8,24},{16,0},{24,8},{1,17},{9,25},{17,1},{25,9},{2,18},{10... | collective-permute-start | bytes 1843208 | tf_op jit(solution)/shard_map/ppermute | solution.py:73
  32.1 3.2 %collective-permute-start.11 = (bf16[160,1280]{1,0:T(8,128)(2,1)S(1)}, bf16[160,1280]{1,0:T(8,128)(2,1)S(1)}, u32[]{:S(2)}, u32[]{:S(2)}) collective-permute-start(bf16[160,1280]{1,0:T(8,128)(2,1)S(1)} %collective-permute-done.8.refs_1_.refs_5_), channel_id=1, source_target_pairs={{0,4},{4,0},{1,5},{5,1},{2,6},{6,2},{3,7},{7,3},{8,12},{12,8},{9,1... | collective-permute-start | bytes 1228808 | tf_op jit(solution)/shard_map/ppermute | solution.py:73
  32.8 2.4 %collective-permute-start.10 = (bf16[80,1280]{1,0:T(8,128)(2,1)S(1)}, bf16[80,1280]{1,0:T(8,128)(2,1)S(1)}, u32[]{:S(2)}, u32[]{:S(2)}) collective-permute-start(bf16[80,1280]{1,0:T(8,128)(2,1)S(1)} %collective-permute-done.3.refs_0_.refs_4_), channel_id=1, source_target_pairs={{0,4},{4,0},{1,5},{5,1},{2,6},{6,2},{3,7},{7,3},{8,12},{12,8},{9,1... | collective-permute-start | bytes 614408 | tf_op jit(solution)/shard_map/ppermute | solution.py:73
  33.9 14.5 %collective-permute-start.14 = (bf16[80,1280]{1,0:T(8,128)(2,1)S(1)}, bf16[80,1280]{1,0:T(8,128)(2,1)S(1)}, u32[]{:S(2)}, u32[]{:S(2)}) collective-permute-start(bf16[80,1280]{1,0:T(8,128)(2,1)S(1)} %get-tuple-element.66), channel_id=1, source_target_pairs={{0,2},{1,3},{2,0},{3,1},{4,6},{5,7},{6,4},{7,5},{8,10},{9,11},{10,... | collective-permute-start | bytes 614408 | tf_op jit(solution)/shard_map/ppermute | solution.py:78
  35.3 16.1 %collective-permute-start.13 = (bf16[80,1280]{1,0:T(8,128)(2,1)S(1)}, bf16[80,1280]{1,0:T(8,128)(2,1)S(1)}, u32[]{:S(2)}, u32[]{:S(2)}) collective-permute-start(bf16[80,1280]{1,0:T(8,128)(2,1)S(1)} %get-tuple-element.65), channel_id=1, source_target_pairs={{0,3},{1,0},{2,1},{3,2},{4,7},{5,4},{6,5},{7,6},{8,11},{9,8},{10,9... | collective-permute-start | bytes 614408 | tf_op jit(solution)/shard_map/ppermute | solution.py:78
  35.3 2.7 %copy-start.1 = (s32[128,1]{0,1:T(1,128)S(1)}, s32[128,1]{0,1:T(1,128)}, u32[]{:S(2)}) copy-start(s32[128,1]{0,1:T(1,128)} %param.6) | copy-start | bytes 1540
  35.3 18.3 %collective-permute-start.15 = (bf16[80,1280]{1,0:T(8,128)(2,1)S(1)}, bf16[80,1280]{1,0:T(8,128)(2,1)S(1)}, u32[]{:S(2)}, u32[]{:S(2)}) collective-permute-start(bf16[80,1280]{1,0:T(8,128)(2,1)S(1)} %get-tuple-element.67), channel_id=1, source_target_pairs={{0,1},{1,2},{2,3},{3,0},{4,5},{5,6},{6,7},{7,4},{8,9},{9,10},{10,1... | collective-permute-start | bytes 614408 | tf_op jit(solution)/shard_map/ppermute | solution.py:78
  46.9 8.0 %collective-permute-start.18 = (bf16[128,1280]{1,0:T(8,128)(2,1)S(1)}, bf16[128,1280]{1,0:T(8,128)(2,1)S(1)}, u32[]{:S(2)}, u32[]{:S(2)}) collective-permute-start(bf16[128,1280]{1,0:T(8,128)(2,1)S(1)} %slice.6), channel_id=1, source_target_pairs={{0,16},{8,24},{16,0},{24,8},{1,17},{9,25},{17,1},{25,9},{2,18},{10... | collective-permute-start | bytes 983048 | tf_op jit(solution)/shard_map/ppermute | solution.py:73
  47.2 7.6 %collective-permute-start.19 = (bf16[112,1280]{1,0:T(8,128)(2,1)S(1)}, bf16[112,1280]{1,0:T(8,128)(2,1)S(1)}, u32[]{:S(2)}, u32[]{:S(2)}) collective-permute-start(bf16[112,1280]{1,0:T(8,128)(2,1)S(1)} %slice.7), channel_id=1, source_target_pairs={{0,8},{8,0},{16,24},{24,16},{1,9},{9,1},{17,25},{25,17},{2,10},{10... | collective-permute-start | bytes 860168 | tf_op jit(solution)/shard_map/ppermute | solution.py:73
  51.4 5.7 %collective-permute-start.21 = (bf16[240,1280]{1,0:T(8,128)(2,1)S(1)}, bf16[240,1280]{1,0:T(8,128)(2,1)S(1)}, u32[]{:S(2)}, u32[]{:S(2)}) collective-permute-start(bf16[240,1280]{1,0:T(8,128)(2,1)S(1)} %collective-permute-done.17.refs_1_), channel_id=1, source_target_pairs={{0,4},{4,0},{1,5},{5,1},{2,6},{6,2},{3,7},{7,3},{8,12},{12,8},{9,1... | collective-permute-start | bytes 1843208 | tf_op jit(solution)/shard_map/ppermute | solution.py:73
  53.6 3.5 %collective-permute-start.20 = (bf16[240,1280]{1,0:T(8,128)(2,1)S(1)}, bf16[240,1280]{1,0:T(8,128)(2,1)S(1)}, u32[]{:S(2)}, u32[]{:S(2)}) collective-permute-start(bf16[240,1280]{1,0:T(8,128)(2,1)S(1)} %collective-permute-done.16.refs_0_), channel_id=1, source_target_pairs={{0,4},{4,0},{1,5},{5,1},{2,6},{6,2},{3,7},{7,3},{8,12},{12,8},{9,1... | collective-permute-start | bytes 1843208 | tf_op jit(solution)/shard_map/ppermute | solution.py:73
  54.8 3.9 %collective-permute-start.22 = (bf16[128,1280]{1,0:T(8,128)(2,1)S(1)}, bf16[128,1280]{1,0:T(8,128)(2,1)S(1)}, u32[]{:S(2)}, u32[]{:S(2)}) collective-permute-start(bf16[128,1280]{1,0:T(8,128)(2,1)S(1)} %collective-permute-done.18.refs_0_.refs_2_), channel_id=1, source_target_pairs={{0,4},{4,0},{1,5},{5,1},{2,6},{6,2},{3,7},{7,3},{8,12},{12,8},{9,1... | collective-permute-start | bytes 983048 | tf_op jit(solution)/shard_map/ppermute | solution.py:73
  57.0 1.7 %collective-permute-start.23 = (bf16[112,1280]{1,0:T(8,128)(2,1)S(1)}, bf16[112,1280]{1,0:T(8,128)(2,1)S(1)}, u32[]{:S(2)}, u32[]{:S(2)}) collective-permute-start(bf16[112,1280]{1,0:T(8,128)(2,1)S(1)} %collective-permute-done.19.refs_1_.refs_3_), channel_id=1, source_target_pairs={{0,4},{4,0},{1,5},{5,1},{2,6},{6,2},{3,7},{7,3},{8,12},{12,8},{9,1... | collective-permute-start | bytes 860168 | tf_op jit(solution)/shard_map/ppermute | solution.py:73

commit v8 on v7

--- a/solution.py
+++ b/solution.py
@@ -124,37 +124,40 @@
     return pl.ds(pl.multiple_of(core * half, 128), half)
 
 
-def load_kernel(gate_ref, up_ref, out, sem):
+def load_kernel(capacity, gate_ref, up_ref, expert_hbm, tokens_hbm, out, other, *scratch):
+    experts, theirs, sem, token_sem = scratch
     core, (units, width) = lax.axis_index("shard"), gate_ref.shape
     half, copies = width // 2, []
     for i, ref in enumerate((gate_ref, up_ref)):
         for j, side in enumerate((core, 1 - core)):
             to = out.at[i * units : (i + 1) * units, j * half : (j + 1) * half]
             copies.append(pltpu.make_async_copy(ref.at[:, side_of(side, half)], to, sem.at[i, j]))
-    for c in copies:
+    first = pltpu.make_async_copy(expert_hbm, experts, token_sem.at[0])
+    second = pltpu.make_async_copy(tokens_hbm.at[:, side_of(1 - core, half)], theirs, token_sem.at[1])
+    for c in (first, second, *copies):
         c.start()
+    first.wait()
+    placing = place_rows(experts, capacity)
+    second.wait()
+    other[...] = dot(placing[:capacity], theirs[...], MATMUL).astype(BF16)
     for c in copies:
         c.wait()
 
 
 def pack_kernel(capacity, expert_hbm, tokens_hbm, *refs):
-    *outs, experts, mine, theirs, sem = refs
+    *outs, experts, mine, sem = refs
     count, core = lax.axis_size("exp"), lax.axis_index("shard")
     half = mine.shape[1]
     first = pltpu.make_async_copy(expert_hbm, experts, sem.at[0])
     second = pltpu.make_async_copy(tokens_hbm.at[:, side_of(core, half)], mine, sem.at[1])
-    third = pltpu.make_async_copy(tokens_hbm.at[:, side_of(1 - core, half)], theirs, sem.at[2])
     first.start()
     second.start()
-    third.start()
     first.wait()
     placing = place_rows(experts, capacity)
     second.wait()
     packed = dot(placing, mine[...], MATMUL).astype(BF16)
     for k in range(count):
         outs[k][...] = packed[k * capacity : (k + 1) * capacity]
-    third.wait()
-    outs[count][...] = dot(placing[:capacity], theirs[...], MATMUL).astype(BF16)
 
 
 def place_kernel(capacity, expert_ref, out):
@@ -312,16 +315,16 @@
     def add(kept, got):
         return call(sum_kernel, [VMEM] * 2, [piece] * count, [kept, got], name="sum")
 
-    *blocks, other = call(
+    packing = [pltpu.with_memory_space_constraint(x, pltpu.HBM) for x in (experts, tokens)]
+    blocks = call(
         functools.partial(pack_kernel, capacity),
         [HBM, HBM],
-        [piece] * (count + 1),
-        [pltpu.with_memory_space_constraint(x, pltpu.HBM) for x in (experts, tokens)],
+        [piece] * count,
+        packing,
         scratch=[
             pltpu.VMEM(experts.shape, jnp.int32),
             pltpu.VMEM((tokens.shape[0], half), BF16),
-            pltpu.VMEM((tokens.shape[0], half), BF16),
-            pltpu.SemaphoreType.DMA((3,)),
+            pltpu.SemaphoreType.DMA((2,)),
         ],
         name="pack",
     )
@@ -330,12 +333,18 @@
     (cotan_sent,) = after([cotan], c0)
     c0_near = across(c0, "rep", 1)
     cotan_near = across(cotan_sent, "rep", 2)
-    (both_rows,) = call(
-        load_kernel,
-        [HBM] * 2,
-        [like(2 * hidden_width, width)],
-        after([pltpu.with_memory_space_constraint(x, pltpu.HBM) for x in (gate_rows, up_rows)], c0),
-        scratch=[pltpu.SemaphoreType.DMA((2, 2))],
+    weights = [pltpu.with_memory_space_constraint(x, pltpu.HBM) for x in (gate_rows, up_rows)]
+    both_rows, other = call(
+        functools.partial(load_kernel, capacity),
+        [HBM] * 4,
+        [like(2 * hidden_width, width), piece],
+        [*after(weights, c0), *packing],
+        scratch=[
+            pltpu.VMEM(experts.shape, jnp.int32),
+            pltpu.VMEM((tokens.shape[0], half), BF16),
+            pltpu.SemaphoreType.DMA((2, 2)),
+            pltpu.SemaphoreType.DMA((2,)),
+        ],
         name="load",
     )
     c0_kept, c0_near_kept = after([c0, c0_near], both_rows)

time: 64.9 us -> 64.7 us (level)
  no operation moved by 1% of the time
where the time goes in v8:
time: 64.7 us; the launch traced here: 64.5 us
  waiting for transfers between devices  23.8 us (37%)
  Pallas kernels  21.9 us (34%)
  starting transfers between devices  17.6 us (27%)
  between operations  0.99 us (2%)
    pallas_call x13, Pallas kernels, call(): pl.pallas_call(kernel, in_specs=ins, out_specs=[out_spec] * len(outs), ou...  21.9 us
    ppermute x6, waiting for transfers between devices, turned(): return lax.ppermute(x, axis, [(i, (i + step) % size) for i in range(size)])  16.8 us
    ppermute x18, starting transfers between devices, across(): return lax.ppermute(x, axis, [(i, i ^ bit) for i in range(size)])  10.9 us
    ppermute x18, waiting for transfers between devices, across(): return lax.ppermute(x, axis, [(i, i ^ bit) for i in range(size)])  6.96 us
    ppermute x6, starting transfers between devices, turned(): return lax.ppermute(x, axis, [(i, (i + step) % size) for i in range(size)])  6.65 us
  transfers between devices with their start and end apart: 24, of which 9 were waited for; matrix products, arithmetic and copies ran while one was open for 0% of the time, Pallas kernels for 18%

profile of v8, /device:TPU:9, one launch (start us, length us, event | category | flops | bytes accessed | tf_op | source)
XLA Modules:
  0.0 64.5 jit_solution(5185986240555325799)
XLA Ops:
  0.6 1.4 %pack.1 = (bf16[80,1280]{1,0:T(8,128)(2,1)S(1)}, bf16[80,1280]{1,0:T(8,128)(2,1)S(1)}, bf16[80,1280]{1,0:T(8,128)(2,1)S(1)}, bf16[80,1280]{1,0:T(8,128)(2,1)S(1)}) custom-call(s32[1,128]{1,0:T(1,128)} %bitcast.13, bf16[128,2560]{1,0:T(8,128)(2,1)} %tokens_hbm.3), custom_call_target="tpu_custom_call" | custom-call | flops 1 | bytes 1 | tf_op jit(solution)/shard_map/pack/pallas_call | solution.py:87
  2.0 1.3 %collective-permute-start.3 = (bf16[80,1280]{1,0:T(8,128)(2,1)S(1)}, bf16[80,1280]{1,0:T(8,128)(2,1)S(1)}, u32[]{:S(2)}, u32[]{:S(2)}) collective-permute-start(bf16[80,1280]{1,0:T(8,128)(2,1)S(1)} %get-tuple-element.50.refs_0_), channel_id=1, source_target_pairs={{0,8},{8,0},{16,24},{24,16},{1,9},{9,1},{17,25},{25,17},{2,10},{10... | collective-permute-start | bytes 614408 | tf_op jit(solution)/shard_map/ppermute | solution.py:73
  3.3 1.2 %collective-permute-start.4 = (bf16[4,80,384]{2,1,0:T(8,128)(2,1)}, bf16[4,80,384]{2,1,0:T(8,128)(2,1)S(1)}, u32[]{:S(2)}, u32[]{:S(2)}) collective-permute-start(bf16[4,80,384]{2,1,0:T(8,128)(2,1)} %bitcast.10), channel_id=1, source_target_pairs={{0,16},{8,24},{16,0},{24,8},{1,17},{9,25},{17,1},{25,9},{2,18},{10... | collective-permute-start | bytes 737288 | tf_op jit(solution)/shard_map/ppermute | solution.py:73
  4.5 1.3 %collective-permute-start = (bf16[80,1280]{1,0:T(8,128)(2,1)S(1)}, bf16[80,1280]{1,0:T(8,128)(2,1)S(1)}, u32[]{:S(2)}, u32[]{:S(2)}) collective-permute-start(bf16[80,1280]{1,0:T(8,128)(2,1)S(1)} %get-tuple-element.44), channel_id=1, source_target_pairs={{0,1},{1,2},{2,3},{3,0},{4,5},{5,6},{6,7},{7,4},{8,9},{9,10},{10,1... | collective-permute-start | bytes 614408 | tf_op jit(solution)/shard_map/ppermute | solution.py:78
  5.8 1.0 %collective-permute-start.1 = (bf16[80,1280]{1,0:T(8,128)(2,1)S(1)}, bf16[80,1280]{1,0:T(8,128)(2,1)S(1)}, u32[]{:S(2)}, u32[]{:S(2)}) collective-permute-start(bf16[80,1280]{1,0:T(8,128)(2,1)S(1)} %get-tuple-element.45), channel_id=1, source_target_pairs={{0,2},{1,3},{2,0},{3,1},{4,6},{5,7},{6,4},{7,5},{8,10},{9,11},{10,... | collective-permute-start | bytes 614408 | tf_op jit(solution)/shard_map/ppermute | solution.py:78
  6.8 1.5 %collective-permute-start.2 = (bf16[80,1280]{1,0:T(8,128)(2,1)S(1)}, bf16[80,1280]{1,0:T(8,128)(2,1)S(1)}, u32[]{:S(2)}, u32[]{:S(2)}) collective-permute-start(bf16[80,1280]{1,0:T(8,128)(2,1)S(1)} %get-tuple-element.46), channel_id=1, source_target_pairs={{0,3},{1,0},{2,1},{3,2},{4,7},{5,4},{6,5},{7,6},{8,11},{9,8},{10,9... | collective-permute-start | bytes 614408 | tf_op jit(solution)/shard_map/ppermute | solution.py:78
  8.3 2.3 %load.1 = (bf16[768,2560]{1,0:T(8,128)(2,1)S(1)}, bf16[80,1280]{1,0:T(8,128)(2,1)S(1)}) custom-call(bf16[384,2560]{1,0:T(8,128)(2,1)} %bitcast.16, bf16[384,2560]{1,0:T(8,128)(2,1)} %bitcast.17, s32[1,128]{1,0:T(1,128)} %bitcast.14, bf16[128,2560]{1,0:T(8,128)(2,1)} %tokens_hbm.3), custom_call_target="tpu_custom_call" | custom-call | flops 1 | bytes 1 | tf_op jit(solution)/shard_map/load/pallas_call | solution.py:87
  11.1 0.6 collective-permute-start.8
  11.7 10.4 %collective-permute-done.1.refs_2_ = bf16[80,1280]{1,0:T(8,128)(2,1)S(1)} collective-permute-done((bf16[80,1280]{1,0:T(8,128)(2,1)S(1)}, bf16[80,1280]{1,0:T(8,128)(2,1)S(1)}, u32[]{:S(2)}, u32[]{:S(2)}) %collective-permute-start.1) | collective-permute-done | bytes 204832 | tf_op jit(solution)/shard_map/ppermute | solution.py:78
  22.1 3.4 %collective-permute-done.2.refs_3_ = bf16[80,1280]{1,0:T(8,128)(2,1)S(1)} collective-permute-done((bf16[80,1280]{1,0:T(8,128)(2,1)S(1)}, bf16[80,1280]{1,0:T(8,128)(2,1)S(1)}, u32[]{:S(2)}, u32[]{:S(2)}) %collective-permute-start.2) | collective-permute-done | bytes 204832 | tf_op jit(solution)/shard_map/ppermute | solution.py:78
  25.5 0.5 collective-permute-start.5
  26.1 0.5 collective-permute-start.7
  26.6 0.6 collective-permute-done.5.refs_5_.refs_7_
  27.1 0.4 collective-permute-done.6.refs_6_.refs_8_
  27.8 3.0 %own.1 = (bf16[320,768]{1,0:T(8,128)(2,1)S(1)}, bf16[320,1280]{1,0:T(8,128)(2,1)S(1)}, bf16[4,80,384]{2,1,0:T(8,128)(2,1)}) custom-call(bf16[80,1280]{1,0:T(8,128)(2,1)S(1)} %get-tuple-element.50.refs_0_, bf16[80,1280]{1,0:T(8,128)(2,1)S(1)} %collective-permute-done.refs_1_, bf16[80,1280]{1,0:T(8,128)(2,1)S(1)} %collective-permute-done.1.refs_2_, ...), custom_call_target="tpu_custom_call" | custom-call | flops 1 | bytes 1 | tf_op jit(solution)/shard_map/own/pallas_call | solution.py:87
  30.8 0.4 collective-permute-start.12
  31.8 0.8 %collective-permute-start.11 = (bf16[160,1280]{1,0:T(8,128)(2,1)S(1)}, bf16[160,1280]{1,0:T(8,128)(2,1)S(1)}, u32[]{:S(2)}, u32[]{:S(2)}) collective-permute-start(bf16[160,1280]{1,0:T(8,128)(2,1)S(1)} %collective-permute-done.8.refs_1_.refs_5_), channel_id=1, source_target_pairs={{0,4},{4,0},{1,5},{5,1},{2,6},{6,2},{3,7},{7,3},{8,12},{12,8},{9,1... | collective-permute-start | bytes 1228808 | tf_op jit(solution)/shard_map/ppermute | solution.py:73
  32.6 0.8 %kept.1.kept_ref = bf16[320,1280]{1,0:T(8,128)(2,1)S(1)} custom-call(bf16[320,768]{1,0:T(8,128)(2,1)S(1)} %get-tuple-element.65.d_ref.refs_12_, bf16[768,2560]{1,0:T(8,128)(2,1)S(1)} %get-tuple-element.49.refs_9_.refs_6_.rows_ref.refs_2_), custom_call_target="tpu_custom_call" | custom-call | flops 1 | bytes 1 | tf_op jit(solution)/shard_map/kept/pallas_call | solution.py:87
  33.6 1.4 %collective-permute-start.14 = (bf16[80,1280]{1,0:T(8,128)(2,1)S(1)}, bf16[80,1280]{1,0:T(8,128)(2,1)S(1)}, u32[]{:S(2)}, u32[]{:S(2)}) collective-permute-start(bf16[80,1280]{1,0:T(8,128)(2,1)S(1)} %get-tuple-element.68), channel_id=1, source_target_pairs={{0,2},{1,3},{2,0},{3,1},{4,6},{5,7},{6,4},{7,5},{8,10},{9,11},{10,... | collective-permute-start | bytes 614408 | tf_op jit(solution)/shard_map/ppermute | solution.py:78
  35.0 1.5 %collective-permute-start.15 = (bf16[80,1280]{1,0:T(8,128)(2,1)S(1)}, bf16[80,1280]{1,0:T(8,128)(2,1)S(1)}, u32[]{:S(2)}, u32[]{:S(2)}) collective-permute-start(bf16[80,1280]{1,0:T(8,128)(2,1)S(1)} %get-tuple-element.69), channel_id=1, source_target_pairs={{0,1},{1,2},{2,3},{3,0},{4,5},{5,6},{6,7},{7,4},{8,9},{9,10},{10,1... | collective-permute-start | bytes 614408 | tf_op jit(solution)/shard_map/ppermute | solution.py:78
  36.5 1.3 %part.3.refs_13_ = bf16[240,768]{1,0:T(8,128)(2,1)S(1)} custom-call(bf16[80,1280]{1,0:T(8,128)(2,1)S(1)} %collective-permute-done.3.refs_0_.refs_4_, bf16[160,1280]{1,0:T(8,128)(2,1)S(1)} %collective-permute-done.8.refs_1_.refs_5_, bf16[80,1280]{1,0:T(8,128)(2,1)S(1)} %collective-permute-done.10.refs_2_.refs_10_, ...), custom_call_target="tpu_custom_call" | custom-call | flops 1 | bytes 1 | tf_op jit(solution)/shard_map/part/pallas_call | solution.py:87
  38.0 3.3 %grads_near.1.refs_10_ = f32[768,2560]{1,0:T(8,128)S(1)} custom-call(bf16[80,1280]{1,0:T(8,128)(2,1)S(1)} %get-tuple-element.50.refs_0_, bf16[80,1280]{1,0:T(8,128)(2,1)S(1)} %collective-permute-done.refs_1_, bf16[80,1280]{1,0:T(8,128)(2,1)S(1)} %collective-permute-done.1.refs_2_, bf16[80,1280]{1,0:T(8,128)(2,1)S(1)} %collective-permute-done.2.refs_3_, ...), custom_call_target="tpu_custom_call" | custom-call | flops 1 | bytes 1 | tf_op jit(solution)/shard_map/grads_near/pallas_call | solution.py:87
  41.3 5.3 %collective-permute-done.16.refs_0_ = bf16[240,1280]{1,0:T(8,128)(2,1)S(1)} collective-permute-done((bf16[240,1280]{1,0:T(8,128)(2,1)S(1)}, bf16[240,1280]{1,0:T(8,128)(2,1)S(1)}, u32[]{:S(2)}, u32[]{:S(2)}) %collective-permute-start.16) | collective-permute-done | bytes 614432 | tf_op jit(solution)/shard_map/ppermute | solution.py:73
  46.9 1.2 %collective-permute-start.19 = (bf16[112,1280]{1,0:T(8,128)(2,1)S(1)}, bf16[112,1280]{1,0:T(8,128)(2,1)S(1)}, u32[]{:S(2)}, u32[]{:S(2)}) collective-permute-start(bf16[112,1280]{1,0:T(8,128)(2,1)S(1)} %slice.7), channel_id=1, source_target_pairs={{0,8},{8,0},{16,24},{24,16},{1,9},{9,1},{17,25},{25,17},{2,10},{10... | collective-permute-start | bytes 860168 | tf_op jit(solution)/shard_map/ppermute | solution.py:73
  48.1 3.0 %collective-permute-done.13.refs_1_ = bf16[80,1280]{1,0:T(8,128)(2,1)S(1)} collective-permute-done((bf16[80,1280]{1,0:T(8,128)(2,1)S(1)}, bf16[80,1280]{1,0:T(8,128)(2,1)S(1)}, u32[]{:S(2)}, u32[]{:S(2)}) %collective-permute-start.13) | collective-permute-done | bytes 204832 | tf_op jit(solution)/shard_map/ppermute | solution.py:78
  51.1 1.0 %collective-permute-start.21 = (bf16[240,1280]{1,0:T(8,128)(2,1)S(1)}, bf16[240,1280]{1,0:T(8,128)(2,1)S(1)}, u32[]{:S(2)}, u32[]{:S(2)}) collective-permute-start(bf16[240,1280]{1,0:T(8,128)(2,1)S(1)} %collective-permute-done.17.refs_1_), channel_id=1, source_target_pairs={{0,4},{4,0},{1,5},{5,1},{2,6},{6,2},{3,7},{7,3},{8,12},{12,8},{9,1... | collective-permute-start | bytes 1843208 | tf_op jit(solution)/shard_map/ppermute | solution.py:73
  52.1 1.2 %begin.1.refs_7_ = f32[480,768]{1,0:T(8,128)S(1)} custom-call(bf16[240,1280]{1,0:T(8,128)(2,1)S(1)} %collective-permute-done.16.refs_0_, bf16[240,1280]{1,0:T(8,128)(2,1)S(1)} %collective-permute-done.17.refs_1_, bf16[768,2560]{1,0:T(8,128)(2,1)S(1)} %get-tuple-element.49.refs_9_.refs_6_.rows_ref.refs_2_), custom_call_target="tpu_custom_call" | custom-call | flops 1 | bytes 1 | tf_op jit(solution)/shard_map/begin/pallas_call | solution.py:87
  53.4 1.1 %unpack.1 = bf16[128,1280]{1,0:T(8,128)(2,1)} custom-call(bf16[128,320]{1,0:T(8,128)(2,1)S(1)} %place.1.placing_ref, bf16[80,1280]{1,0:T(8,128)(2,1)S(1)} %get-tuple-element.66.refs_0_, bf16[80,1280]{1,0:T(8,128)(2,1)S(1)} %collective-permute-done.13.refs_1_, bf16[80,1280]{1,0:T(8,128)(2,1)S(1)} %collective-permute-done.14.refs_2_, ...), custom_call_target="tpu_custom_call" | custom-call | flops 6000000000 | bytes 1 | tf_op jit(solution)/shard_map/unpack/pallas_call | solution.py:87
  54.6 2.2 %collective-permute-start.22 = (bf16[128,1280]{1,0:T(8,128)(2,1)S(1)}, bf16[128,1280]{1,0:T(8,128)(2,1)S(1)}, u32[]{:S(2)}, u32[]{:S(2)}) collective-permute-start(bf16[128,1280]{1,0:T(8,128)(2,1)S(1)} %collective-permute-done.18.refs_0_.refs_2_), channel_id=1, source_target_pairs={{0,4},{4,0},{1,5},{5,1},{2,6},{6,2},{3,7},{7,3},{8,12},{12,8},{9,1... | collective-permute-start | bytes 983048 | tf_op jit(solution)/shard_map/ppermute | solution.py:73
  56.8 1.4 %part.4.refs_8_ = bf16[480,768]{1,0:T(8,128)(2,1)S(1)} custom-call(bf16[240,1280]{1,0:T(8,128)(2,1)S(1)} %collective-permute-done.16.refs_0_, bf16[240,1280]{1,0:T(8,128)(2,1)S(1)} %collective-permute-done.17.refs_1_, bf16[240,1280]{1,0:T(8,128)(2,1)S(1)} %collective-permute-done.20.refs_2_.refs_4_, ...), custom_call_target="tpu_custom_call" | custom-call | flops 1 | bytes 1 | tf_op jit(solution)/shard_map/part/pallas_call | solution.py:87
  58.5 1.3 %part.5.refs_9_ = bf16[240,768]{1,0:T(8,128)(2,1)S(1)} custom-call(bf16[128,1280]{1,0:T(8,128)(2,1)S(1)} %collective-permute-done.18.refs_0_.refs_2_, bf16[112,1280]{1,0:T(8,128)(2,1)S(1)} %collective-permute-done.19.refs_1_.refs_3_, bf16[128,1280]{1,0:T(8,128)(2,1)S(1)} %collective-permute-done.22.refs_2_.refs_6_, ...), custom_call_target="tpu_custom_call" | custom-call | flops 1 | bytes 1 | tf_op jit(solution)/shard_map/part/pallas_call | solution.py:87
  59.7 4.6 %grads.1 = (bf16[384,2560]{1,0:T(8,128)(2,1)}, bf16[384,2560]{1,0:T(8,128)(2,1)}) custom-call(bf16[240,1280]{1,0:T(8,128)(2,1)S(1)} %collective-permute-done.16.refs_0_, bf16[240,1280]{1,0:T(8,128)(2,1)S(1)} %collective-permute-done.17.refs_1_, bf16[128,1280]{1,0:T(8,128)(2,1)S(1)} %collective-permute-done.18.refs_0_.refs_2_, ...), custom_call_target="tpu_custom_call" | custom-call | flops 1 | bytes 1 | tf_op jit(solution)/shard_map/grads/pallas_call | solution.py:87
  (39 shorter events, 2.6 us)
Async XLA Ops:
  2.0 8.6 %collective-permute-start.3 = (bf16[80,1280]{1,0:T(8,128)(2,1)S(1)}, bf16[80,1280]{1,0:T(8,128)(2,1)S(1)}, u32[]{:S(2)}, u32[]{:S(2)}) collective-permute-start(bf16[80,1280]{1,0:T(8,128)(2,1)S(1)} %get-tuple-element.50.refs_0_), channel_id=1, source_target_pairs={{0,8},{8,0},{16,24},{24,16},{1,9},{9,1},{17,25},{25,17},{2,10},{10... | collective-permute-start | bytes 614408 | tf_op jit(solution)/shard_map/ppermute | solution.py:73
  3.3 7.4 %collective-permute-start.4 = (bf16[4,80,384]{2,1,0:T(8,128)(2,1)}, bf16[4,80,384]{2,1,0:T(8,128)(2,1)S(1)}, u32[]{:S(2)}, u32[]{:S(2)}) collective-permute-start(bf16[4,80,384]{2,1,0:T(8,128)(2,1)} %bitcast.10), channel_id=1, source_target_pairs={{0,16},{8,24},{16,0},{24,8},{1,17},{9,25},{17,1},{25,9},{2,18},{10... | collective-permute-start | bytes 737288 | tf_op jit(solution)/shard_map/ppermute | solution.py:73
  4.5 7.2 %collective-permute-start = (bf16[80,1280]{1,0:T(8,128)(2,1)S(1)}, bf16[80,1280]{1,0:T(8,128)(2,1)S(1)}, u32[]{:S(2)}, u32[]{:S(2)}) collective-permute-start(bf16[80,1280]{1,0:T(8,128)(2,1)S(1)} %get-tuple-element.44), channel_id=1, source_target_pairs={{0,1},{1,2},{2,3},{3,0},{4,5},{5,6},{6,7},{7,4},{8,9},{9,10},{10,1... | collective-permute-start | bytes 614408 | tf_op jit(solution)/shard_map/ppermute | solution.py:78
  5.8 16.3 %collective-permute-start.1 = (bf16[80,1280]{1,0:T(8,128)(2,1)S(1)}, bf16[80,1280]{1,0:T(8,128)(2,1)S(1)}, u32[]{:S(2)}, u32[]{:S(2)}) collective-permute-start(bf16[80,1280]{1,0:T(8,128)(2,1)S(1)} %get-tuple-element.45), channel_id=1, source_target_pairs={{0,2},{1,3},{2,0},{3,1},{4,6},{5,7},{6,4},{7,5},{8,10},{9,11},{10,... | collective-permute-start | bytes 614408 | tf_op jit(solution)/shard_map/ppermute | solution.py:78
  6.8 18.7 %collective-permute-start.2 = (bf16[80,1280]{1,0:T(8,128)(2,1)S(1)}, bf16[80,1280]{1,0:T(8,128)(2,1)S(1)}, u32[]{:S(2)}, u32[]{:S(2)}) collective-permute-start(bf16[80,1280]{1,0:T(8,128)(2,1)S(1)} %get-tuple-element.46), channel_id=1, source_target_pairs={{0,3},{1,0},{2,1},{3,2},{4,7},{5,4},{6,5},{7,6},{8,11},{9,8},{10,9... | collective-permute-start | bytes 614408 | tf_op jit(solution)/shard_map/ppermute | solution.py:78
  8.3 2.4 %copy-start = (bf16[1,1,4,80,384]{4,3,2,1,0:T(8,128)(2,1)S(1)}, bf16[1,1,4,80,384]{4,3,2,1,0:T(8,128)(2,1)}, u32[]{:S(2)}) copy-start(bf16[1,1,4,80,384]{4,3,2,1,0:T(8,128)(2,1)} %param.9) | copy-start | bytes 737284
  10.7 17.1 %collective-permute-start.9 = (bf16[2,4,80,384]{3,2,1,0:T(8,128)(2,1)S(1)}, bf16[2,4,80,384]{3,2,1,0:T(8,128)(2,1)S(1)}, u32[]{:S(2)}, u32[]{:S(2)}) collective-permute-start(bf16[2,4,80,384]{3,2,1,0:T(8,128)(2,1)S(1)} %pad_maximum_fusion.1), channel_id=1, source_target_pairs={{0,8},{8,0},{16,24},{24,16},{1,9},{9,1},{17,25},{25,17},{2,10},{10... | collective-permute-start | bytes 1474568 | tf_op jit(solution)/shard_map/ppermute | solution.py:73
  11.1 16.7 %collective-permute-start.8 = (bf16[160,1280]{1,0:T(8,128)(2,1)S(1)}, bf16[160,1280]{1,0:T(8,128)(2,1)S(1)}, u32[]{:S(2)}, u32[]{:S(2)}) collective-permute-start(bf16[160,1280]{1,0:T(8,128)(2,1)S(1)} %constant_dynamic-update-slice_fusion), channel_id=1, source_target_pairs={{0,16},{8,24},{16,0},{24,8},{1,17},{9,25},{17,1},{25,9},{2,18},{10... | collective-permute-start | bytes 1228808 | tf_op jit(solution)/shard_map/ppermute | solution.py:73
  25.5 1.6 %collective-permute-start.5 = (bf16[80,1280]{1,0:T(8,128)(2,1)S(1)}, bf16[80,1280]{1,0:T(8,128)(2,1)S(1)}, u32[]{:S(2)}, u32[]{:S(2)}) collective-permute-start(bf16[80,1280]{1,0:T(8,128)(2,1)S(1)} %collective-permute-done.refs_1_), channel_id=1, source_target_pairs={{0,4},{4,0},{1,5},{5,1},{2,6},{6,2},{3,7},{7,3},{8,12},{12,8},{9,1... | collective-permute-start | bytes 614408 | tf_op jit(solution)/shard_map/ppermute | solution.py:73
  26.0 1.5 %collective-permute-start.6 = (bf16[80,1280]{1,0:T(8,128)(2,1)S(1)}, bf16[80,1280]{1,0:T(8,128)(2,1)S(1)}, u32[]{:S(2)}, u32[]{:S(2)}) collective-permute-start(bf16[80,1280]{1,0:T(8,128)(2,1)S(1)} %collective-permute-done.1.refs_2_), channel_id=1, source_target_pairs={{0,4},{4,0},{1,5},{5,1},{2,6},{6,2},{3,7},{7,3},{8,12},{12,8},{9,1... | collective-permute-start | bytes 614408 | tf_op jit(solution)/shard_map/ppermute | solution.py:73
  26.1 1.7 %collective-permute-start.7 = (bf16[80,1280]{1,0:T(8,128)(2,1)S(1)}, bf16[80,1280]{1,0:T(8,128)(2,1)S(1)}, u32[]{:S(2)}, u32[]{:S(2)}) collective-permute-start(bf16[80,1280]{1,0:T(8,128)(2,1)S(1)} %collective-permute-done.2.refs_3_), channel_id=1, source_target_pairs={{0,4},{4,0},{1,5},{5,1},{2,6},{6,2},{3,7},{7,3},{8,12},{12,8},{9,1... | collective-permute-start | bytes 614408 | tf_op jit(solution)/shard_map/ppermute | solution.py:73
  30.8 2.5 %collective-permute-start.12 = (bf16[320,1280]{1,0:T(8,128)(2,1)S(1)}, bf16[320,1280]{1,0:T(8,128)(2,1)S(1)}, u32[]{:S(2)}, u32[]{:S(2)}) collective-permute-start(bf16[320,1280]{1,0:T(8,128)(2,1)S(1)} %get-tuple-element.61), channel_id=1, source_target_pairs={{0,4},{4,0},{1,5},{5,1},{2,6},{6,2},{3,7},{7,3},{8,12},{12,8},{9,1... | collective-permute-start | bytes 2457608 | tf_op jit(solution)/shard_map/ppermute | solution.py:73
  31.2 15.3 %collective-permute-start.16 = (bf16[240,1280]{1,0:T(8,128)(2,1)S(1)}, bf16[240,1280]{1,0:T(8,128)(2,1)S(1)}, u32[]{:S(2)}, u32[]{:S(2)}) collective-permute-start(bf16[240,1280]{1,0:T(8,128)(2,1)S(1)} %pad_maximum_fusion), channel_id=1, source_target_pairs={{0,8},{8,0},{16,24},{24,16},{1,9},{9,1},{17,25},{25,17},{2,10},{10... | collective-permute-start | bytes 1843208 | tf_op jit(solution)/shard_map/ppermute | solution.py:73
  31.6 15.0 %collective-permute-start.17 = (bf16[240,1280]{1,0:T(8,128)(2,1)S(1)}, bf16[240,1280]{1,0:T(8,128)(2,1)S(1)}, u32[]{:S(2)}, u32[]{:S(2)}) collective-permute-start(bf16[240,1280]{1,0:T(8,128)(2,1)S(1)} %pad_maximum_fusion), channel_id=1, source_target_pairs={{0,16},{8,24},{16,0},{24,8},{1,17},{9,25},{17,1},{25,9},{2,18},{10... | collective-permute-start | bytes 1843208 | tf_op jit(solution)/shard_map/ppermute | solution.py:73
  31.8 3.2 %collective-permute-start.11 = (bf16[160,1280]{1,0:T(8,128)(2,1)S(1)}, bf16[160,1280]{1,0:T(8,128)(2,1)S(1)}, u32[]{:S(2)}, u32[]{:S(2)}) collective-permute-start(bf16[160,1280]{1,0:T(8,128)(2,1)S(1)} %collective-permute-done.8.refs_1_.refs_5_), channel_id=1, source_target_pairs={{0,4},{4,0},{1,5},{5,1},{2,6},{6,2},{3,7},{7,3},{8,12},{12,8},{9,1... | collective-permute-start | bytes 1228808 | tf_op jit(solution)/shard_map/ppermute | solution.py:73
  32.6 2.5 %collective-permute-start.10 = (bf16[80,1280]{1,0:T(8,128)(2,1)S(1)}, bf16[80,1280]{1,0:T(8,128)(2,1)S(1)}, u32[]{:S(2)}, u32[]{:S(2)}) collective-permute-start(bf16[80,1280]{1,0:T(8,128)(2,1)S(1)} %collective-permute-done.3.refs_0_.refs_4_), channel_id=1, source_target_pairs={{0,4},{4,0},{1,5},{5,1},{2,6},{6,2},{3,7},{7,3},{8,12},{12,8},{9,1... | collective-permute-start | bytes 614408 | tf_op jit(solution)/shard_map/ppermute | solution.py:73
  33.6 14.5 %collective-permute-start.14 = (bf16[80,1280]{1,0:T(8,128)(2,1)S(1)}, bf16[80,1280]{1,0:T(8,128)(2,1)S(1)}, u32[]{:S(2)}, u32[]{:S(2)}) collective-permute-start(bf16[80,1280]{1,0:T(8,128)(2,1)S(1)} %get-tuple-element.68), channel_id=1, source_target_pairs={{0,2},{1,3},{2,0},{3,1},{4,6},{5,7},{6,4},{7,5},{8,10},{9,11},{10,... | collective-permute-start | bytes 614408 | tf_op jit(solution)/shard_map/ppermute | solution.py:78
  35.0 16.1 %collective-permute-start.13 = (bf16[80,1280]{1,0:T(8,128)(2,1)S(1)}, bf16[80,1280]{1,0:T(8,128)(2,1)S(1)}, u32[]{:S(2)}, u32[]{:S(2)}) collective-permute-start(bf16[80,1280]{1,0:T(8,128)(2,1)S(1)} %get-tuple-element.67), channel_id=1, source_target_pairs={{0,3},{1,0},{2,1},{3,2},{4,7},{5,4},{6,5},{7,6},{8,11},{9,8},{10,9... | collective-permute-start | bytes 614408 | tf_op jit(solution)/shard_map/ppermute | solution.py:78
  35.0 2.7 %copy-start.1 = (s32[128,1]{0,1:T(1,128)S(1)}, s32[128,1]{0,1:T(1,128)}, u32[]{:S(2)}) copy-start(s32[128,1]{0,1:T(1,128)} %param.6) | copy-start | bytes 1540
  35.0 18.3 %collective-permute-start.15 = (bf16[80,1280]{1,0:T(8,128)(2,1)S(1)}, bf16[80,1280]{1,0:T(8,128)(2,1)S(1)}, u32[]{:S(2)}, u32[]{:S(2)}) collective-permute-start(bf16[80,1280]{1,0:T(8,128)(2,1)S(1)} %get-tuple-element.69), channel_id=1, source_target_pairs={{0,1},{1,2},{2,3},{3,0},{4,5},{5,6},{6,7},{7,4},{8,9},{9,10},{10,1... | collective-permute-start | bytes 614408 | tf_op jit(solution)/shard_map/ppermute | solution.py:78
  46.6 8.0 %collective-permute-start.18 = (bf16[128,1280]{1,0:T(8,128)(2,1)S(1)}, bf16[128,1280]{1,0:T(8,128)(2,1)S(1)}, u32[]{:S(2)}, u32[]{:S(2)}) collective-permute-start(bf16[128,1280]{1,0:T(8,128)(2,1)S(1)} %slice.6), channel_id=1, source_target_pairs={{0,16},{8,24},{16,0},{24,8},{1,17},{9,25},{17,1},{25,9},{2,18},{10... | collective-permute-start | bytes 983048 | tf_op jit(solution)/shard_map/ppermute | solution.py:73
  46.9 7.6 %collective-permute-start.19 = (bf16[112,1280]{1,0:T(8,128)(2,1)S(1)}, bf16[112,1280]{1,0:T(8,128)(2,1)S(1)}, u32[]{:S(2)}, u32[]{:S(2)}) collective-permute-start(bf16[112,1280]{1,0:T(8,128)(2,1)S(1)} %slice.7), channel_id=1, source_target_pairs={{0,8},{8,0},{16,24},{24,16},{1,9},{9,1},{17,25},{25,17},{2,10},{10... | collective-permute-start | bytes 860168 | tf_op jit(solution)/shard_map/ppermute | solution.py:73
  51.1 5.7 %collective-permute-start.21 = (bf16[240,1280]{1,0:T(8,128)(2,1)S(1)}, bf16[240,1280]{1,0:T(8,128)(2,1)S(1)}, u32[]{:S(2)}, u32[]{:S(2)}) collective-permute-start(bf16[240,1280]{1,0:T(8,128)(2,1)S(1)} %collective-permute-done.17.refs_1_), channel_id=1, source_target_pairs={{0,4},{4,0},{1,5},{5,1},{2,6},{6,2},{3,7},{7,3},{8,12},{12,8},{9,1... | collective-permute-start | bytes 1843208 | tf_op jit(solution)/shard_map/ppermute | solution.py:73
  53.3 3.5 %collective-permute-start.20 = (bf16[240,1280]{1,0:T(8,128)(2,1)S(1)}, bf16[240,1280]{1,0:T(8,128)(2,1)S(1)}, u32[]{:S(2)}, u32[]{:S(2)}) collective-permute-start(bf16[240,1280]{1,0:T(8,128)(2,1)S(1)} %collective-permute-done.16.refs_0_), channel_id=1, source_target_pairs={{0,4},{4,0},{1,5},{5,1},{2,6},{6,2},{3,7},{7,3},{8,12},{12,8},{9,1... | collective-permute-start | bytes 1843208 | tf_op jit(solution)/shard_map/ppermute | solution.py:73
  54.6 3.9 %collective-permute-start.22 = (bf16[128,1280]{1,0:T(8,128)(2,1)S(1)}, bf16[128,1280]{1,0:T(8,128)(2,1)S(1)}, u32[]{:S(2)}, u32[]{:S(2)}) collective-permute-start(bf16[128,1280]{1,0:T(8,128)(2,1)S(1)} %collective-permute-done.18.refs_0_.refs_2_), channel_id=1, source_target_pairs={{0,4},{4,0},{1,5},{5,1},{2,6},{6,2},{3,7},{7,3},{8,12},{12,8},{9,1... | collective-permute-start | bytes 983048 | tf_op jit(solution)/shard_map/ppermute | solution.py:73
  56.8 1.7 %collective-permute-start.23 = (bf16[112,1280]{1,0:T(8,128)(2,1)S(1)}, bf16[112,1280]{1,0:T(8,128)(2,1)S(1)}, u32[]{:S(2)}, u32[]{:S(2)}) collective-permute-start(bf16[112,1280]{1,0:T(8,128)(2,1)S(1)} %collective-permute-done.19.refs_1_.refs_3_), channel_id=1, source_target_pairs={{0,4},{4,0},{1,5},{5,1},{2,6},{6,2},{3,7},{7,3},{8,12},{12,8},{9,1... | collective-permute-start | bytes 860168 | tf_op jit(solution)/shard_map/ppermute | solution.py:73
